TPU v7x, 256 devices: a whole 4x4x8 slice. The times are simulated.
256 devices in a mesh: prow: 16 (over y_lo, z), pcol: 16 (over y_hi, x, core).
Axes of the slice: x: 4, y: 4 (y_hi: 2, y_lo: 2; y = y_hi * 2 + y_lo), z: 8, core: 2. Of those that a mesh axis runs over, the one named last changes fastest.
Arguments:
- ainv: float32 [3, 16, 256, 3, 16, 256], P(None, 'prow', None, None, 'pcol')
- panel: float32 [4, 3, 16, 256, 256], P(None, None, 'prow', 'pcol'), may hold values from -6 to 6
- diag_inv: float32 [4, 256, 256], replicated, may hold values from -0.03125 to 0.03125
- dinv: float32 [4, 256, 256], replicated, may hold values from -6 to 6
- present: int32 [4, 48], replicated, may hold values from 0 to 1, as said below
Outputs:
- column_blocks: float32 [4, 3, 16, 256, 256], P(None, None, 'prow', 'pcol')
- diag_blocks: float32 [4, 256, 256], replicated
Inputs may be any that keep to these rules, and one draw needn't show every extreme that they name: `present`: each supernode lists between 60 percent (rounded up) and all of the 48 blocks; one supernode lists all of them and one exactly (148) // 5.
All inputs are finite; a program needn't handle non-finite values.
Results may differ from a plain program's by a relative error of at most 0.000071.
Values sent between devices are 32-bit elements; how exact they have to be, the bound alone decides.
No kernel may reach another device: no remote copies, remote signals or barrier semaphores. Data moves between devices by JAX's collectives and lax.ppermute only.
A program may use at most 64 MiB of HBM per device.

v0:
```python
import functools

import jax
import jax.numpy as jnp
from jax import lax
from jax.experimental import pallas as pl
from jax.experimental.pallas import tpu as pltpu
from jax.sharding import Mesh, PartitionSpec as P


F32 = jnp.float32
BF16 = jnp.bfloat16
HIGHEST = lax.Precision.HIGHEST

AXES = ("y_lo", "z", "y_hi", "x", "core")
PLANE = ("y_lo", "y_hi", "x")
LANDING = (0, 4, 1, 6, 2, 7, 3, 5)
SOURCE = tuple(LANDING.index(d) for d in range(8))
SMEM = pl.BlockSpec(memory_space=pltpu.SMEM)
VMEM = pl.BlockSpec(memory_space=pltpu.VMEM)


def to_columns(v):
    pairs = []
    for p in range(16):
        for q in range(16):
            row = (q // 8) * 8 + (p % 8 + LANDING[q % 8]) % 8
            pairs.append((p * 16 + q, row * 16 + p))
    return lax.ppermute(v, AXES, pairs)


def swap_y(v):
    return lax.ppermute(v, "y_lo", [(0, 1), (1, 0)])


def shift_z(v, d):
    return lax.ppermute(v, "z", [(p, (p + d) % 8) for p in range(8)])


def swap_core(v):
    return lax.ppermute(v, "core", [(0, 1), (1, 0)])


def shift_plane(v, k):
    pairs = []
    for q in range(8):
        pairs.append((q, (q // 4 + k // 4) % 2 * 4 + (q + k) % 4))
    return lax.ppermute(v, ("y_hi", "x"), pairs)


def call(body, outs, specs, scratch=(), flops=0, limit=8):
    return pl.pallas_call(
        body,
        out_shape=outs,
        in_specs=specs,
        out_specs=jax.tree.map(lambda _: VMEM, outs),
        scratch_shapes=list(scratch),
        compiler_params=pltpu.CompilerParams(vmem_limit_bytes=limit << 20),
        cost_estimate=pl.CostEstimate(flops=flops, transcendentals=0, bytes_accessed=4 << 20),
    )


def shape(*dims, dtype=F32):
    return jax.ShapeDtypeStruct(dims, dtype)


def split_two(v):
    high = v.astype(BF16)
    return high, (v - high.astype(F32)).astype(BF16)


def panel_body(which, tab, present, panel, inverse, out):
    p = tab[which]
    for s in range(4):
        value = jnp.dot(panel[s], inverse[s], precision=HIGHEST, preferred_element_type=F32)
        for i in range(3):
            live = present[s, i * 16 + p].astype(F32)
            out[s, i * 16 : i * 16 + 16] = value[i * 16 : i * 16 + 16] * live


def matrix_body(tab, a, out):
    core, x, yh = tab[2], tab[3], tab[5]

    @pl.loop(0, 16)
    def _(g):
        place = (yh + g // 4) % 2 * 4 + (x + g) % 4
        start = place * 32 + ((core + g // 8) % 2) * 16
        for i in range(3):
            at = pl.ds(pl.multiple_of(g * 48 + i * 16, 16), 16)
            for j in range(3):
                for half in range(2):
                    block = a[pl.ds(((i * 256 + start) * 3 + j) * 2 + half, 16, stride=6), :]
                    h, l = split_two(-block)
                    for term, part in enumerate((h, l, h)):
                        col = term * 384 + j * 128
                        out[half, at, col : col + 128] = part


def product_body(flip, sides, tab, matrix, *refs):
    n = len(sides)
    before, pieces = (refs[:n], refs[n : n + 9]) if flip else (None, refs[:9])
    outs, held = refs[-n - 1 : -1], refs[-1]
    half = (tab[1] + flip) % 2

    def put(block, d):
        start = pl.multiple_of(tab[8 + d % 8], 16)
        h, l = split_two(block)
        for i in range(3):
            for term, part in enumerate((l, h, h)):
                held[pl.ds(term * 384 + i * 128 + start, 16), :] = part[i * 16 : i * 16 + 16]

    @pl.loop(0, 4)
    def _(s):
        for ref, d in zip(pieces[:7], (0, 1, 2, 3, -1, -2, -3)):
            put(ref[s], d)

        @pl.when(s < 2)
        def _():
            put(pieces[7][s % 2], 4)

        @pl.when(s >= 2)
        def _():
            put(pieces[8][s % 2], 4)

        for n, c in enumerate(sides):
            value = jnp.dot(
                matrix[half, c * 384 : c * 384 + 384, :], held[...], preferred_element_type=F32
            )
            for k in range(8):
                part = value[k * 48 : k * 48 + 48]
                outs[n][k, s] = part if before is None else before[n][k, s] + part


def halves_body(a, b, *outs):
    for k in range(8):
        outs[k][...] = a[k] + b[k]


def sum_body(*refs):
    value = refs[0][...]
    for r in refs[1:-1]:
        value = value + r[...]
    refs[-1][...] = value


def term_body(tab, la, lb, sa, sb, out):
    cols = pl.ds(pl.multiple_of(tab[2] * 128, 128), 128)

    @pl.loop(0, 4)
    def _(s):
        value = [
            lax.dot_general(
                l[s, :, cols], r[s], (((0,), (0,)), ((), ())),
                precision=HIGHEST, preferred_element_type=F32,
            )
            for l, r in ((la, sa), (lb, sb))
        ]
        total = value[0] + value[1]
        for e in range(16):
            out[e, s] = total[e * 8 : e * 8 + 8]


def last_body(tab, own, other, dinv, out):
    core = tab[2]
    for k, r in enumerate((own, other)):
        base = pl.multiple_of(((core + k) % 2) * 128, 128)
        for s in range(4):
            for e in range(16):
                at = pl.ds(base + e * 8, 8)
                out[s, at, :] = dinv[s, at, :] - r[e, s]


def process(ainv, panel, diag_inv, dinv, present):
    yl, z, yh, x, core = (lax.axis_index(a) for a in AXES)
    place = jnp.arange(8, dtype=jnp.int32)
    landed = (z - place - (x * 2 + core)) % 8
    source = sum(jnp.where(landed == d, SOURCE[d], 0) for d in range(8))
    head = jnp.stack([yl * 8 + z, yl, core, x, z, yh, yh * 8 + x * 2 + core, yh]).astype(jnp.int32)
    tab = jnp.concatenate([head, (source * 16).astype(jnp.int32)])

    panel = panel.reshape(4, 48, 256)

    def normalize(which, rows):
        return call(
            functools.partial(panel_body, which), shape(4, 48, 256), [SMEM, SMEM, VMEM, VMEM]
        )(tab, present, rows, diag_inv)

    arrived = to_columns(panel)
    lhat = normalize(0, panel)
    mate = swap_core(lhat)
    matrix = call(matrix_body, shape(2, 768, 1152, dtype=BF16), [SMEM, VMEM])(
        tab, ainv.reshape(4608, 128)
    )
    arrived, mate, matrix = lax.optimization_barrier((arrived, mate, matrix))
    own = normalize(6, arrived)

    chains = []
    for first in (own, swap_y(own)):
        a1, b1 = shift_z(first, 1), shift_z(first, -1)
        a2, b2 = shift_z(a1, 1), shift_z(b1, -1)
        a3, b3 = shift_z(a2, 1), shift_z(b2, -1)
        a4, b4 = shift_z(a3[:2], 1), shift_z(b3[2:], -1)
        chains.append((first, a1, a2, a3, b1, b2, b3, a4, b4))

    def product(flip, sides, *before):
        return call(
            functools.partial(product_body, flip, sides),
            [shape(8, 4, 48, 256)] * len(sides),
            [SMEM] + [VMEM] * (1 + len(before) + 9),
            [pltpu.VMEM((1152, 256), BF16)],
            flops=3 * 768 * 384 * 1024 * len(sides),
            limit=12,
        )(tab, matrix, *before, *chains[flip])

    keep, send = product(0, (0, 1))
    (send,) = product(1, (1,), send)
    other = swap_core(send)
    (keep,) = product(1, (0,), keep)
    parts = call(halves_body, [shape(4, 48, 256)] * 8, [VMEM] * 2)(keep, other)
    parts = [parts[0]] + [shift_plane(parts[k], k) for k in (6, 5, 7, 4, 2, 1, 3)]
    shares = call(sum_body, shape(4, 48, 256), [VMEM] * 8)(*parts)

    term = call(term_body, shape(16, 4, 8, 256), [SMEM] + [VMEM] * 4)(
        tab, lhat, mate, shares, swap_core(shares)
    )
    total = jnp.sum(lax.all_to_all(term, PLANE, 0, 0), axis=0)
    spread = jnp.broadcast_to(total[None], (8, 4, 8, 256))
    total = jnp.sum(lax.all_to_all(spread, "z", 0, 0), axis=0)
    spread = jnp.broadcast_to(total[None], (16, 4, 8, 256))
    total = lax.all_to_all(spread, PLANE, 0, 0)
    diag = call(last_body, shape(4, 256, 256), [SMEM] + [VMEM] * 3)(
        tab, total, swap_core(total), dinv
    )
    return shares.reshape(4, 3, 1, 16, 256), diag


def solution(mesh):
    fine = Mesh(mesh.devices.reshape(2, 8, 2, 4, 2), AXES)
    rows, columns = ("y_lo", "z"), ("y_hi", "x", "core")
    return jax.shard_map(
        process,
        mesh=fine,
        in_specs=(
            P(None, rows, None, None, columns, None),
            P(None, None, rows, columns, None),
            P(),
            P(),
            P(),
        ),
        out_specs=(P(None, None, rows, columns, None), P()),
        check_vma=False,
    )
```

profile of v0, /device:TPU:2, one launch (start us, length us, event | category | flops | bytes accessed | tf_op | source)
XLA Modules:
  0.0 151.2 jit_solution(3826769545860864854)
XLA Ops:
  0.7 0.1 concatenate.3.tab
  0.8 1.2 copy-done
  2.0 0.7 copy-done.5
  2.7 1.6 %shard_map.68.la = f32[4,48,256]{2,1,0:T(8,128)S(1)} custom-call(s32[16]{0:T(128)S(1)} %concatenate.3.tab, s32[4,48]{1,0:T(4,128)S(1)} %copy-done.5, f32[4,48,256]{2,1,0:T(8,128)} %bitcast.7.panel, f32[4,256,256]{2,1,0:T(8,128)S(1)} %copy-done), custom_call_target="tpu_custom_call" | custom-call | bytes 4194304 | tf_op jit(solution)/shard_map/pallas_call | solution.py:184
  4.3 0.1 collective-permute-start.1
  4.4 3.8 %collective-permute-start = (f32[4,48,256]{2,1,0:T(8,128)}, f32[4,48,256]{2,1,0:T(8,128)S(1)}, u32[]{:S(2)}, u32[]{:S(2)}) collective-permute-start(f32[4,48,256]{2,1,0:T(8,128)} %bitcast.7.panel), channel_id=1, source_target_pairs={{0,0},{1,64},{2,16},{3,96},{4,32},{5,112},{6,48},{7,80},{8,128},{9... | collective-permute-start | bytes 589832 | tf_op jit(solution)/shard_map/ppermute | solution.py:29
  8.2 0.0 copy-start.2
  8.2 1.7 %copy-done.2 = f32[3,1,256,3,1,256]{5,4,3,2,1,0:T(1,128)S(1)} copy-done((f32[3,1,256,3,1,256]{5,4,3,2,1,0:T(1,128)S(1)}, f32[3,1,256,3,1,256]{5,4,3,2,1,0:T(1,128)}, u32[]{:S(2)}) %copy-start.2) | copy-done | bytes 2359320
  9.9 1.4 shard_map.69.matrix
  11.3 0.0 collective-permute-done.1.lb
  11.3 4.1 %collective-permute-done.panel = f32[4,48,256]{2,1,0:T(8,128)S(1)} collective-permute-done((f32[4,48,256]{2,1,0:T(8,128)}, f32[4,48,256]{2,1,0:T(8,128)S(1)}, u32[]{:S(2)}, u32[]{:S(2)}) %collective-permute-start) | collective-permute-done | bytes 196640 | tf_op jit(solution)/shard_map/ppermute | solution.py:29
  15.4 1.3 shard_map.70.refs_0_
  16.7 2.7 %collective-permute-start.10 = (f32[4,48,256]{2,1,0:T(8,128)S(1)}, f32[4,48,256]{2,1,0:T(8,128)S(1)}, u32[]{:S(2)}, u32[]{:S(2)}) collective-permute-start(f32[4,48,256]{2,1,0:T(8,128)S(1)} %shard_map.70.refs_0_), channel_id=1, source_target_pairs={{0,128},{128,0},{1,129},{129,1},{2,130},{130,2},{3,131},{131,3},{4... | collective-permute-start | bytes 589832 | tf_op jit(solution)/shard_map/ppermute | solution.py:33
  19.4 9.9 %collective-permute-start.5 = (f32[4,48,256]{2,1,0:T(8,128)S(1)}, f32[4,48,256]{2,1,0:T(8,128)S(1)}, u32[]{:S(2)}, u32[]{:S(2)}) collective-permute-start(f32[4,48,256]{2,1,0:T(8,128)S(1)} %shard_map.70.refs_0_), channel_id=1, source_target_pairs={{0,112},{16,0},{32,16},{48,32},{64,48},{80,64},{96,80},{112,96},{1... | collective-permute-start | bytes 589832 | tf_op jit(solution)/shard_map/ppermute | solution.py:37
  29.3 0.0 collective-permute-start.2
  29.3 0.0 collective-permute-done.10.refs_1_
  29.3 5.1 %collective-permute-start.14 = (f32[4,48,256]{2,1,0:T(8,128)S(1)}, f32[4,48,256]{2,1,0:T(8,128)S(1)}, u32[]{:S(2)}, u32[]{:S(2)}) collective-permute-start(f32[4,48,256]{2,1,0:T(8,128)S(1)} %collective-permute-done.10.refs_1_), channel_id=1, source_target_pairs={{0,112},{16,0},{32,16},{48,32},{64,48},{80,64},{96,80},{112,96},{1... | collective-permute-start | bytes 589832 | tf_op jit(solution)/shard_map/ppermute | solution.py:37
  34.5 0.0 collective-permute-start.11
  34.5 0.0 collective-permute-done.5.refs_4_
  34.5 3.2 %collective-permute-start.6 = (f32[4,48,256]{2,1,0:T(8,128)S(1)}, f32[4,48,256]{2,1,0:T(8,128)S(1)}, u32[]{:S(2)}, u32[]{:S(2)}) collective-permute-start(f32[4,48,256]{2,1,0:T(8,128)S(1)} %collective-permute-done.5.refs_4_), channel_id=1, source_target_pairs={{0,112},{16,0},{32,16},{48,32},{64,48},{80,64},{96,80},{112,96},{1... | collective-permute-start | bytes 589832 | tf_op jit(solution)/shard_map/ppermute | solution.py:37
  37.7 0.0 collective-permute-done.2.refs_1_
  37.7 0.0 collective-permute-start.3
  37.7 2.0 %collective-permute-done.14.refs_5_ = f32[4,48,256]{2,1,0:T(8,128)S(1)} collective-permute-done((f32[4,48,256]{2,1,0:T(8,128)S(1)}, f32[4,48,256]{2,1,0:T(8,128)S(1)}, u32[]{:S(2)}, u32[]{:S(2)}) %collective-permute-start.14) | collective-permute-done | bytes 196640 | tf_op jit(solution)/shard_map/ppermute | solution.py:37
  39.8 3.7 %collective-permute-start.15 = (f32[4,48,256]{2,1,0:T(8,128)S(1)}, f32[4,48,256]{2,1,0:T(8,128)S(1)}, u32[]{:S(2)}, u32[]{:S(2)}) collective-permute-start(f32[4,48,256]{2,1,0:T(8,128)S(1)} %collective-permute-done.14.refs_5_), channel_id=1, source_target_pairs={{0,112},{16,0},{32,16},{48,32},{64,48},{80,64},{96,80},{112,96},{1... | collective-permute-start | bytes 589832 | tf_op jit(solution)/shard_map/ppermute | solution.py:37
  43.5 0.0 collective-permute-done.11.refs_2_
  43.5 0.0 collective-permute-start.12
  43.5 0.5 collective-permute-done.6.refs_5_
  44.0 3.7 %collective-permute-start.7 = (f32[4,48,256]{2,1,0:T(8,128)S(1)}, f32[4,48,256]{2,1,0:T(8,128)S(1)}, u32[]{:S(2)}, u32[]{:S(2)}) collective-permute-start(f32[4,48,256]{2,1,0:T(8,128)S(1)} %collective-permute-done.6.refs_5_), channel_id=1, source_target_pairs={{0,112},{16,0},{32,16},{48,32},{64,48},{80,64},{96,80},{112,96},{1... | collective-permute-start | bytes 589832 | tf_op jit(solution)/shard_map/ppermute | solution.py:37
  47.7 0.8 collective-permute-done.15.refs_6_
  48.5 3.7 %collective-permute-start.16 = (f32[4,48,256]{2,1,0:T(8,128)S(1)}, f32[4,48,256]{2,1,0:T(8,128)S(1)}, u32[]{:S(2)}, u32[]{:S(2)}) collective-permute-start(f32[4,48,256]{2,1,0:T(8,128)S(1)} %collective-permute-done.15.refs_6_), channel_id=1, source_target_pairs={{0,112},{16,0},{32,16},{48,32},{64,48},{80,64},{96,80},{112,96},{1... | collective-permute-start | bytes 589832 | tf_op jit(solution)/shard_map/ppermute | solution.py:37
  52.2 0.1 collective-permute-done.12.refs_3_
  52.3 0.7 collective-permute-done.7.refs_6_
  53.0 4.0 %collective-permute-start.9 = (f32[2,48,256]{2,1,0:T(8,128)S(1)}, f32[2,48,256]{2,1,0:T(8,128)S(1)}, u32[]{:S(2)}, u32[]{:S(2)}) collective-permute-start(f32[2,48,256]{2,1,0:T(8,128)S(1)} %slice.17), channel_id=1, source_target_pairs={{0,112},{16,0},{32,16},{48,32},{64,48},{80,64},{96,80},{112,96},{1... | collective-permute-start | bytes 294920 | tf_op jit(solution)/shard_map/ppermute | solution.py:37
  56.9 0.1 collective-permute-start.8
  57.1 3.3 %collective-permute-start.18 = (f32[2,48,256]{2,1,0:T(8,128)S(1)}, f32[2,48,256]{2,1,0:T(8,128)S(1)}, u32[]{:S(2)}, u32[]{:S(2)}) collective-permute-start(f32[2,48,256]{2,1,0:T(8,128)S(1)} %slice.19), channel_id=1, source_target_pairs={{0,112},{16,0},{32,16},{48,32},{64,48},{80,64},{96,80},{112,96},{1... | collective-permute-start | bytes 294920 | tf_op jit(solution)/shard_map/ppermute | solution.py:37
  60.4 0.1 collective-permute-start.17
  60.5 2.4 %collective-permute-done.8.refs_7_ = f32[2,48,256]{2,1,0:T(8,128)S(1)} collective-permute-done((f32[2,48,256]{2,1,0:T(8,128)S(1)}, f32[2,48,256]{2,1,0:T(8,128)S(1)}, u32[]{:S(2)}, u32[]{:S(2)}) %collective-permute-start.8) | collective-permute-done | bytes 98336 | tf_op jit(solution)/shard_map/ppermute | solution.py:37
  62.8 3.7 %shard_map.71 = (f32[8,4,48,256]{3,2,1,0:T(8,128)S(1)}, f32[8,4,48,256]{3,2,1,0:T(8,128)S(1)}) custom-call(s32[16]{0:T(128)S(1)} %concatenate.3.tab, bf16[2,768,1152]{2,1,0:T(8,128)(2,1)S(1)} %shard_map.69.matrix, f32[4,48,256]{2,1,0:T(8,128)S(1)} %shard_map.70.refs_0_, f32[4,48,256]{2,1,0:T(8,128)S(1)} %collective-permute-done.2.refs_1_, ...), custom_call_target="tpu_custom_call" | custom-call | flops 1811939328 | bytes 4194304 | tf_op jit(solution)/shard_map/pallas_call | solution.py:206
  66.5 2.7 %shard_map.73 = f32[8,4,48,256]{3,2,1,0:T(8,128)S(1)} custom-call(s32[16]{0:T(128)S(1)} %concatenate.3.tab, bf16[2,768,1152]{2,1,0:T(8,128)(2,1)S(1)} %shard_map.69.matrix, f32[8,4,48,256]{3,2,1,0:T(8,128)S(1)} %get-tuple-element.18.refs_0_, f32[4,48,256]{2,1,0:T(8,128)S(1)} %collective-permute-done.10.refs_1_, ...), custom_call_target="tpu_custom_call" | custom-call | flops 905969664 | bytes 4194304 | tf_op jit(solution)/shard_map/pallas_call | solution.py:206
  69.3 0.1 collective-permute-start.19
  69.4 2.7 %shard_map.72.a = f32[8,4,48,256]{3,2,1,0:T(8,128)S(1)} custom-call(s32[16]{0:T(128)S(1)} %concatenate.3.tab, bf16[2,768,1152]{2,1,0:T(8,128)(2,1)S(1)} %shard_map.69.matrix, f32[8,4,48,256]{3,2,1,0:T(8,128)S(1)} %get-tuple-element.17.refs_0_, f32[4,48,256]{2,1,0:T(8,128)S(1)} %collective-permute-done.10.refs_1_, ...), custom_call_target="tpu_custom_call" | custom-call | flops 905969664 | bytes 4194304 | tf_op jit(solution)/shard_map/pallas_call | solution.py:206
  72.1 0.7 collective-permute-done.19.b
  72.8 0.2 shard_map.74
  72.9 0.9 collective-permute-start.20
  73.8 1.4 collective-permute-start.21
  75.2 3.0 %collective-permute-start.22 = (f32[4,48,256]{2,1,0:T(8,128)S(1)}, f32[4,48,256]{2,1,0:T(8,128)S(1)}, u32[]{:S(2)}, u32[]{:S(2)}) collective-permute-start(f32[4,48,256]{2,1,0:T(8,128)S(1)} %get-tuple-element.22), channel_id=1, source_target_pairs={{0,14},{2,8},{4,10},{6,12},{8,6},{10,0},{12,2},{14,4},{1,15},{3,9}... | collective-permute-start | bytes 589832 | tf_op jit(solution)/shard_map/ppermute | solution.py:48
  78.2 2.7 %collective-permute-start.23 = (f32[4,48,256]{2,1,0:T(8,128)S(1)}, f32[4,48,256]{2,1,0:T(8,128)S(1)}, u32[]{:S(2)}, u32[]{:S(2)}) collective-permute-start(f32[4,48,256]{2,1,0:T(8,128)S(1)} %get-tuple-element.23), channel_id=1, source_target_pairs={{0,8},{2,10},{4,12},{6,14},{8,0},{10,2},{12,4},{14,6},{1,9},{3,11}... | collective-permute-start | bytes 589832 | tf_op jit(solution)/shard_map/ppermute | solution.py:48
  80.9 3.0 %collective-permute-start.24 = (f32[4,48,256]{2,1,0:T(8,128)S(1)}, f32[4,48,256]{2,1,0:T(8,128)S(1)}, u32[]{:S(2)}, u32[]{:S(2)}) collective-permute-start(f32[4,48,256]{2,1,0:T(8,128)S(1)} %get-tuple-element.24), channel_id=1, source_target_pairs={{0,4},{2,6},{4,0},{6,2},{8,12},{10,14},{12,8},{14,10},{1,5},{3,7},... | collective-permute-start | bytes 589832 | tf_op jit(solution)/shard_map/ppermute | solution.py:48
  83.9 4.6 %collective-permute-done.20.refs_1_ = f32[4,48,256]{2,1,0:T(8,128)S(1)} collective-permute-done((f32[4,48,256]{2,1,0:T(8,128)S(1)}, f32[4,48,256]{2,1,0:T(8,128)S(1)}, u32[]{:S(2)}, u32[]{:S(2)}) %collective-permute-start.20) | collective-permute-done | bytes 196640 | tf_op jit(solution)/shard_map/ppermute | solution.py:48
  88.6 1.8 %collective-permute-done.21.refs_2_ = f32[4,48,256]{2,1,0:T(8,128)S(1)} collective-permute-done((f32[4,48,256]{2,1,0:T(8,128)S(1)}, f32[4,48,256]{2,1,0:T(8,128)S(1)}, u32[]{:S(2)}, u32[]{:S(2)}) %collective-permute-start.21) | collective-permute-done | bytes 196640 | tf_op jit(solution)/shard_map/ppermute | solution.py:48
  90.3 0.2 collective-permute-start.26
  90.6 5.1 %collective-permute-done.22.refs_3_ = f32[4,48,256]{2,1,0:T(8,128)S(1)} collective-permute-done((f32[4,48,256]{2,1,0:T(8,128)S(1)}, f32[4,48,256]{2,1,0:T(8,128)S(1)}, u32[]{:S(2)}, u32[]{:S(2)}) %collective-permute-start.22) | collective-permute-done | bytes 196640 | tf_op jit(solution)/shard_map/ppermute | solution.py:48
  95.7 0.6 collective-permute-done.23.refs_4_
  96.3 1.5 %collective-permute-done.25.refs_6_ = f32[4,48,256]{2,1,0:T(8,128)S(1)} collective-permute-done((f32[4,48,256]{2,1,0:T(8,128)S(1)}, f32[4,48,256]{2,1,0:T(8,128)S(1)}, u32[]{:S(2)}, u32[]{:S(2)}) %collective-permute-start.25) | collective-permute-done | bytes 196640 | tf_op jit(solution)/shard_map/ppermute | solution.py:48
  97.8 1.6 %collective-permute-done.26.refs_7_ = f32[4,48,256]{2,1,0:T(8,128)S(1)} collective-permute-done((f32[4,48,256]{2,1,0:T(8,128)S(1)}, f32[4,48,256]{2,1,0:T(8,128)S(1)}, u32[]{:S(2)}, u32[]{:S(2)}) %collective-permute-start.26) | collective-permute-done | bytes 196640 | tf_op jit(solution)/shard_map/ppermute | solution.py:48
  99.4 0.7 shard_map.75.sa
  100.2 1.6 %collective-permute-done.27.sb = f32[4,48,256]{2,1,0:T(8,128)S(1)} collective-permute-done((f32[4,48,256]{2,1,0:T(8,128)}, f32[4,48,256]{2,1,0:T(8,128)S(1)}, u32[]{:S(2)}, u32[]{:S(2)}) %collective-permute-start.27) | collective-permute-done | bytes 196640 | tf_op jit(solution)/shard_map/ppermute | solution.py:41
  101.8 0.9 copy-done.4
  102.7 2.2 %shard_map.76 = f32[16,4,8,256]{3,2,1,0:T(8,128)S(1)} custom-call(s32[16]{0:T(128)S(1)} %concatenate.3.tab, f32[4,48,256]{2,1,0:T(8,128)S(1)} %shard_map.68.la, f32[4,48,256]{2,1,0:T(8,128)S(1)} %collective-permute-done.1.lb, f32[4,48,256]{2,1,0:T(8,128)S(1)} %copy-done.4, f32[4,48,256]{2,1,0:T(8,128)S(1)} %collective-permute-done.27.sb), custom_call_target="tpu_custom_call" | custom-call | bytes 4194304 | tf_op jit(solution)/shard_map/pallas_call | solution.py:223
  105.0 13.9 %all_to_all.15 = f32[16,4,8,256]{3,2,1,0:T(8,128)S(1)} all-to-all(f32[16,4,8,256]{3,2,1,0:T(8,128)S(1)} %shard_map.76), channel_id=1, replica_groups=mesh['y_lo'=2,'z'=8,'y_hi'=2,'x'=4,'core'=2] {'y_lo','y_hi','x'}, dimensions={0} | all-to-all | bytes 1048576 | tf_op jit(solution)/shard_map/all_to_all | solution.py:226
  118.9 15.9 %all_to_all.16 = f32[8,4,8,256]{3,2,1,0:T(8,128)S(1)} all-to-all(f32[8,4,8,256]{3,2,1,0:T(8,128)S(1)} %broadcast_in_dim.39), channel_id=1, replica_groups=mesh['y_lo'=2,'z'=8,'y_hi'=2,'x'=4,'core'=2] {'z'}, dimensions={0} | all-to-all | bytes 524288 | tf_op jit(solution)/shard_map/all_to_all | solution.py:228
  134.9 12.8 %all_to_all.17.own = f32[16,4,8,256]{3,2,1,0:T(8,128)S(1)} all-to-all(f32[16,4,8,256]{3,2,1,0:T(8,128)S(1)} %broadcast_in_dim.40), channel_id=1, replica_groups=mesh['y_lo'=2,'z'=8,'y_hi'=2,'x'=4,'core'=2] {'y_lo','y_hi','x'}, dimensions={0} | all-to-all | bytes 1048576 | tf_op jit(solution)/shard_map/all_to_all | solution.py:230
  147.7 1.9 %collective-permute-done.28.other = f32[16,4,8,256]{3,2,1,0:T(8,128)S(1)} collective-permute-done((f32[16,4,8,256]{3,2,1,0:T(8,128)S(1)}, f32[16,4,8,256]{3,2,1,0:T(8,128)S(1)}, u32[]{:S(2)}, u32[]{:S(2)}) %collective-permute-start.28) | collective-permute-done | bytes 524320 | tf_op jit(solution)/shard_map/ppermute | solution.py:41
  149.6 1.7 %shard_map.77 = f32[4,256,256]{2,1,0:T(8,128)} custom-call(s32[16]{0:T(128)S(1)} %concatenate.3.tab, f32[16,4,8,256]{3,2,1,0:T(8,128)S(1)} %all_to_all.17.own, f32[16,4,8,256]{3,2,1,0:T(8,128)S(1)} %collective-permute-done.28.other, f32[4,256,256]{2,1,0:T(8,128)S(1)} %copy-done.3), custom_call_target="tpu_custom_call" | custom-call | bytes 4194304 | tf_op jit(solution)/shard_map/pallas_call | solution.py:231
  (31 shorter events, 0.2 us)
Async XLA Ops:
  0.8 1.2 copy-start
  2.0 0.7 copy-start.5
  4.3 7.0 %collective-permute-start.1 = (f32[4,48,256]{2,1,0:T(8,128)S(1)}, f32[4,48,256]{2,1,0:T(8,128)S(1)}, u32[]{:S(2)}, u32[]{:S(2)}) collective-permute-start(f32[4,48,256]{2,1,0:T(8,128)S(1)} %shard_map.68.la), channel_id=1, source_target_pairs={{0,1},{1,0},{2,3},{3,2},{4,5},{5,4},{6,7},{7,6},{8,9},{9,8},{10,11... | collective-permute-start | bytes 589832 | tf_op jit(solution)/shard_map/ppermute | solution.py:41
  4.4 11.0 %collective-permute-start = (f32[4,48,256]{2,1,0:T(8,128)}, f32[4,48,256]{2,1,0:T(8,128)S(1)}, u32[]{:S(2)}, u32[]{:S(2)}) collective-permute-start(f32[4,48,256]{2,1,0:T(8,128)} %bitcast.7.panel), channel_id=1, source_target_pairs={{0,0},{1,64},{2,16},{3,96},{4,32},{5,112},{6,48},{7,80},{8,128},{9... | collective-permute-start | bytes 589832 | tf_op jit(solution)/shard_map/ppermute | solution.py:29
  8.2 1.7 %copy-start.2 = (f32[3,1,256,3,1,256]{5,4,3,2,1,0:T(1,128)S(1)}, f32[3,1,256,3,1,256]{5,4,3,2,1,0:T(1,128)}, u32[]{:S(2)}) copy-start(f32[3,1,256,3,1,256]{5,4,3,2,1,0:T(1,128)} %param.5) | copy-start | bytes 7077892
  9.9 5.5 %copy-start.1 = (f32[4,256,256]{2,1,0:T(8,128)S(1)}, f32[4,256,256]{2,1,0:T(8,128)}, u32[]{:S(2)}) copy-start(f32[4,256,256]{2,1,0:T(8,128)} %inverse.3) | copy-start | bytes 3145732
  9.9 5.5 %copy-start.6 = (s32[4,48]{1,0:T(4,128)S(1)}, s32[4,48]{1,0:T(4,128)}, u32[]{:S(2)}) copy-start(s32[4,48]{1,0:T(4,128)} %present.3) | copy-start | bytes 2308
  16.7 12.6 %collective-permute-start.10 = (f32[4,48,256]{2,1,0:T(8,128)S(1)}, f32[4,48,256]{2,1,0:T(8,128)S(1)}, u32[]{:S(2)}, u32[]{:S(2)}) collective-permute-start(f32[4,48,256]{2,1,0:T(8,128)S(1)} %shard_map.70.refs_0_), channel_id=1, source_target_pairs={{0,128},{128,0},{1,129},{129,1},{2,130},{130,2},{3,131},{131,3},{4... | collective-permute-start | bytes 589832 | tf_op jit(solution)/shard_map/ppermute | solution.py:33
  19.4 15.1 %collective-permute-start.5 = (f32[4,48,256]{2,1,0:T(8,128)S(1)}, f32[4,48,256]{2,1,0:T(8,128)S(1)}, u32[]{:S(2)}, u32[]{:S(2)}) collective-permute-start(f32[4,48,256]{2,1,0:T(8,128)S(1)} %shard_map.70.refs_0_), channel_id=1, source_target_pairs={{0,112},{16,0},{32,16},{48,32},{64,48},{80,64},{96,80},{112,96},{1... | collective-permute-start | bytes 589832 | tf_op jit(solution)/shard_map/ppermute | solution.py:37
  29.3 8.4 %collective-permute-start.2 = (f32[4,48,256]{2,1,0:T(8,128)S(1)}, f32[4,48,256]{2,1,0:T(8,128)S(1)}, u32[]{:S(2)}, u32[]{:S(2)}) collective-permute-start(f32[4,48,256]{2,1,0:T(8,128)S(1)} %shard_map.70.refs_0_), channel_id=1, source_target_pairs={{0,16},{16,32},{32,48},{48,64},{64,80},{80,96},{96,112},{112,0},{1... | collective-permute-start | bytes 589832 | tf_op jit(solution)/shard_map/ppermute | solution.py:37
  29.3 10.4 %collective-permute-start.14 = (f32[4,48,256]{2,1,0:T(8,128)S(1)}, f32[4,48,256]{2,1,0:T(8,128)S(1)}, u32[]{:S(2)}, u32[]{:S(2)}) collective-permute-start(f32[4,48,256]{2,1,0:T(8,128)S(1)} %collective-permute-done.10.refs_1_), channel_id=1, source_target_pairs={{0,112},{16,0},{32,16},{48,32},{64,48},{80,64},{96,80},{112,96},{1... | collective-permute-start | bytes 589832 | tf_op jit(solution)/shard_map/ppermute | solution.py:37
  34.5 9.0 %collective-permute-start.11 = (f32[4,48,256]{2,1,0:T(8,128)S(1)}, f32[4,48,256]{2,1,0:T(8,128)S(1)}, u32[]{:S(2)}, u32[]{:S(2)}) collective-permute-start(f32[4,48,256]{2,1,0:T(8,128)S(1)} %collective-permute-done.10.refs_1_), channel_id=1, source_target_pairs={{0,16},{16,32},{32,48},{48,64},{64,80},{80,96},{96,112},{112,0},{1... | collective-permute-start | bytes 589832 | tf_op jit(solution)/shard_map/ppermute | solution.py:37
  34.5 9.5 %collective-permute-start.6 = (f32[4,48,256]{2,1,0:T(8,128)S(1)}, f32[4,48,256]{2,1,0:T(8,128)S(1)}, u32[]{:S(2)}, u32[]{:S(2)}) collective-permute-start(f32[4,48,256]{2,1,0:T(8,128)S(1)} %collective-permute-done.5.refs_4_), channel_id=1, source_target_pairs={{0,112},{16,0},{32,16},{48,32},{64,48},{80,64},{96,80},{112,96},{1... | collective-permute-start | bytes 589832 | tf_op jit(solution)/shard_map/ppermute | solution.py:37
  37.7 10.0 %collective-permute-start.3 = (f32[4,48,256]{2,1,0:T(8,128)S(1)}, f32[4,48,256]{2,1,0:T(8,128)S(1)}, u32[]{:S(2)}, u32[]{:S(2)}) collective-permute-start(f32[4,48,256]{2,1,0:T(8,128)S(1)} %collective-permute-done.2.refs_1_), channel_id=1, source_target_pairs={{0,16},{16,32},{32,48},{48,64},{64,80},{80,96},{96,112},{112,0},{1... | collective-permute-start | bytes 589832 | tf_op jit(solution)/shard_map/ppermute | solution.py:37
  39.8 8.7 %collective-permute-start.15 = (f32[4,48,256]{2,1,0:T(8,128)S(1)}, f32[4,48,256]{2,1,0:T(8,128)S(1)}, u32[]{:S(2)}, u32[]{:S(2)}) collective-permute-start(f32[4,48,256]{2,1,0:T(8,128)S(1)} %collective-permute-done.14.refs_5_), channel_id=1, source_target_pairs={{0,112},{16,0},{32,16},{48,32},{64,48},{80,64},{96,80},{112,96},{1... | collective-permute-start | bytes 589832 | tf_op jit(solution)/shard_map/ppermute | solution.py:37
  43.5 8.8 %collective-permute-start.12 = (f32[4,48,256]{2,1,0:T(8,128)S(1)}, f32[4,48,256]{2,1,0:T(8,128)S(1)}, u32[]{:S(2)}, u32[]{:S(2)}) collective-permute-start(f32[4,48,256]{2,1,0:T(8,128)S(1)} %collective-permute-done.11.refs_2_), channel_id=1, source_target_pairs={{0,16},{16,32},{32,48},{48,64},{64,80},{80,96},{96,112},{112,0},{1... | collective-permute-start | bytes 589832 | tf_op jit(solution)/shard_map/ppermute | solution.py:37
  44.0 9.0 %collective-permute-start.7 = (f32[4,48,256]{2,1,0:T(8,128)S(1)}, f32[4,48,256]{2,1,0:T(8,128)S(1)}, u32[]{:S(2)}, u32[]{:S(2)}) collective-permute-start(f32[4,48,256]{2,1,0:T(8,128)S(1)} %collective-permute-done.6.refs_5_), channel_id=1, source_target_pairs={{0,112},{16,0},{32,16},{48,32},{64,48},{80,64},{96,80},{112,96},{1... | collective-permute-start | bytes 589832 | tf_op jit(solution)/shard_map/ppermute | solution.py:37
  47.7 9.3 %collective-permute-start.4 = (f32[4,48,256]{2,1,0:T(8,128)S(1)}, f32[4,48,256]{2,1,0:T(8,128)S(1)}, u32[]{:S(2)}, u32[]{:S(2)}) collective-permute-start(f32[4,48,256]{2,1,0:T(8,128)S(1)} %collective-permute-done.3.refs_2_), channel_id=1, source_target_pairs={{0,16},{16,32},{32,48},{48,64},{64,80},{80,96},{96,112},{112,0},{1... | collective-permute-start | bytes 589832 | tf_op jit(solution)/shard_map/ppermute | solution.py:37
  48.5 8.5 %collective-permute-start.16 = (f32[4,48,256]{2,1,0:T(8,128)S(1)}, f32[4,48,256]{2,1,0:T(8,128)S(1)}, u32[]{:S(2)}, u32[]{:S(2)}) collective-permute-start(f32[4,48,256]{2,1,0:T(8,128)S(1)} %collective-permute-done.15.refs_6_), channel_id=1, source_target_pairs={{0,112},{16,0},{32,16},{48,32},{64,48},{80,64},{96,80},{112,96},{1... | collective-permute-start | bytes 589832 | tf_op jit(solution)/shard_map/ppermute | solution.py:37
  52.3 8.1 %collective-permute-start.13 = (f32[4,48,256]{2,1,0:T(8,128)S(1)}, f32[4,48,256]{2,1,0:T(8,128)S(1)}, u32[]{:S(2)}, u32[]{:S(2)}) collective-permute-start(f32[4,48,256]{2,1,0:T(8,128)S(1)} %collective-permute-done.12.refs_3_), channel_id=1, source_target_pairs={{0,16},{16,32},{32,48},{48,64},{64,80},{80,96},{96,112},{112,0},{1... | collective-permute-start | bytes 589832 | tf_op jit(solution)/shard_map/ppermute | solution.py:37
  53.0 7.5 %collective-permute-start.9 = (f32[2,48,256]{2,1,0:T(8,128)S(1)}, f32[2,48,256]{2,1,0:T(8,128)S(1)}, u32[]{:S(2)}, u32[]{:S(2)}) collective-permute-start(f32[2,48,256]{2,1,0:T(8,128)S(1)} %slice.17), channel_id=1, source_target_pairs={{0,112},{16,0},{32,16},{48,32},{64,48},{80,64},{96,80},{112,96},{1... | collective-permute-start | bytes 294920 | tf_op jit(solution)/shard_map/ppermute | solution.py:37
  56.9 5.9 %collective-permute-start.8 = (f32[2,48,256]{2,1,0:T(8,128)S(1)}, f32[2,48,256]{2,1,0:T(8,128)S(1)}, u32[]{:S(2)}, u32[]{:S(2)}) collective-permute-start(f32[2,48,256]{2,1,0:T(8,128)S(1)} %slice.16), channel_id=1, source_target_pairs={{0,16},{16,32},{32,48},{48,64},{64,80},{80,96},{96,112},{112,0},{1... | collective-permute-start | bytes 294920 | tf_op jit(solution)/shard_map/ppermute | solution.py:37
  57.1 9.5 %collective-permute-start.18 = (f32[2,48,256]{2,1,0:T(8,128)S(1)}, f32[2,48,256]{2,1,0:T(8,128)S(1)}, u32[]{:S(2)}, u32[]{:S(2)}) collective-permute-start(f32[2,48,256]{2,1,0:T(8,128)S(1)} %slice.19), channel_id=1, source_target_pairs={{0,112},{16,0},{32,16},{48,32},{64,48},{80,64},{96,80},{112,96},{1... | collective-permute-start | bytes 294920 | tf_op jit(solution)/shard_map/ppermute | solution.py:37
  60.4 6.2 %collective-permute-start.17 = (f32[2,48,256]{2,1,0:T(8,128)S(1)}, f32[2,48,256]{2,1,0:T(8,128)S(1)}, u32[]{:S(2)}, u32[]{:S(2)}) collective-permute-start(f32[2,48,256]{2,1,0:T(8,128)S(1)} %slice.18), channel_id=1, source_target_pairs={{0,16},{16,32},{32,48},{48,64},{64,80},{80,96},{96,112},{112,0},{1... | collective-permute-start | bytes 294920 | tf_op jit(solution)/shard_map/ppermute | solution.py:37
  69.3 3.5 %collective-permute-start.19 = (f32[8,4,48,256]{3,2,1,0:T(8,128)S(1)}, f32[8,4,48,256]{3,2,1,0:T(8,128)S(1)}, u32[]{:S(2)}, u32[]{:S(2)}) collective-permute-start(f32[8,4,48,256]{3,2,1,0:T(8,128)S(1)} %shard_map.73), channel_id=1, source_target_pairs={{0,1},{1,0},{2,3},{3,2},{4,5},{5,4},{6,7},{7,6},{8,9},{9,8},{10,11... | collective-permute-start | bytes 4718600 | tf_op jit(solution)/shard_map/ppermute | solution.py:41
  72.9 15.6 %collective-permute-start.20 = (f32[4,48,256]{2,1,0:T(8,128)S(1)}, f32[4,48,256]{2,1,0:T(8,128)S(1)}, u32[]{:S(2)}, u32[]{:S(2)}) collective-permute-start(f32[4,48,256]{2,1,0:T(8,128)S(1)} %get-tuple-element.20), channel_id=1, source_target_pairs={{0,12},{2,14},{4,8},{6,10},{8,4},{10,6},{12,0},{14,2},{1,13},{3,15... | collective-permute-start | bytes 589832 | tf_op jit(solution)/shard_map/ppermute | solution.py:48
  73.8 16.5 %collective-permute-start.21 = (f32[4,48,256]{2,1,0:T(8,128)S(1)}, f32[4,48,256]{2,1,0:T(8,128)S(1)}, u32[]{:S(2)}, u32[]{:S(2)}) collective-permute-start(f32[4,48,256]{2,1,0:T(8,128)S(1)} %get-tuple-element.21), channel_id=1, source_target_pairs={{0,10},{2,12},{4,14},{6,8},{8,2},{10,4},{12,6},{14,0},{1,11},{3,13... | collective-permute-start | bytes 589832 | tf_op jit(solution)/shard_map/ppermute | solution.py:48
  75.2 20.4 %collective-permute-start.22 = (f32[4,48,256]{2,1,0:T(8,128)S(1)}, f32[4,48,256]{2,1,0:T(8,128)S(1)}, u32[]{:S(2)}, u32[]{:S(2)}) collective-permute-start(f32[4,48,256]{2,1,0:T(8,128)S(1)} %get-tuple-element.22), channel_id=1, source_target_pairs={{0,14},{2,8},{4,10},{6,12},{8,6},{10,0},{12,2},{14,4},{1,15},{3,9}... | collective-permute-start | bytes 589832 | tf_op jit(solution)/shard_map/ppermute | solution.py:48
  78.2 18.1 %collective-permute-start.23 = (f32[4,48,256]{2,1,0:T(8,128)S(1)}, f32[4,48,256]{2,1,0:T(8,128)S(1)}, u32[]{:S(2)}, u32[]{:S(2)}) collective-permute-start(f32[4,48,256]{2,1,0:T(8,128)S(1)} %get-tuple-element.23), channel_id=1, source_target_pairs={{0,8},{2,10},{4,12},{6,14},{8,0},{10,2},{12,4},{14,6},{1,9},{3,11}... | collective-permute-start | bytes 589832 | tf_op jit(solution)/shard_map/ppermute | solution.py:48
  80.9 15.4 %collective-permute-start.24 = (f32[4,48,256]{2,1,0:T(8,128)S(1)}, f32[4,48,256]{2,1,0:T(8,128)S(1)}, u32[]{:S(2)}, u32[]{:S(2)}) collective-permute-start(f32[4,48,256]{2,1,0:T(8,128)S(1)} %get-tuple-element.24), channel_id=1, source_target_pairs={{0,4},{2,6},{4,0},{6,2},{8,12},{10,14},{12,8},{14,10},{1,5},{3,7},... | collective-permute-start | bytes 589832 | tf_op jit(solution)/shard_map/ppermute | solution.py:48
  88.6 9.3 %collective-permute-start.25 = (f32[4,48,256]{2,1,0:T(8,128)S(1)}, f32[4,48,256]{2,1,0:T(8,128)S(1)}, u32[]{:S(2)}, u32[]{:S(2)}) collective-permute-start(f32[4,48,256]{2,1,0:T(8,128)S(1)} %get-tuple-element.25), channel_id=1, source_target_pairs={{0,2},{2,4},{4,6},{6,0},{8,10},{10,12},{12,14},{14,8},{1,3},{3,5},... | collective-permute-start | bytes 589832 | tf_op jit(solution)/shard_map/ppermute | solution.py:48
  90.3 9.1 %collective-permute-start.26 = (f32[4,48,256]{2,1,0:T(8,128)S(1)}, f32[4,48,256]{2,1,0:T(8,128)S(1)}, u32[]{:S(2)}, u32[]{:S(2)}) collective-permute-start(f32[4,48,256]{2,1,0:T(8,128)S(1)} %get-tuple-element.26), channel_id=1, source_target_pairs={{0,6},{2,0},{4,2},{6,4},{8,14},{10,8},{12,10},{14,12},{1,7},{3,1},... | collective-permute-start | bytes 589832 | tf_op jit(solution)/shard_map/ppermute | solution.py:48
  100.2 1.7 %collective-permute-start.27 = (f32[4,48,256]{2,1,0:T(8,128)}, f32[4,48,256]{2,1,0:T(8,128)S(1)}, u32[]{:S(2)}, u32[]{:S(2)}) collective-permute-start(f32[4,48,256]{2,1,0:T(8,128)} %shard_map.75.sa), channel_id=1, source_target_pairs={{0,1},{1,0},{2,3},{3,2},{4,5},{5,4},{6,7},{7,6},{8,9},{9,8},{10,11... | collective-permute-start | bytes 589832 | tf_op jit(solution)/shard_map/ppermute | solution.py:41
  101.8 0.9 copy-start.4
  118.8 30.7 %copy-start.3 = (f32[4,256,256]{2,1,0:T(8,128)S(1)}, f32[4,256,256]{2,1,0:T(8,128)}, u32[]{:S(2)}) copy-start(f32[4,256,256]{2,1,0:T(8,128)} %dinv.1) | copy-start | bytes 3145732
  147.7 1.9 %collective-permute-start.28 = (f32[16,4,8,256]{3,2,1,0:T(8,128)S(1)}, f32[16,4,8,256]{3,2,1,0:T(8,128)S(1)}, u32[]{:S(2)}, u32[]{:S(2)}) collective-permute-start(f32[16,4,8,256]{3,2,1,0:T(8,128)S(1)} %all_to_all.17.own), channel_id=1, source_target_pairs={{0,1},{1,0},{2,3},{3,2},{4,5},{5,4},{6,7},{7,6},{8,9},{9,8},{10,11... | collective-permute-start | bytes 1572872 | tf_op jit(solution)/shard_map/ppermute | solution.py:41
where the time goes:
time: 154 us; the launch traced here: 151 us
  starting transfers between devices  54.7 us (36%)
  blocking collectives  42.6 us (28%)
  waiting for transfers between devices  30.1 us (20%)
  Pallas kernels  18.2 us (12%)
  local copies, waits for them, and re-layouts  4.69 us (3%)
    ppermute x16, starting transfers between devices, shift_z(): return lax.ppermute(v, 'z', [(p, (p + d) % 8) for p in range(8)])  36.8 us
    all_to_all x1, blocking collectives, process(): total = jnp.sum(lax.all_to_all(spread, 'z', 0, 0), axis=0)  15.9 us
    ppermute x7, waiting for transfers between devices, shift_plane(): return lax.ppermute(v, ('y_hi', 'x'), pairs)  15.2 us
    all_to_all x1, blocking collectives, process(): total = jnp.sum(lax.all_to_all(term, PLANE, 0, 0), axis=0)  13.9 us
    all_to_all x1, blocking collectives, process(): total = lax.all_to_all(spread, PLANE, 0, 0)  12.8 us
    ppermute x7, starting transfers between devices, shift_plane(): return lax.ppermute(v, ('y_hi', 'x'), pairs)  11.3 us
    pallas_call x3, Pallas kernels, product(): call(functools.partial(product_body, flip, sides), [shape(8, 4, 48, 256)]...  9.1 us
    ppermute x16, waiting for transfers between devices, shift_z(): return lax.ppermute(v, 'z', [(p, (p + d) % 8) for p in range(8)])  6.56 us
  transfers between devices with their start and end apart: 29, of which 16 were waited for; matrix products, arithmetic and copies ran while one was open for 0% of the time, Pallas kernels for 5%

commit v1 on v0

--- a/solution.py
+++ b/solution.py
@@ -41,11 +41,12 @@
     return lax.ppermute(v, "core", [(0, 1), (1, 0)])
 
 
-def shift_plane(v, k):
-    pairs = []
-    for q in range(8):
-        pairs.append((q, (q // 4 + k // 4) % 2 * 4 + (q + k) % 4))
-    return lax.ppermute(v, ("y_hi", "x"), pairs)
+def flip_y(v):
+    return lax.ppermute(v, "y_hi", [(0, 1), (1, 0)])
+
+
+def shift_x(v, d):
+    return lax.ppermute(v, "x", [(p, (p + d) % 4) for p in range(4)])
 
 
 def call(body, outs, specs, scratch=(), flops=0, limit=8):
@@ -83,7 +84,7 @@
 
     @pl.loop(0, 16)
     def _(g):
-        place = (yh + g // 4) % 2 * 4 + (x + g) % 4
+        place = (yh + g) % 2 * 4 + (x + g // 2) % 4
         start = place * 32 + ((core + g // 8) % 2) * 16
         for i in range(3):
             at = pl.ds(pl.multiple_of(g * 48 + i * 16, 16), 16)
@@ -131,9 +132,35 @@
                 outs[n][k, s] = part if before is None else before[n][k, s] + part
 
 
-def halves_body(a, b, *outs):
-    for k in range(8):
-        outs[k][...] = a[k] + b[k]
+def spread_body(*refs):
+    rows, out, held = refs[:4], refs[4], refs[5]
+
+    @pl.loop(0, 4)
+    def _(s):
+        for k in range(8):
+            held[k * 48 : k * 48 + 48, :] = rows[k // 2][k % 2, s]
+        h, l = split_two(held[...].T)
+        for term, part in enumerate((h, l, h)):
+            out[s, :, term * 384 : term * 384 + 384] = part
+
+
+def pair_body(tab, keep, other, spread, *refs):
+    parts, (mine, yours, held, value) = refs[:4], refs[4:]
+    core = tab[2]
+
+    @pl.loop(0, 4)
+    def _(s):
+        for k in range(8):
+            part = keep[k, s] + other[k, s]
+            parts[k // 2][k % 2, s] = part
+            h, l = split_two(part)
+            for term, piece in enumerate((l, h, h)):
+                at = term * 384 + k * 48
+                held[at : at + 48, :] = piece
+        value[...] = jnp.dot(spread[s], held[...], preferred_element_type=F32)
+        for out, base in ((mine, core * 128), (yours, 128 - core * 128)):
+            for e in range(16):
+                out[e, s] = value[pl.ds(pl.multiple_of(base + e * 8, 8), 8), :]
 
 
 def sum_body(*refs):
@@ -141,23 +168,6 @@
     for r in refs[1:-1]:
         value = value + r[...]
     refs[-1][...] = value
-
-
-def term_body(tab, la, lb, sa, sb, out):
-    cols = pl.ds(pl.multiple_of(tab[2] * 128, 128), 128)
-
-    @pl.loop(0, 4)
-    def _(s):
-        value = [
-            lax.dot_general(
-                l[s, :, cols], r[s], (((0,), (0,)), ((), ())),
-                precision=HIGHEST, preferred_element_type=F32,
-            )
-            for l, r in ((la, sa), (lb, sb))
-        ]
-        total = value[0] + value[1]
-        for e in range(16):
-            out[e, s] = total[e * 8 : e * 8 + 8]
 
 
 def last_body(tab, own, other, dinv, out):
@@ -187,12 +197,19 @@
 
     arrived = to_columns(panel)
     lhat = normalize(0, panel)
-    mate = swap_core(lhat)
+    pair = jnp.stack([lhat, flip_y(lhat)])
     matrix = call(matrix_body, shape(2, 768, 1152, dtype=BF16), [SMEM, VMEM])(
         tab, ainv.reshape(4608, 128)
     )
-    arrived, mate, matrix = lax.optimization_barrier((arrived, mate, matrix))
+    arrived, pair, matrix = lax.optimization_barrier((arrived, pair, matrix))
     own = normalize(6, arrived)
+    near = [shift_x(pair, -d) for d in (1, 2, 3)]
+    spread = call(
+        spread_body,
+        shape(4, 256, 1152, dtype=BF16),
+        [VMEM] * 4,
+        [pltpu.VMEM((384, 256), F32)],
+    )(pair, *near)
 
     chains = []
     for first in (own, swap_y(own)):
@@ -213,21 +230,32 @@
         )(tab, matrix, *before, *chains[flip])
 
     keep, send = product(0, (0, 1))
+    keep, send, spread = lax.optimization_barrier((keep, send, spread))
     (send,) = product(1, (1,), send)
     other = swap_core(send)
     (keep,) = product(1, (0,), keep)
-    parts = call(halves_body, [shape(4, 48, 256)] * 8, [VMEM] * 2)(keep, other)
-    parts = [parts[0]] + [shift_plane(parts[k], k) for k in (6, 5, 7, 4, 2, 1, 3)]
-    shares = call(sum_body, shape(4, 48, 256), [VMEM] * 8)(*parts)
-
-    term = call(term_body, shape(16, 4, 8, 256), [SMEM] + [VMEM] * 4)(
-        tab, lhat, mate, shares, swap_core(shares)
-    )
-    total = jnp.sum(lax.all_to_all(term, PLANE, 0, 0), axis=0)
-    spread = jnp.broadcast_to(total[None], (8, 4, 8, 256))
-    total = jnp.sum(lax.all_to_all(spread, "z", 0, 0), axis=0)
-    spread = jnp.broadcast_to(total[None], (16, 4, 8, 256))
-    total = lax.all_to_all(spread, PLANE, 0, 0)
+    *parts, mine, yours = call(
+        pair_body,
+        [shape(2, 4, 48, 256)] * 4 + [shape(16, 4, 8, 256)] * 2,
+        [SMEM] + [VMEM] * 3,
+        [pltpu.VMEM((1152, 256), BF16), pltpu.VMEM((256, 256), F32)],
+        flops=6 * 256 * 384 * 1024,
+        limit=12,
+    )(tab, keep, other, spread)
+    term = mine + swap_core(yours)
+
+    term = lax.all_to_all(term, PLANE, 0, 0)
+    parts, term = lax.optimization_barrier((parts, term))
+    parts = [parts[0]] + [shift_x(parts[k], k) for k in (1, 2, 3)]
+    total = jnp.sum(term, axis=0)
+    total = lax.all_to_all(jnp.broadcast_to(total[None], (8, 4, 8, 256)), "z", 0, 0)
+    *parts, total = lax.optimization_barrier((*parts, total))
+    parts = call(sum_body, shape(2, 4, 48, 256), [VMEM] * 4)(*parts)
+    part = flip_y(parts[1])
+    total = jnp.sum(total, axis=0)
+    total = lax.all_to_all(jnp.broadcast_to(total[None], (16, 4, 8, 256)), PLANE, 0, 0)
+    part, total = lax.optimization_barrier((part, total))
+    shares = parts[0] + part
     diag = call(last_body, shape(4, 256, 256), [SMEM] + [VMEM] * 3)(
         tab, total, swap_core(total), dinv
     )

time: 154 us -> 150 us (0.974)
  blocking collectives: 42.6 us -> 15.3 us
  waiting for transfers between devices: 30.1 us -> 45.4 us
  starting transfers between devices: 54.7 us -> 62.7 us
    all_to_all x3 -> x1, blocking collectives: 42.6 us -> 15.3 us  [process(): term = lax.all_to_all(term, PLANE, 0, 0)]
    ppermute x7 -> x8, waiting for transfers between devices: 15.2 us -> 28.5 us  [the longest x6 18.1 us: shift_x(): return lax.ppermute(v, 'x', [(p, (p + d) % 4) for p in range(4)])]
    all_to_all x0 -> x2, starting transfers between devices: none -> 9.65 us  [the longest x1 5.55 us: process(): lax.all_to_all(jnp.broadcast_to(total[None], (16, 4, 8, 256)), PLANE, 0, 0)]
    ppermute x16, waiting for transfers between devices: 6.56 us -> 9.93 us  [shift_z(): return lax.ppermute(v, 'z', [(p, (p + d) % 8) for p in range(8)])]
    ppermute x16, starting transfers between devices: 36.8 us -> 34.8 us  [shift_z(): return lax.ppermute(v, 'z', [(p, (p + d) % 8) for p in range(8)])]
    unnamed x14 -> x12, local copies, waits for them, and re-layouts: 4.51 us -> 3.58 us
    ppermute x4 -> x3, waiting for transfers between devices: 4.23 us -> 3.68 us  [swap_core(): return lax.ppermute(v, 'core', [(0, 1), (1, 0)])]
    ppermute x7 -> x8, starting transfers between devices: 11.3 us -> 11.1 us  [the longest x2 6.34 us: flip_y(): return lax.ppermute(v, 'y_hi', [(0, 1), (1, 0)])]
  transfers between devices with their start and end apart: 29 -> 31, of which waited for: 16 -> 15; matrix products, arithmetic and copies ran while one was open for 0% -> 1% of each run, Pallas kernels for 5% -> 6%
where the time goes in v1:
time: 150 us; the launch traced here: 148 us
  starting transfers between devices  62.7 us (42%)
  waiting for transfers between devices  45.4 us (30%)
  Pallas kernels  17.9 us (12%)
  blocking collectives  15.3 us (10%)
  local copies, waits for them, and re-layouts  5.29 us (4%)
    ppermute x16, starting transfers between devices, shift_z(): return lax.ppermute(v, 'z', [(p, (p + d) % 8) for p in range(8)])  34.8 us
    ppermute x6, waiting for transfers between devices, shift_x(): return lax.ppermute(v, 'x', [(p, (p + d) % 4) for p in range(4)])  18.1 us
    all_to_all x1, blocking collectives, process(): term = lax.all_to_all(term, PLANE, 0, 0)  15.3 us
    ppermute x2, waiting for transfers between devices, flip_y(): return lax.ppermute(v, 'y_hi', [(0, 1), (1, 0)])  10.3 us
    ppermute x16, waiting for transfers between devices, shift_z(): return lax.ppermute(v, 'z', [(p, (p + d) % 8) for p in range(8)])  9.93 us
    pallas_call x3, Pallas kernels, product(): call(functools.partial(product_body, flip, sides), [shape(8, 4, 48, 256)]...  9.09 us
    ppermute x2, starting transfers between devices, flip_y(): return lax.ppermute(v, 'y_hi', [(0, 1), (1, 0)])  6.34 us
    all_to_all x1, starting transfers between devices, process(): lax.all_to_all(jnp.broadcast_to(total[None], (16, 4, 8, 256)), PLANE, 0, 0)  5.55 us
  transfers between devices with their start and end apart: 31, of which 15 were waited for; matrix products, arithmetic and copies ran while one was open for 1% of the time, Pallas kernels for 6%

profile of v1, /device:TPU:2, one launch (start us, length us, event | category | flops | bytes accessed | tf_op | source)
XLA Modules:
  0.0 148.4 jit_solution(3503604552910562798)
XLA Ops:
  0.7 0.1 concatenate.3.tab
  0.8 1.2 copy-done
  2.0 0.7 copy-done.4
  2.7 1.6 %shard_map.68 = f32[4,48,256]{2,1,0:T(8,128)S(1)} custom-call(s32[16]{0:T(128)S(1)} %concatenate.3.tab, s32[4,48]{1,0:T(4,128)S(1)} %copy-done.4, f32[4,48,256]{2,1,0:T(8,128)} %bitcast.7.panel, f32[4,256,256]{2,1,0:T(8,128)S(1)} %copy-done), custom_call_target="tpu_custom_call" | custom-call | bytes 4194304 | tf_op jit(solution)/shard_map/pallas_call | solution.py:194
  4.3 3.3 %collective-permute-start.1 = (f32[4,48,256]{2,1,0:T(8,128)S(1)}, f32[4,48,256]{2,1,0:T(8,128)S(1)}, u32[]{:S(2)}, u32[]{:S(2)}) collective-permute-start(f32[4,48,256]{2,1,0:T(8,128)S(1)} %shard_map.68), channel_id=1, source_target_pairs={{0,8},{8,0},{1,9},{9,1},{2,10},{10,2},{3,11},{11,3},{4,12},{12,4},... | collective-permute-start | bytes 589832 | tf_op jit(solution)/shard_map/ppermute | solution.py:45
  7.6 3.8 %collective-permute-start = (f32[4,48,256]{2,1,0:T(8,128)}, f32[4,48,256]{2,1,0:T(8,128)S(1)}, u32[]{:S(2)}, u32[]{:S(2)}) collective-permute-start(f32[4,48,256]{2,1,0:T(8,128)} %bitcast.7.panel), channel_id=1, source_target_pairs={{0,0},{1,64},{2,16},{3,96},{4,32},{5,112},{6,48},{7,80},{8,128},{9... | collective-permute-start | bytes 589832 | tf_op jit(solution)/shard_map/ppermute | solution.py:29
  11.4 0.0 copy-start.2
  11.4 1.7 %copy-done.2 = f32[3,1,256,3,1,256]{5,4,3,2,1,0:T(1,128)S(1)} copy-done((f32[3,1,256,3,1,256]{5,4,3,2,1,0:T(1,128)S(1)}, f32[3,1,256,3,1,256]{5,4,3,2,1,0:T(1,128)}, u32[]{:S(2)}) %copy-start.2) | copy-done | bytes 2359320
  13.1 1.4 shard_map.69.matrix
  14.5 3.4 %collective-permute-done.panel = f32[4,48,256]{2,1,0:T(8,128)S(1)} collective-permute-done((f32[4,48,256]{2,1,0:T(8,128)}, f32[4,48,256]{2,1,0:T(8,128)S(1)}, u32[]{:S(2)}, u32[]{:S(2)}) %collective-permute-start) | collective-permute-done | bytes 196640 | tf_op jit(solution)/shard_map/ppermute | solution.py:29
  17.9 1.3 shard_map.70.refs_0_
  19.2 3.1 %collective-permute-start.13 = (f32[4,48,256]{2,1,0:T(8,128)S(1)}, f32[4,48,256]{2,1,0:T(8,128)S(1)}, u32[]{:S(2)}, u32[]{:S(2)}) collective-permute-start(f32[4,48,256]{2,1,0:T(8,128)S(1)} %shard_map.70.refs_0_), channel_id=1, source_target_pairs={{0,128},{128,0},{1,129},{129,1},{2,130},{130,2},{3,131},{131,3},{4... | collective-permute-start | bytes 589832 | tf_op jit(solution)/shard_map/ppermute | solution.py:33
  22.2 9.1 %collective-permute-start.5 = (f32[4,48,256]{2,1,0:T(8,128)S(1)}, f32[4,48,256]{2,1,0:T(8,128)S(1)}, u32[]{:S(2)}, u32[]{:S(2)}) collective-permute-start(f32[4,48,256]{2,1,0:T(8,128)S(1)} %shard_map.70.refs_0_), channel_id=1, source_target_pairs={{0,112},{16,0},{32,16},{48,32},{64,48},{80,64},{96,80},{112,96},{1... | collective-permute-start | bytes 589832 | tf_op jit(solution)/shard_map/ppermute | solution.py:37
  31.3 0.0 collective-permute-start.2
  31.3 0.0 collective-permute-done.13.refs_1_
  31.3 4.0 %collective-permute-start.17 = (f32[4,48,256]{2,1,0:T(8,128)S(1)}, f32[4,48,256]{2,1,0:T(8,128)S(1)}, u32[]{:S(2)}, u32[]{:S(2)}) collective-permute-start(f32[4,48,256]{2,1,0:T(8,128)S(1)} %collective-permute-done.13.refs_1_), channel_id=1, source_target_pairs={{0,112},{16,0},{32,16},{48,32},{64,48},{80,64},{96,80},{112,96},{1... | collective-permute-start | bytes 589832 | tf_op jit(solution)/shard_map/ppermute | solution.py:37
  35.3 0.0 collective-permute-start.14
  35.3 0.0 collective-permute-done.5.refs_4_
  35.4 3.5 %collective-permute-start.6 = (f32[4,48,256]{2,1,0:T(8,128)S(1)}, f32[4,48,256]{2,1,0:T(8,128)S(1)}, u32[]{:S(2)}, u32[]{:S(2)}) collective-permute-start(f32[4,48,256]{2,1,0:T(8,128)S(1)} %collective-permute-done.5.refs_4_), channel_id=1, source_target_pairs={{0,112},{16,0},{32,16},{48,32},{64,48},{80,64},{96,80},{112,96},{1... | collective-permute-start | bytes 589832 | tf_op jit(solution)/shard_map/ppermute | solution.py:37
  38.8 0.0 collective-permute-done.2.refs_1_
  38.8 0.0 collective-permute-start.3
  38.8 0.9 collective-permute-done.17.refs_5_
  39.8 3.7 %collective-permute-start.18 = (f32[4,48,256]{2,1,0:T(8,128)S(1)}, f32[4,48,256]{2,1,0:T(8,128)S(1)}, u32[]{:S(2)}, u32[]{:S(2)}) collective-permute-start(f32[4,48,256]{2,1,0:T(8,128)S(1)} %collective-permute-done.17.refs_5_), channel_id=1, source_target_pairs={{0,112},{16,0},{32,16},{48,32},{64,48},{80,64},{96,80},{112,96},{1... | collective-permute-start | bytes 589832 | tf_op jit(solution)/shard_map/ppermute | solution.py:37
  43.5 0.7 collective-permute-done.14.refs_2_
  44.1 1.2 collective-permute-start.11
  45.3 2.5 %collective-permute-done.3.refs_2_ = f32[4,48,256]{2,1,0:T(8,128)S(1)} collective-permute-done((f32[4,48,256]{2,1,0:T(8,128)S(1)}, f32[4,48,256]{2,1,0:T(8,128)S(1)}, u32[]{:S(2)}, u32[]{:S(2)}) %collective-permute-start.3) | collective-permute-done | bytes 196640 | tf_op jit(solution)/shard_map/ppermute | solution.py:37
  47.8 0.0 collective-permute-start.10
  47.8 3.0 %collective-permute-start.7 = (f32[4,48,256]{2,1,0:T(8,128)S(1)}, f32[4,48,256]{2,1,0:T(8,128)S(1)}, u32[]{:S(2)}, u32[]{:S(2)}) collective-permute-start(f32[4,48,256]{2,1,0:T(8,128)S(1)} %collective-permute-done.6.refs_5_), channel_id=1, source_target_pairs={{0,112},{16,0},{32,16},{48,32},{64,48},{80,64},{96,80},{112,96},{1... | collective-permute-start | bytes 589832 | tf_op jit(solution)/shard_map/ppermute | solution.py:37
  50.8 0.2 collective-permute-done.15.refs_3_
  51.0 0.0 collective-permute-start.4
  51.0 3.5 %collective-permute-done.7.refs_6_ = f32[4,48,256]{2,1,0:T(8,128)S(1)} collective-permute-done((f32[4,48,256]{2,1,0:T(8,128)S(1)}, f32[4,48,256]{2,1,0:T(8,128)S(1)}, u32[]{:S(2)}, u32[]{:S(2)}) %collective-permute-start.7) | collective-permute-done | bytes 196640 | tf_op jit(solution)/shard_map/ppermute | solution.py:37
  54.5 3.7 %collective-permute-start.19 = (f32[4,48,256]{2,1,0:T(8,128)S(1)}, f32[4,48,256]{2,1,0:T(8,128)S(1)}, u32[]{:S(2)}, u32[]{:S(2)}) collective-permute-start(f32[4,48,256]{2,1,0:T(8,128)S(1)} %collective-permute-done.18.refs_6_), channel_id=1, source_target_pairs={{0,112},{16,0},{32,16},{48,32},{64,48},{80,64},{96,80},{112,96},{1... | collective-permute-start | bytes 589832 | tf_op jit(solution)/shard_map/ppermute | solution.py:37
  58.2 3.3 %collective-permute-start.9 = (f32[2,48,256]{2,1,0:T(8,128)S(1)}, f32[2,48,256]{2,1,0:T(8,128)S(1)}, u32[]{:S(2)}, u32[]{:S(2)}) collective-permute-start(f32[2,48,256]{2,1,0:T(8,128)S(1)} %slice.25), channel_id=1, source_target_pairs={{0,112},{16,0},{32,16},{48,32},{64,48},{80,64},{96,80},{112,96},{1... | collective-permute-start | bytes 294920 | tf_op jit(solution)/shard_map/ppermute | solution.py:37
  61.6 1.5 collective-permute-done.10.refs_1_
  63.0 0.7 shard_map.72.spread
  63.7 4.5 %collective-permute-start.21 = (f32[2,48,256]{2,1,0:T(8,128)S(1)}, f32[2,48,256]{2,1,0:T(8,128)S(1)}, u32[]{:S(2)}, u32[]{:S(2)}) collective-permute-start(f32[2,48,256]{2,1,0:T(8,128)S(1)} %slice.27), channel_id=1, source_target_pairs={{0,112},{16,0},{32,16},{48,32},{64,48},{80,64},{96,80},{112,96},{1... | collective-permute-start | bytes 294920 | tf_op jit(solution)/shard_map/ppermute | solution.py:37
  68.2 0.1 collective-permute-start.20
  68.3 3.7 %shard_map.71 = (f32[8,4,48,256]{3,2,1,0:T(8,128)S(1)}, f32[8,4,48,256]{3,2,1,0:T(8,128)S(1)}) custom-call(s32[16]{0:T(128)S(1)} %concatenate.3.tab, bf16[2,768,1152]{2,1,0:T(8,128)(2,1)S(1)} %shard_map.69.matrix, f32[4,48,256]{2,1,0:T(8,128)S(1)} %shard_map.70.refs_0_, f32[4,48,256]{2,1,0:T(8,128)S(1)} %collective-permute-done.2.refs_1_, ...), custom_call_target="tpu_custom_call" | custom-call | flops 1811939328 | bytes 4194304 | tf_op jit(solution)/shard_map/pallas_call | solution.py:223
  72.0 2.1 %collective-permute-done.20.refs_8_ = f32[2,48,256]{2,1,0:T(8,128)S(1)} collective-permute-done((f32[2,48,256]{2,1,0:T(8,128)S(1)}, f32[2,48,256]{2,1,0:T(8,128)S(1)}, u32[]{:S(2)}, u32[]{:S(2)}) %collective-permute-start.20) | collective-permute-done | bytes 98336 | tf_op jit(solution)/shard_map/ppermute | solution.py:37
  74.1 2.7 %shard_map.74 = f32[8,4,48,256]{3,2,1,0:T(8,128)S(1)} custom-call(s32[16]{0:T(128)S(1)} %concatenate.3.tab, bf16[2,768,1152]{2,1,0:T(8,128)(2,1)S(1)} %shard_map.69.matrix, f32[8,4,48,256]{3,2,1,0:T(8,128)S(1)} %get-tuple-element.34.refs_0_, f32[4,48,256]{2,1,0:T(8,128)S(1)} %collective-permute-done.13.refs_1_, ...), custom_call_target="tpu_custom_call" | custom-call | flops 905969664 | bytes 4194304 | tf_op jit(solution)/shard_map/pallas_call | solution.py:223
  76.8 0.1 collective-permute-start.22
  76.9 2.7 %shard_map.73.keep = f32[8,4,48,256]{3,2,1,0:T(8,128)S(1)} custom-call(s32[16]{0:T(128)S(1)} %concatenate.3.tab, bf16[2,768,1152]{2,1,0:T(8,128)(2,1)S(1)} %shard_map.69.matrix, f32[8,4,48,256]{3,2,1,0:T(8,128)S(1)} %get-tuple-element.33.refs_0_, f32[4,48,256]{2,1,0:T(8,128)S(1)} %collective-permute-done.13.refs_1_, ...), custom_call_target="tpu_custom_call" | custom-call | flops 905969664 | bytes 4194304 | tf_op jit(solution)/shard_map/pallas_call | solution.py:223
  79.6 0.7 collective-permute-done.22.other
  80.3 2.1 %shard_map.75 = (f32[2,4,48,256]{3,2,1,0:T(8,128)S(1)}, f32[2,4,48,256]{3,2,1,0:T(8,128)S(1)}, f32[2,4,48,256]{3,2,1,0:T(8,128)S(1)}, f32[2,4,48,256]{3,2,1,0:T(...) custom-call(s32[16]{0:T(128)S(1)} %concatenate.3.tab, f32[8,4,48,256]{3,2,1,0:T(8,128)S(1)} %shard_map.73.keep, ...), custom_call_target="tpu_custom_call" | custom-call | flops 603979776 | bytes 4194304 | tf_op jit(solution)/shard_map/pallas_call | solution.py:237
  82.4 0.2 collective-permute-start.23
  82.7 1.8 %collective-permute-done.23 = f32[16,4,8,256]{3,2,1,0:T(8,128)S(1)} collective-permute-done((f32[16,4,8,256]{3,2,1,0:T(8,128)S(1)}, f32[16,4,8,256]{3,2,1,0:T(8,128)S(1)}, u32[]{:S(2)}, u32[]{:S(2)}) %collective-permute-start.23) | collective-permute-done | bytes 524320 | tf_op jit(solution)/shard_map/ppermute | solution.py:41
  84.4 0.1 add.54
  84.5 15.3 %all_to_all.15 = f32[16,4,8,256]{3,2,1,0:T(8,128)S(1)} all-to-all(f32[16,4,8,256]{3,2,1,0:T(8,128)S(1)} %add.54), channel_id=1, replica_groups=mesh['y_lo'=2,'z'=8,'y_hi'=2,'x'=4,'core'=2] {'y_lo','y_hi','x'}, dimensions={0} | all-to-all | bytes 1048576 | tf_op jit(solution)/shard_map/all_to_all | solution.py:247
  99.8 0.7 broadcast_in_dim.39
  100.6 4.1 %all-to-all-start.1 = ((f32[8,4,8,256]{3,2,1,0:T(8,128)}), f32[8,4,8,256]{3,2,1,0:T(8,128)S(1)}, u32[]{:S(2)}, u32[]{:S(2)}) async-start(f32[8,4,8,256]{3,2,1,0:T(8,128)} %broadcast_in_dim.39), calls=%async_computation.1 | async-start | bytes 524288 | tf_op jit(solution)/shard_map/all_to_all | solution.py:251
  104.7 0.6 collective-permute-start.24
  105.2 3.0 %collective-permute-start.25 = (f32[2,4,48,256]{3,2,1,0:T(8,128)S(1)}, f32[2,4,48,256]{3,2,1,0:T(8,128)S(1)}, u32[]{:S(2)}, u32[]{:S(2)}) collective-permute-start(f32[2,4,48,256]{3,2,1,0:T(8,128)S(1)} %get-tuple-element.44), channel_id=1, source_target_pairs={{0,4},{2,6},{4,0},{6,2},{1,5},{3,7},{5,1},{7,3},{8,12},{10,14},{12... | collective-permute-start | bytes 1179656 | tf_op jit(solution)/shard_map/ppermute | solution.py:49
  108.2 0.1 collective-permute-start.26
  108.3 8.4 %collective-permute-done.24.refs_1_ = f32[2,4,48,256]{3,2,1,0:T(8,128)S(1)} collective-permute-done((f32[2,4,48,256]{3,2,1,0:T(8,128)S(1)}, f32[2,4,48,256]{3,2,1,0:T(8,128)S(1)}, u32[]{:S(2)}, u32[]{:S(2)}) %collective-permute-start.24) | collective-permute-done | bytes 393248 | tf_op jit(solution)/shard_map/ppermute | solution.py:49
  116.6 2.1 %collective-permute-done.25.refs_2_ = f32[2,4,48,256]{3,2,1,0:T(8,128)S(1)} collective-permute-done((f32[2,4,48,256]{3,2,1,0:T(8,128)S(1)}, f32[2,4,48,256]{3,2,1,0:T(8,128)S(1)}, u32[]{:S(2)}, u32[]{:S(2)}) %collective-permute-start.25) | collective-permute-done | bytes 393248 | tf_op jit(solution)/shard_map/ppermute | solution.py:49
  118.7 6.2 %collective-permute-done.26.refs_3_ = f32[2,4,48,256]{3,2,1,0:T(8,128)S(1)} collective-permute-done((f32[2,4,48,256]{3,2,1,0:T(8,128)S(1)}, f32[2,4,48,256]{3,2,1,0:T(8,128)S(1)}, u32[]{:S(2)}, u32[]{:S(2)}) %collective-permute-start.26) | collective-permute-done | bytes 393248 | tf_op jit(solution)/shard_map/ppermute | solution.py:49
  125.0 0.8 broadcast_in_dim.40
  125.8 5.5 %all-to-all-start.2 = ((f32[16,4,8,256]{3,2,1,0:T(8,128)}), f32[16,4,8,256]{3,2,1,0:T(8,128)S(1)}, u32[]{:S(2)}, u32[]{:S(2)}) async-start(f32[16,4,8,256]{3,2,1,0:T(8,128)} %broadcast_in_dim.40), calls=%async_computation.2 | async-start | bytes 1048576 | tf_op jit(solution)/shard_map/all_to_all | solution.py:256
  131.4 0.1 shard_map.76
  131.5 3.1 %collective-permute-start.27 = (f32[4,48,256]{2,1,0:T(8,128)S(1)}, f32[4,48,256]{2,1,0:T(8,128)S(1)}, u32[]{:S(2)}, u32[]{:S(2)}) collective-permute-start(f32[4,48,256]{2,1,0:T(8,128)S(1)} %slice_bitcast_fusion), channel_id=1, source_target_pairs={{0,8},{8,0},{1,9},{9,1},{2,10},{10,2},{3,11},{11,3},{4,12},{12,4},... | collective-permute-start | bytes 589832 | tf_op jit(solution)/shard_map/ppermute | solution.py:45
  134.5 10.3 %collective-permute-done.27 = f32[4,48,256]{2,1,0:T(8,128)S(1)} collective-permute-done((f32[4,48,256]{2,1,0:T(8,128)S(1)}, f32[4,48,256]{2,1,0:T(8,128)S(1)}, u32[]{:S(2)}, u32[]{:S(2)}) %collective-permute-start.27) | collective-permute-done | bytes 196640 | tf_op jit(solution)/shard_map/ppermute | solution.py:45
  144.8 0.7 fusion
  145.5 1.2 collective-permute-done.28.other
  146.7 1.7 %shard_map.77 = f32[4,256,256]{2,1,0:T(8,128)} custom-call(s32[16]{0:T(128)S(1)} %concatenate.3.tab, f32[16,4,8,256]{3,2,1,0:T(8,128)S(1)} %all-to-all-done.2.own, f32[16,4,8,256]{3,2,1,0:T(8,128)S(1)} %collective-permute-done.28.other, f32[4,256,256]{2,1,0:T(8,128)S(1)} %copy-done.3), custom_call_target="tpu_custom_call" | custom-call | bytes 4194304 | tf_op jit(solution)/shard_map/pallas_call | solution.py:259
  (35 shorter events, 0.2 us)
Async XLA Ops:
  0.8 1.2 copy-start
  2.0 0.7 copy-start.4
  4.3 10.1 %collective-permute-start.1 = (f32[4,48,256]{2,1,0:T(8,128)S(1)}, f32[4,48,256]{2,1,0:T(8,128)S(1)}, u32[]{:S(2)}, u32[]{:S(2)}) collective-permute-start(f32[4,48,256]{2,1,0:T(8,128)S(1)} %shard_map.68), channel_id=1, source_target_pairs={{0,8},{8,0},{1,9},{9,1},{2,10},{10,2},{3,11},{11,3},{4,12},{12,4},... | collective-permute-start | bytes 589832 | tf_op jit(solution)/shard_map/ppermute | solution.py:45
  7.6 10.3 %collective-permute-start = (f32[4,48,256]{2,1,0:T(8,128)}, f32[4,48,256]{2,1,0:T(8,128)S(1)}, u32[]{:S(2)}, u32[]{:S(2)}) collective-permute-start(f32[4,48,256]{2,1,0:T(8,128)} %bitcast.7.panel), channel_id=1, source_target_pairs={{0,0},{1,64},{2,16},{3,96},{4,32},{5,112},{6,48},{7,80},{8,128},{9... | collective-permute-start | bytes 589832 | tf_op jit(solution)/shard_map/ppermute | solution.py:29
  11.4 1.7 %copy-start.2 = (f32[3,1,256,3,1,256]{5,4,3,2,1,0:T(1,128)S(1)}, f32[3,1,256,3,1,256]{5,4,3,2,1,0:T(1,128)}, u32[]{:S(2)}) copy-start(f32[3,1,256,3,1,256]{5,4,3,2,1,0:T(1,128)} %param.5) | copy-start | bytes 7077892
  13.1 4.8 %copy-start.1 = (f32[4,256,256]{2,1,0:T(8,128)S(1)}, f32[4,256,256]{2,1,0:T(8,128)}, u32[]{:S(2)}) copy-start(f32[4,256,256]{2,1,0:T(8,128)} %inverse.3) | copy-start | bytes 3145732
  13.1 4.8 %copy-start.5 = (s32[4,48]{1,0:T(4,128)S(1)}, s32[4,48]{1,0:T(4,128)}, u32[]{:S(2)}) copy-start(s32[4,48]{1,0:T(4,128)} %present.3) | copy-start | bytes 2308
  19.2 12.1 %collective-permute-start.13 = (f32[4,48,256]{2,1,0:T(8,128)S(1)}, f32[4,48,256]{2,1,0:T(8,128)S(1)}, u32[]{:S(2)}, u32[]{:S(2)}) collective-permute-start(f32[4,48,256]{2,1,0:T(8,128)S(1)} %shard_map.70.refs_0_), channel_id=1, source_target_pairs={{0,128},{128,0},{1,129},{129,1},{2,130},{130,2},{3,131},{131,3},{4... | collective-permute-start | bytes 589832 | tf_op jit(solution)/shard_map/ppermute | solution.py:33
  22.2 13.1 %collective-permute-start.5 = (f32[4,48,256]{2,1,0:T(8,128)S(1)}, f32[4,48,256]{2,1,0:T(8,128)S(1)}, u32[]{:S(2)}, u32[]{:S(2)}) collective-permute-start(f32[4,48,256]{2,1,0:T(8,128)S(1)} %shard_map.70.refs_0_), channel_id=1, source_target_pairs={{0,112},{16,0},{32,16},{48,32},{64,48},{80,64},{96,80},{112,96},{1... | collective-permute-start | bytes 589832 | tf_op jit(solution)/shard_map/ppermute | solution.py:37
  31.3 7.5 %collective-permute-start.2 = (f32[4,48,256]{2,1,0:T(8,128)S(1)}, f32[4,48,256]{2,1,0:T(8,128)S(1)}, u32[]{:S(2)}, u32[]{:S(2)}) collective-permute-start(f32[4,48,256]{2,1,0:T(8,128)S(1)} %shard_map.70.refs_0_), channel_id=1, source_target_pairs={{0,16},{16,32},{32,48},{48,64},{64,80},{80,96},{96,112},{112,0},{1... | collective-permute-start | bytes 589832 | tf_op jit(solution)/shard_map/ppermute | solution.py:37
  31.3 8.5 %collective-permute-start.17 = (f32[4,48,256]{2,1,0:T(8,128)S(1)}, f32[4,48,256]{2,1,0:T(8,128)S(1)}, u32[]{:S(2)}, u32[]{:S(2)}) collective-permute-start(f32[4,48,256]{2,1,0:T(8,128)S(1)} %collective-permute-done.13.refs_1_), channel_id=1, source_target_pairs={{0,112},{16,0},{32,16},{48,32},{64,48},{80,64},{96,80},{112,96},{1... | collective-permute-start | bytes 589832 | tf_op jit(solution)/shard_map/ppermute | solution.py:37
  35.3 8.8 %collective-permute-start.14 = (f32[4,48,256]{2,1,0:T(8,128)S(1)}, f32[4,48,256]{2,1,0:T(8,128)S(1)}, u32[]{:S(2)}, u32[]{:S(2)}) collective-permute-start(f32[4,48,256]{2,1,0:T(8,128)S(1)} %collective-permute-done.13.refs_1_), channel_id=1, source_target_pairs={{0,16},{16,32},{32,48},{48,64},{64,80},{80,96},{96,112},{112,0},{1... | collective-permute-start | bytes 589832 | tf_op jit(solution)/shard_map/ppermute | solution.py:37
  35.4 8.8 %collective-permute-start.6 = (f32[4,48,256]{2,1,0:T(8,128)S(1)}, f32[4,48,256]{2,1,0:T(8,128)S(1)}, u32[]{:S(2)}, u32[]{:S(2)}) collective-permute-start(f32[4,48,256]{2,1,0:T(8,128)S(1)} %collective-permute-done.5.refs_4_), channel_id=1, source_target_pairs={{0,112},{16,0},{32,16},{48,32},{64,48},{80,64},{96,80},{112,96},{1... | collective-permute-start | bytes 589832 | tf_op jit(solution)/shard_map/ppermute | solution.py:37
  38.8 9.0 %collective-permute-start.3 = (f32[4,48,256]{2,1,0:T(8,128)S(1)}, f32[4,48,256]{2,1,0:T(8,128)S(1)}, u32[]{:S(2)}, u32[]{:S(2)}) collective-permute-start(f32[4,48,256]{2,1,0:T(8,128)S(1)} %collective-permute-done.2.refs_1_), channel_id=1, source_target_pairs={{0,16},{16,32},{32,48},{48,64},{64,80},{80,96},{96,112},{112,0},{1... | collective-permute-start | bytes 589832 | tf_op jit(solution)/shard_map/ppermute | solution.py:37
  39.8 8.1 %collective-permute-start.18 = (f32[4,48,256]{2,1,0:T(8,128)S(1)}, f32[4,48,256]{2,1,0:T(8,128)S(1)}, u32[]{:S(2)}, u32[]{:S(2)}) collective-permute-start(f32[4,48,256]{2,1,0:T(8,128)S(1)} %collective-permute-done.17.refs_5_), channel_id=1, source_target_pairs={{0,112},{16,0},{32,16},{48,32},{64,48},{80,64},{96,80},{112,96},{1... | collective-permute-start | bytes 589832 | tf_op jit(solution)/shard_map/ppermute | solution.py:37
  44.1 6.9 %collective-permute-start.15 = (f32[4,48,256]{2,1,0:T(8,128)S(1)}, f32[4,48,256]{2,1,0:T(8,128)S(1)}, u32[]{:S(2)}, u32[]{:S(2)}) collective-permute-start(f32[4,48,256]{2,1,0:T(8,128)S(1)} %collective-permute-done.14.refs_2_), channel_id=1, source_target_pairs={{0,16},{16,32},{32,48},{48,64},{64,80},{80,96},{96,112},{112,0},{1... | collective-permute-start | bytes 589832 | tf_op jit(solution)/shard_map/ppermute | solution.py:37
  44.1 14.1 %collective-permute-start.12 = (f32[2,4,48,256]{3,2,1,0:T(8,128)S(1)}, f32[2,4,48,256]{3,2,1,0:T(8,128)S(1)}, u32[]{:S(2)}, u32[]{:S(2)}) collective-permute-start(f32[2,4,48,256]{3,2,1,0:T(8,128)S(1)} %pad_maximum_fusion.refs_0_), channel_id=1, source_target_pairs={{0,2},{2,4},{4,6},{6,0},{1,3},{3,5},{5,7},{7,1},{8,10},{10,12},{12... | collective-permute-start | bytes 1179656 | tf_op jit(solution)/shard_map/ppermute | solution.py:49
  44.1 17.4 %collective-permute-start.11 = (f32[2,4,48,256]{3,2,1,0:T(8,128)S(1)}, f32[2,4,48,256]{3,2,1,0:T(8,128)S(1)}, u32[]{:S(2)}, u32[]{:S(2)}) collective-permute-start(f32[2,4,48,256]{3,2,1,0:T(8,128)S(1)} %pad_maximum_fusion.refs_0_), channel_id=1, source_target_pairs={{0,4},{2,6},{4,0},{6,2},{1,5},{3,7},{5,1},{7,3},{8,12},{10,14},{12... | collective-permute-start | bytes 1179656 | tf_op jit(solution)/shard_map/ppermute | solution.py:49
  47.8 15.2 %collective-permute-start.10 = (f32[2,4,48,256]{3,2,1,0:T(8,128)S(1)}, f32[2,4,48,256]{3,2,1,0:T(8,128)S(1)}, u32[]{:S(2)}, u32[]{:S(2)}) collective-permute-start(f32[2,4,48,256]{3,2,1,0:T(8,128)S(1)} %pad_maximum_fusion.refs_0_), channel_id=1, source_target_pairs={{0,6},{2,0},{4,2},{6,4},{1,7},{3,1},{5,3},{7,5},{8,14},{10,8},{12,... | collective-permute-start | bytes 1179656 | tf_op jit(solution)/shard_map/ppermute | solution.py:49
  47.8 6.7 %collective-permute-start.7 = (f32[4,48,256]{2,1,0:T(8,128)S(1)}, f32[4,48,256]{2,1,0:T(8,128)S(1)}, u32[]{:S(2)}, u32[]{:S(2)}) collective-permute-start(f32[4,48,256]{2,1,0:T(8,128)S(1)} %collective-permute-done.6.refs_5_), channel_id=1, source_target_pairs={{0,112},{16,0},{32,16},{48,32},{64,48},{80,64},{96,80},{112,96},{1... | collective-permute-start | bytes 589832 | tf_op jit(solution)/shard_map/ppermute | solution.py:37
  51.0 7.2 %collective-permute-start.4 = (f32[4,48,256]{2,1,0:T(8,128)S(1)}, f32[4,48,256]{2,1,0:T(8,128)S(1)}, u32[]{:S(2)}, u32[]{:S(2)}) collective-permute-start(f32[4,48,256]{2,1,0:T(8,128)S(1)} %collective-permute-done.3.refs_2_), channel_id=1, source_target_pairs={{0,16},{16,32},{32,48},{48,64},{64,80},{80,96},{96,112},{112,0},{1... | collective-permute-start | bytes 589832 | tf_op jit(solution)/shard_map/ppermute | solution.py:37
  54.5 9.2 %collective-permute-start.19 = (f32[4,48,256]{2,1,0:T(8,128)S(1)}, f32[4,48,256]{2,1,0:T(8,128)S(1)}, u32[]{:S(2)}, u32[]{:S(2)}) collective-permute-start(f32[4,48,256]{2,1,0:T(8,128)S(1)} %collective-permute-done.18.refs_6_), channel_id=1, source_target_pairs={{0,112},{16,0},{32,16},{48,32},{64,48},{80,64},{96,80},{112,96},{1... | collective-permute-start | bytes 589832 | tf_op jit(solution)/shard_map/ppermute | solution.py:37
  58.2 10.0 %collective-permute-start.16 = (f32[4,48,256]{2,1,0:T(8,128)S(1)}, f32[4,48,256]{2,1,0:T(8,128)S(1)}, u32[]{:S(2)}, u32[]{:S(2)}) collective-permute-start(f32[4,48,256]{2,1,0:T(8,128)S(1)} %collective-permute-done.15.refs_3_), channel_id=1, source_target_pairs={{0,16},{16,32},{32,48},{48,64},{64,80},{80,96},{96,112},{112,0},{1... | collective-permute-start | bytes 589832 | tf_op jit(solution)/shard_map/ppermute | solution.py:37
  58.2 10.1 %collective-permute-start.9 = (f32[2,48,256]{2,1,0:T(8,128)S(1)}, f32[2,48,256]{2,1,0:T(8,128)S(1)}, u32[]{:S(2)}, u32[]{:S(2)}) collective-permute-start(f32[2,48,256]{2,1,0:T(8,128)S(1)} %slice.25), channel_id=1, source_target_pairs={{0,112},{16,0},{32,16},{48,32},{64,48},{80,64},{96,80},{112,96},{1... | collective-permute-start | bytes 294920 | tf_op jit(solution)/shard_map/ppermute | solution.py:37
  61.5 6.8 %collective-permute-start.8 = (f32[2,48,256]{2,1,0:T(8,128)S(1)}, f32[2,48,256]{2,1,0:T(8,128)S(1)}, u32[]{:S(2)}, u32[]{:S(2)}) collective-permute-start(f32[2,48,256]{2,1,0:T(8,128)S(1)} %slice.24), channel_id=1, source_target_pairs={{0,16},{16,32},{32,48},{48,64},{64,80},{80,96},{96,112},{112,0},{1... | collective-permute-start | bytes 294920 | tf_op jit(solution)/shard_map/ppermute | solution.py:37
  63.7 8.3 %collective-permute-start.21 = (f32[2,48,256]{2,1,0:T(8,128)S(1)}, f32[2,48,256]{2,1,0:T(8,128)S(1)}, u32[]{:S(2)}, u32[]{:S(2)}) collective-permute-start(f32[2,48,256]{2,1,0:T(8,128)S(1)} %slice.27), channel_id=1, source_target_pairs={{0,112},{16,0},{32,16},{48,32},{64,48},{80,64},{96,80},{112,96},{1... | collective-permute-start | bytes 294920 | tf_op jit(solution)/shard_map/ppermute | solution.py:37
  68.2 5.9 %collective-permute-start.20 = (f32[2,48,256]{2,1,0:T(8,128)S(1)}, f32[2,48,256]{2,1,0:T(8,128)S(1)}, u32[]{:S(2)}, u32[]{:S(2)}) collective-permute-start(f32[2,48,256]{2,1,0:T(8,128)S(1)} %slice.26), channel_id=1, source_target_pairs={{0,16},{16,32},{32,48},{48,64},{64,80},{80,96},{96,112},{112,0},{1... | collective-permute-start | bytes 294920 | tf_op jit(solution)/shard_map/ppermute | solution.py:37
  76.8 3.5 %collective-permute-start.22 = (f32[8,4,48,256]{3,2,1,0:T(8,128)S(1)}, f32[8,4,48,256]{3,2,1,0:T(8,128)S(1)}, u32[]{:S(2)}, u32[]{:S(2)}) collective-permute-start(f32[8,4,48,256]{3,2,1,0:T(8,128)S(1)} %shard_map.74), channel_id=1, source_target_pairs={{0,1},{1,0},{2,3},{3,2},{4,5},{5,4},{6,7},{7,6},{8,9},{9,8},{10,11... | collective-permute-start | bytes 4718600 | tf_op jit(solution)/shard_map/ppermute | solution.py:41
  82.4 2.0 %collective-permute-start.23 = (f32[16,4,8,256]{3,2,1,0:T(8,128)S(1)}, f32[16,4,8,256]{3,2,1,0:T(8,128)S(1)}, u32[]{:S(2)}, u32[]{:S(2)}) collective-permute-start(f32[16,4,8,256]{3,2,1,0:T(8,128)S(1)} %get-tuple-element.41), channel_id=1, source_target_pairs={{0,1},{1,0},{2,3},{3,2},{4,5},{5,4},{6,7},{7,6},{8,9},{9,8},{10,11... | collective-permute-start | bytes 1572872 | tf_op jit(solution)/shard_map/ppermute | solution.py:41
  100.6 24.4 %all-to-all-start.1 = ((f32[8,4,8,256]{3,2,1,0:T(8,128)}), f32[8,4,8,256]{3,2,1,0:T(8,128)S(1)}, u32[]{:S(2)}, u32[]{:S(2)}) async-start(f32[8,4,8,256]{3,2,1,0:T(8,128)} %broadcast_in_dim.39), calls=%async_computation.1 | async-start | bytes 524288 | tf_op jit(solution)/shard_map/all_to_all | solution.py:251
  104.7 12.0 %collective-permute-start.24 = (f32[2,4,48,256]{3,2,1,0:T(8,128)S(1)}, f32[2,4,48,256]{3,2,1,0:T(8,128)S(1)}, u32[]{:S(2)}, u32[]{:S(2)}) collective-permute-start(f32[2,4,48,256]{3,2,1,0:T(8,128)S(1)} %get-tuple-element.43), channel_id=1, source_target_pairs={{0,2},{2,4},{4,6},{6,0},{1,3},{3,5},{5,7},{7,1},{8,10},{10,12},{12... | collective-permute-start | bytes 1179656 | tf_op jit(solution)/shard_map/ppermute | solution.py:49
  105.2 13.5 %collective-permute-start.25 = (f32[2,4,48,256]{3,2,1,0:T(8,128)S(1)}, f32[2,4,48,256]{3,2,1,0:T(8,128)S(1)}, u32[]{:S(2)}, u32[]{:S(2)}) collective-permute-start(f32[2,4,48,256]{3,2,1,0:T(8,128)S(1)} %get-tuple-element.44), channel_id=1, source_target_pairs={{0,4},{2,6},{4,0},{6,2},{1,5},{3,7},{5,1},{7,3},{8,12},{10,14},{12... | collective-permute-start | bytes 1179656 | tf_op jit(solution)/shard_map/ppermute | solution.py:49
  108.2 16.8 %collective-permute-start.26 = (f32[2,4,48,256]{3,2,1,0:T(8,128)S(1)}, f32[2,4,48,256]{3,2,1,0:T(8,128)S(1)}, u32[]{:S(2)}, u32[]{:S(2)}) collective-permute-start(f32[2,4,48,256]{3,2,1,0:T(8,128)S(1)} %get-tuple-element.45), channel_id=1, source_target_pairs={{0,6},{2,0},{4,2},{6,4},{1,7},{3,1},{5,3},{7,5},{8,14},{10,8},{12,... | collective-permute-start | bytes 1179656 | tf_op jit(solution)/shard_map/ppermute | solution.py:49
  125.8 19.0 %all-to-all-start.2 = ((f32[16,4,8,256]{3,2,1,0:T(8,128)}), f32[16,4,8,256]{3,2,1,0:T(8,128)S(1)}, u32[]{:S(2)}, u32[]{:S(2)}) async-start(f32[16,4,8,256]{3,2,1,0:T(8,128)} %broadcast_in_dim.40), calls=%async_computation.2 | async-start | bytes 1048576 | tf_op jit(solution)/shard_map/all_to_all | solution.py:256
  131.4 15.4 %copy-start.3 = (f32[4,256,256]{2,1,0:T(8,128)S(1)}, f32[4,256,256]{2,1,0:T(8,128)}, u32[]{:S(2)}) copy-start(f32[4,256,256]{2,1,0:T(8,128)} %dinv.1) | copy-start | bytes 3145732
  131.5 13.4 %collective-permute-start.27 = (f32[4,48,256]{2,1,0:T(8,128)S(1)}, f32[4,48,256]{2,1,0:T(8,128)S(1)}, u32[]{:S(2)}, u32[]{:S(2)}) collective-permute-start(f32[4,48,256]{2,1,0:T(8,128)S(1)} %slice_bitcast_fusion), channel_id=1, source_target_pairs={{0,8},{8,0},{1,9},{9,1},{2,10},{10,2},{3,11},{11,3},{4,12},{12,4},... | collective-permute-start | bytes 589832 | tf_op jit(solution)/shard_map/ppermute | solution.py:45
  144.8 1.9 %collective-permute-start.28 = (f32[16,4,8,256]{3,2,1,0:T(8,128)S(1)}, f32[16,4,8,256]{3,2,1,0:T(8,128)S(1)}, u32[]{:S(2)}, u32[]{:S(2)}) collective-permute-start(f32[16,4,8,256]{3,2,1,0:T(8,128)S(1)} %all-to-all-done.2.own), channel_id=1, source_target_pairs={{0,1},{1,0},{2,3},{3,2},{4,5},{5,4},{6,7},{7,6},{8,9},{9,8},{10,11... | collective-permute-start | bytes 1572872 | tf_op jit(solution)/shard_map/ppermute | solution.py:41

commit v2 on v1

--- a/solution.py
+++ b/solution.py
@@ -18,6 +18,8 @@
 SOURCE = tuple(LANDING.index(d) for d in range(8))
 SMEM = pl.BlockSpec(memory_space=pltpu.SMEM)
 VMEM = pl.BlockSpec(memory_space=pltpu.VMEM)
+HBM = pl.BlockSpec(memory_space=pltpu.MemorySpace.HBM)
+DMA = pltpu.SemaphoreType.DMA
 
 
 def to_columns(v):
@@ -70,6 +72,16 @@
     return high, (v - high.astype(F32)).astype(BF16)
 
 
+def fetched_body(tab, *refs):
+    sources, out, targets, sems = refs[:3], refs[3], refs[4:7], refs[7:]
+    copies = [pltpu.make_async_copy(*c) for c in zip(sources, targets, sems)]
+    for c in copies:
+        c.start()
+    for c in copies:
+        c.wait()
+    panel_body(0, tab, *targets, out)
+
+
 def panel_body(which, tab, present, panel, inverse, out):
     p = tab[which]
     for s in range(4):
@@ -79,14 +91,20 @@
             out[s, i * 16 : i * 16 + 16] = value[i * 16 : i * 16 + 16] * live
 
 
-def matrix_body(tab, a, out):
+def matrix_body(tab, source, out, a, *sems):
     core, x, yh = tab[2], tab[3], tab[5]
-
-    @pl.loop(0, 16)
-    def _(g):
-        place = (yh + g) % 2 * 4 + (x + g // 2) % 4
-        start = place * 32 + ((core + g // 8) % 2) * 16
-        for i in range(3):
+    copies = []
+    for i in range(3):
+        at = pl.ds(i * 1536, 1536)
+        copies.append(pltpu.make_async_copy(source.at[at], a.at[at], sems[i]))
+        copies[i].start()
+    for i in range(3):
+        copies[i].wait()
+
+        @pl.loop(0, 16)
+        def _(g):
+            place = (yh + g) % 2 * 4 + (x + g // 2) % 4
+            start = place * 32 + ((core + g // 8) % 2) * 16
             at = pl.ds(pl.multiple_of(g * 48 + i * 16, 16), 16)
             for j in range(3):
                 for half in range(2):
@@ -133,12 +151,12 @@
 
 
 def spread_body(*refs):
-    rows, out, held = refs[:4], refs[4], refs[5]
+    rows, out, held = refs[:2], refs[2], refs[3]
 
     @pl.loop(0, 4)
     def _(s):
         for k in range(8):
-            held[k * 48 : k * 48 + 48, :] = rows[k // 2][k % 2, s]
+            held[k * 48 : k * 48 + 48, :] = rows[k % 2][k // 2, s]
         h, l = split_two(held[...].T)
         for term, part in enumerate((h, l, h)):
             out[s, :, term * 384 : term * 384 + 384] = part
@@ -190,26 +208,36 @@
 
     panel = panel.reshape(4, 48, 256)
 
-    def normalize(which, rows):
-        return call(
-            functools.partial(panel_body, which), shape(4, 48, 256), [SMEM, SMEM, VMEM, VMEM]
-        )(tab, present, rows, diag_inv)
-
     arrived = to_columns(panel)
-    lhat = normalize(0, panel)
-    pair = jnp.stack([lhat, flip_y(lhat)])
-    matrix = call(matrix_body, shape(2, 768, 1152, dtype=BF16), [SMEM, VMEM])(
-        tab, ainv.reshape(4608, 128)
-    )
-    arrived, pair, matrix = lax.optimization_barrier((arrived, pair, matrix))
-    own = normalize(6, arrived)
-    near = [shift_x(pair, -d) for d in (1, 2, 3)]
+    lhat = call(
+        fetched_body,
+        shape(4, 48, 256),
+        [SMEM] + [HBM] * 3,
+        [
+            pltpu.SMEM((4, 48), jnp.int32),
+            pltpu.VMEM((4, 48, 256), F32),
+            pltpu.VMEM((4, 256, 256), F32),
+            DMA, DMA, DMA,
+        ],
+    )(tab, present, panel, diag_inv)
+    near = jnp.stack([lhat] + [shift_x(lhat, -d) for d in (1, 2, 3)])
+    matrix = call(
+        matrix_body,
+        shape(2, 768, 1152, dtype=BF16),
+        [SMEM, HBM],
+        [pltpu.VMEM((4608, 128), F32), DMA, DMA, DMA],
+    )(tab, ainv.reshape(4608, 128))
+    arrived, matrix = lax.optimization_barrier((arrived, matrix))
+    own = call(
+        functools.partial(panel_body, 6), shape(4, 48, 256), [SMEM, SMEM, VMEM, VMEM]
+    )(tab, present, arrived, diag_inv)
+    far = flip_y(near)
     spread = call(
         spread_body,
         shape(4, 256, 1152, dtype=BF16),
-        [VMEM] * 4,
+        [VMEM] * 2,
         [pltpu.VMEM((384, 256), F32)],
-    )(pair, *near)
+    )(near, far)
 
     chains = []
     for first in (own, swap_y(own)):
@@ -242,20 +270,16 @@
         flops=6 * 256 * 384 * 1024,
         limit=12,
     )(tab, keep, other, spread)
-    term = mine + swap_core(yours)
-
-    term = lax.all_to_all(term, PLANE, 0, 0)
-    parts, term = lax.optimization_barrier((parts, term))
     parts = [parts[0]] + [shift_x(parts[k], k) for k in (1, 2, 3)]
-    total = jnp.sum(term, axis=0)
-    total = lax.all_to_all(jnp.broadcast_to(total[None], (8, 4, 8, 256)), "z", 0, 0)
-    *parts, total = lax.optimization_barrier((*parts, total))
     parts = call(sum_body, shape(2, 4, 48, 256), [VMEM] * 4)(*parts)
     part = flip_y(parts[1])
+    shares = parts[0] + part
+
+    term = mine + swap_core(yours)
+    total = jnp.sum(lax.all_to_all(term, PLANE, 0, 0), axis=0)
+    total = lax.all_to_all(jnp.broadcast_to(total[None], (8, 4, 8, 256)), "z", 0, 0)
     total = jnp.sum(total, axis=0)
     total = lax.all_to_all(jnp.broadcast_to(total[None], (16, 4, 8, 256)), PLANE, 0, 0)
-    part, total = lax.optimization_barrier((part, total))
-    shares = parts[0] + part
     diag = call(last_body, shape(4, 256, 256), [SMEM] + [VMEM] * 3)(
         tab, total, swap_core(total), dinv
     )

time: 150 us -> 149 us (level)
  blocking collectives: 15.3 us -> 31.3 us
  waiting for transfers between devices: 45.4 us -> 32.7 us
  starting transfers between devices: 62.7 us -> 56.1 us
    all_to_all x1 -> x2, blocking collectives: 15.3 us -> 31.3 us  [the longest x1 16.6 us: process(): total = jnp.sum(lax.all_to_all(term, PLANE, 0, 0), axis=0)]
    ppermute x16, starting transfers between devices: 34.8 us -> 27.1 us  [shift_z(): return lax.ppermute(v, 'z', [(p, (p + d) % 8) for p in range(8)])]
    ppermute x6, starting transfers between devices: 4.78 us -> 12.3 us  [shift_x(): return lax.ppermute(v, 'x', [(p, (p + d) % 4) for p in range(4)])]
    ppermute x2, waiting for transfers between devices: 10.3 us -> 5.81 us  [flip_y(): return lax.ppermute(v, 'y_hi', [(0, 1), (1, 0)])]
    all_to_all x1 -> x0, starting transfers between devices: 4.1 us -> none  [process(): lax.all_to_all(jnp.broadcast_to(total[None], (8, 4, 8, 256)), 'z', 0, 0)]
    ppermute x1, waiting for transfers between devices: 3.38 us -> 0.01 us  [to_columns(): return lax.ppermute(v, AXES, pairs)]
    ppermute x16, waiting for transfers between devices: 9.93 us -> 6.63 us  [shift_z(): return lax.ppermute(v, 'z', [(p, (p + d) % 8) for p in range(8)])]
  transfers between devices with their start and end apart: 31 -> 30, of which waited for: 15 -> 12; matrix products, arithmetic and copies ran while one was open for 1% -> 1% of each run, Pallas kernels for 6% -> 9%
where the time goes in v2:
time: 149 us; the launch traced here: 146 us
  starting transfers between devices  56.1 us (38%)
  waiting for transfers between devices  32.7 us (22%)
  blocking collectives  31.3 us (21%)
  Pallas kernels  19 us (13%)
  local copies, waits for them, and re-layouts  5.5 us (4%)
    ppermute x16, starting transfers between devices, shift_z(): return lax.ppermute(v, 'z', [(p, (p + d) % 8) for p in range(8)])  27.1 us
    ppermute x6, waiting for transfers between devices, shift_x(): return lax.ppermute(v, 'x', [(p, (p + d) % 4) for p in range(4)])  17.3 us
    all_to_all x1, blocking collectives, process(): total = jnp.sum(lax.all_to_all(term, PLANE, 0, 0), axis=0)  16.6 us
    all_to_all x1, blocking collectives, process(): lax.all_to_all(jnp.broadcast_to(total[None], (8, 4, 8, 256)), 'z', 0, 0)  14.7 us
    ppermute x6, starting transfers between devices, shift_x(): return lax.ppermute(v, 'x', [(p, (p + d) % 4) for p in range(4)])  12.3 us
    pallas_call x3, Pallas kernels, product(): call(functools.partial(product_body, flip, sides), [shape(8, 4, 48, 256)]...  9.1 us
    ppermute x16, waiting for transfers between devices, shift_z(): return lax.ppermute(v, 'z', [(p, (p + d) % 8) for p in range(8)])  6.63 us
    ppermute x2, waiting for transfers between devices, flip_y(): return lax.ppermute(v, 'y_hi', [(0, 1), (1, 0)])  5.81 us
  transfers between devices with their start and end apart: 30, of which 12 were waited for; matrix products, arithmetic and copies ran while one was open for 1% of the time, Pallas kernels for 9%

profile of v2, /device:TPU:2, one launch (start us, length us, event | category | flops | bytes accessed | tf_op | source)
XLA Modules:
  0.0 146.5 jit_solution(8170955173399189606)
XLA Ops:
  0.6 3.8 %collective-permute-start = (f32[4,48,256]{2,1,0:T(8,128)}, f32[4,48,256]{2,1,0:T(8,128)S(1)}, u32[]{:S(2)}, u32[]{:S(2)}) collective-permute-start(f32[4,48,256]{2,1,0:T(8,128)} %bitcast.24), channel_id=1, source_target_pairs={{0,0},{1,64},{2,16},{3,96},{4,32},{5,112},{6,48},{7,80},{8,128},{9... | collective-permute-start | bytes 589832 | tf_op jit(solution)/shard_map/ppermute | solution.py:31
  4.5 0.1 concatenate.3.tab
  4.6 1.2 copy-done
  5.8 0.9 copy-done.4
  6.7 0.7 copy-done.5
  7.4 1.8 %shard_map.71 = f32[4,48,256]{2,1,0:T(8,128)S(1)} custom-call(s32[16]{0:T(128)S(1)} %concatenate.3.tab, s32[4,48]{1,0:T(4,128)S(1)} %copy-done.5, f32[4,48,256]{2,1,0:T(8,128)S(1)} %bitcast.25, f32[4,256,256]{2,1,0:T(8,128)S(1)} %copy-done), custom_call_target="tpu_custom_call" | custom-call | bytes 4194304 | tf_op jit(solution)/shard_map/pallas_call | solution.py:212
  9.3 2.9 %collective-permute-start.11 = (f32[4,48,256]{2,1,0:T(8,128)S(1)}, f32[4,48,256]{2,1,0:T(8,128)S(1)}, u32[]{:S(2)}, u32[]{:S(2)}) collective-permute-start(f32[4,48,256]{2,1,0:T(8,128)S(1)} %shard_map.71), channel_id=1, source_target_pairs={{0,2},{2,4},{4,6},{6,0},{1,3},{3,5},{5,7},{7,1},{8,10},{10,12},{12... | collective-permute-start | bytes 589832 | tf_op jit(solution)/shard_map/ppermute | solution.py:51
  12.2 2.1 %collective-permute-start.10 = (f32[4,48,256]{2,1,0:T(8,128)S(1)}, f32[4,48,256]{2,1,0:T(8,128)S(1)}, u32[]{:S(2)}, u32[]{:S(2)}) collective-permute-start(f32[4,48,256]{2,1,0:T(8,128)S(1)} %shard_map.71), channel_id=1, source_target_pairs={{0,4},{2,6},{4,0},{6,2},{1,5},{3,7},{5,1},{7,3},{8,12},{10,14},{12... | collective-permute-start | bytes 589832 | tf_op jit(solution)/shard_map/ppermute | solution.py:51
  14.2 2.5 %collective-permute-start.9 = (f32[4,48,256]{2,1,0:T(8,128)S(1)}, f32[4,48,256]{2,1,0:T(8,128)S(1)}, u32[]{:S(2)}, u32[]{:S(2)}) collective-permute-start(f32[4,48,256]{2,1,0:T(8,128)S(1)} %shard_map.71), channel_id=1, source_target_pairs={{0,6},{2,0},{4,2},{6,4},{1,7},{3,1},{5,3},{7,5},{8,14},{10,8},{12,... | collective-permute-start | bytes 589832 | tf_op jit(solution)/shard_map/ppermute | solution.py:51
  16.7 1.7 %copy-done.2 = f32[3,1,256,3,1,256]{5,4,3,2,1,0:T(1,128)S(1)} copy-done((f32[3,1,256,3,1,256]{5,4,3,2,1,0:T(1,128)S(1)}, f32[3,1,256,3,1,256]{5,4,3,2,1,0:T(1,128)}, u32[]{:S(2)}) %copy-start.2) | copy-done | bytes 2359320
  18.4 2.3 %shard_map.68.matrix = bf16[2,768,1152]{2,1,0:T(8,128)(2,1)S(1)} custom-call(s32[16]{0:T(128)S(1)} %concatenate.3.tab, f32[4608,128]{1,0:T(8,128)S(1)} %bitcast.22), custom_call_target="tpu_custom_call" | custom-call | bytes 4194304 | tf_op jit(solution)/shard_map/pallas_call | solution.py:224
  20.7 1.3 shard_map.69.refs_0_
  22.0 2.7 %collective-permute-start.13 = (f32[4,48,256]{2,1,0:T(8,128)S(1)}, f32[4,48,256]{2,1,0:T(8,128)S(1)}, u32[]{:S(2)}, u32[]{:S(2)}) collective-permute-start(f32[4,48,256]{2,1,0:T(8,128)S(1)} %shard_map.69.refs_0_), channel_id=1, source_target_pairs={{0,128},{128,0},{1,129},{129,1},{2,130},{130,2},{3,131},{131,3},{4... | collective-permute-start | bytes 589832 | tf_op jit(solution)/shard_map/ppermute | solution.py:35
  24.7 1.4 collective-permute-start.4
  26.1 0.0 collective-permute-done.11
  26.1 1.2 collective-permute-start.1
  27.3 0.0 collective-permute-done.9
  27.3 0.1 pad_maximum_fusion.refs_0_
  27.3 2.0 %collective-permute-start.12 = (f32[4,4,48,256]{3,2,1,0:T(8,128)S(1)}, f32[4,4,48,256]{3,2,1,0:T(8,128)S(1)}, u32[]{:S(2)}, u32[]{:S(2)}) collective-permute-start(f32[4,4,48,256]{3,2,1,0:T(8,128)S(1)} %pad_maximum_fusion.refs_0_), channel_id=1, source_target_pairs={{0,8},{8,0},{1,9},{9,1},{2,10},{10,2},{3,11},{11,3},{4,12},{12,4},... | collective-permute-start | bytes 2359304 | tf_op jit(solution)/shard_map/ppermute | solution.py:47
  29.3 0.4 collective-permute-done.13.refs_1_
  29.7 3.0 %collective-permute-start.17 = (f32[4,48,256]{2,1,0:T(8,128)S(1)}, f32[4,48,256]{2,1,0:T(8,128)S(1)}, u32[]{:S(2)}, u32[]{:S(2)}) collective-permute-start(f32[4,48,256]{2,1,0:T(8,128)S(1)} %collective-permute-done.13.refs_1_), channel_id=1, source_target_pairs={{0,112},{16,0},{32,16},{48,32},{64,48},{80,64},{96,80},{112,96},{1... | collective-permute-start | bytes 589832 | tf_op jit(solution)/shard_map/ppermute | solution.py:39
  32.7 0.0 collective-permute-start.14
  32.7 0.0 collective-permute-done.4.refs_4_
  32.7 3.2 %collective-permute-start.5 = (f32[4,48,256]{2,1,0:T(8,128)S(1)}, f32[4,48,256]{2,1,0:T(8,128)S(1)}, u32[]{:S(2)}, u32[]{:S(2)}) collective-permute-start(f32[4,48,256]{2,1,0:T(8,128)S(1)} %collective-permute-done.4.refs_4_), channel_id=1, source_target_pairs={{0,112},{16,0},{32,16},{48,32},{64,48},{80,64},{96,80},{112,96},{1... | collective-permute-start | bytes 589832 | tf_op jit(solution)/shard_map/ppermute | solution.py:39
  36.0 2.0 %collective-permute-done.17.refs_5_ = f32[4,48,256]{2,1,0:T(8,128)S(1)} collective-permute-done((f32[4,48,256]{2,1,0:T(8,128)S(1)}, f32[4,48,256]{2,1,0:T(8,128)S(1)}, u32[]{:S(2)}, u32[]{:S(2)}) %collective-permute-start.17) | collective-permute-done | bytes 196640 | tf_op jit(solution)/shard_map/ppermute | solution.py:39
  38.0 3.7 %collective-permute-start.18 = (f32[4,48,256]{2,1,0:T(8,128)S(1)}, f32[4,48,256]{2,1,0:T(8,128)S(1)}, u32[]{:S(2)}, u32[]{:S(2)}) collective-permute-start(f32[4,48,256]{2,1,0:T(8,128)S(1)} %collective-permute-done.17.refs_5_), channel_id=1, source_target_pairs={{0,112},{16,0},{32,16},{48,32},{64,48},{80,64},{96,80},{112,96},{1... | collective-permute-start | bytes 589832 | tf_op jit(solution)/shard_map/ppermute | solution.py:39
  41.7 0.0 collective-permute-done.14.refs_2_
  41.7 0.5 collective-permute-done.5.refs_5_
  42.2 3.7 %collective-permute-start.6 = (f32[4,48,256]{2,1,0:T(8,128)S(1)}, f32[4,48,256]{2,1,0:T(8,128)S(1)}, u32[]{:S(2)}, u32[]{:S(2)}) collective-permute-start(f32[4,48,256]{2,1,0:T(8,128)S(1)} %collective-permute-done.5.refs_5_), channel_id=1, source_target_pairs={{0,112},{16,0},{32,16},{48,32},{64,48},{80,64},{96,80},{112,96},{1... | collective-permute-start | bytes 589832 | tf_op jit(solution)/shard_map/ppermute | solution.py:39
  45.9 0.0 collective-permute-start.3
  45.9 0.8 collective-permute-done.18.refs_6_
  46.7 3.7 %collective-permute-start.19 = (f32[4,48,256]{2,1,0:T(8,128)S(1)}, f32[4,48,256]{2,1,0:T(8,128)S(1)}, u32[]{:S(2)}, u32[]{:S(2)}) collective-permute-start(f32[4,48,256]{2,1,0:T(8,128)S(1)} %collective-permute-done.18.refs_6_), channel_id=1, source_target_pairs={{0,112},{16,0},{32,16},{48,32},{64,48},{80,64},{96,80},{112,96},{1... | collective-permute-start | bytes 589832 | tf_op jit(solution)/shard_map/ppermute | solution.py:39
  50.4 0.8 collective-permute-done.6.refs_6_
  51.2 3.8 %collective-permute-start.8 = (f32[2,48,256]{2,1,0:T(8,128)S(1)}, f32[2,48,256]{2,1,0:T(8,128)S(1)}, u32[]{:S(2)}, u32[]{:S(2)}) collective-permute-start(f32[2,48,256]{2,1,0:T(8,128)S(1)} %slice.25), channel_id=1, source_target_pairs={{0,112},{16,0},{32,16},{48,32},{64,48},{80,64},{96,80},{112,96},{1... | collective-permute-start | bytes 294920 | tf_op jit(solution)/shard_map/ppermute | solution.py:39
  55.0 0.1 collective-permute-start.7
  55.1 3.3 %collective-permute-start.21 = (f32[2,48,256]{2,1,0:T(8,128)S(1)}, f32[2,48,256]{2,1,0:T(8,128)S(1)}, u32[]{:S(2)}, u32[]{:S(2)}) collective-permute-start(f32[2,48,256]{2,1,0:T(8,128)S(1)} %slice.27), channel_id=1, source_target_pairs={{0,112},{16,0},{32,16},{48,32},{64,48},{80,64},{96,80},{112,96},{1... | collective-permute-start | bytes 294920 | tf_op jit(solution)/shard_map/ppermute | solution.py:39
  58.5 0.1 collective-permute-start.20
  58.6 2.5 %collective-permute-done.7.refs_7_ = f32[2,48,256]{2,1,0:T(8,128)S(1)} collective-permute-done((f32[2,48,256]{2,1,0:T(8,128)S(1)}, f32[2,48,256]{2,1,0:T(8,128)S(1)}, u32[]{:S(2)}, u32[]{:S(2)}) %collective-permute-start.7) | collective-permute-done | bytes 98336 | tf_op jit(solution)/shard_map/ppermute | solution.py:39
  61.0 3.7 %shard_map.70 = (f32[8,4,48,256]{3,2,1,0:T(8,128)S(1)}, f32[8,4,48,256]{3,2,1,0:T(8,128)S(1)}) custom-call(s32[16]{0:T(128)S(1)} %concatenate.3.tab, bf16[2,768,1152]{2,1,0:T(8,128)(2,1)S(1)} %shard_map.68.matrix, f32[4,48,256]{2,1,0:T(8,128)S(1)} %shard_map.69.refs_0_, f32[4,48,256]{2,1,0:T(8,128)S(1)} %collective-permute-done.1.refs_1_, ...), custom_call_target="tpu_custom_call" | custom-call | flops 1811939328 | bytes 4194304 | tf_op jit(solution)/shard_map/pallas_call | solution.py:251
  64.7 0.7 shard_map.72.spread
  65.4 2.7 %shard_map.74 = f32[8,4,48,256]{3,2,1,0:T(8,128)S(1)} custom-call(s32[16]{0:T(128)S(1)} %concatenate.3.tab, bf16[2,768,1152]{2,1,0:T(8,128)(2,1)S(1)} %shard_map.68.matrix, f32[8,4,48,256]{3,2,1,0:T(8,128)S(1)} %get-tuple-element.20.refs_0_, f32[4,48,256]{2,1,0:T(8,128)S(1)} %collective-permute-done.13.refs_1_, ...), custom_call_target="tpu_custom_call" | custom-call | flops 905969664 | bytes 4194304 | tf_op jit(solution)/shard_map/pallas_call | solution.py:251
  68.1 0.1 collective-permute-start.22
  68.2 2.7 %shard_map.73.keep = f32[8,4,48,256]{3,2,1,0:T(8,128)S(1)} custom-call(s32[16]{0:T(128)S(1)} %concatenate.3.tab, bf16[2,768,1152]{2,1,0:T(8,128)(2,1)S(1)} %shard_map.68.matrix, f32[8,4,48,256]{3,2,1,0:T(8,128)S(1)} %get-tuple-element.19.refs_0_, f32[4,48,256]{2,1,0:T(8,128)S(1)} %collective-permute-done.13.refs_1_, ...), custom_call_target="tpu_custom_call" | custom-call | flops 905969664 | bytes 4194304 | tf_op jit(solution)/shard_map/pallas_call | solution.py:251
  71.0 0.7 collective-permute-done.22.other
  71.6 2.1 %shard_map.75 = (f32[2,4,48,256]{3,2,1,0:T(8,128)S(1)}, f32[2,4,48,256]{3,2,1,0:T(8,128)S(1)}, f32[2,4,48,256]{3,2,1,0:T(8,128)S(1)}, f32[2,4,48,256]{3,2,1,0:T(...) custom-call(s32[16]{0:T(128)S(1)} %concatenate.3.tab, f32[8,4,48,256]{3,2,1,0:T(8,128)S(1)} %shard_map.73.keep, ...), custom_call_target="tpu_custom_call" | custom-call | flops 603979776 | bytes 4194304 | tf_op jit(solution)/shard_map/pallas_call | solution.py:265
  73.7 0.2 collective-permute-start.27
  74.0 1.8 %collective-permute-done.27 = f32[16,4,8,256]{3,2,1,0:T(8,128)S(1)} collective-permute-done((f32[16,4,8,256]{3,2,1,0:T(8,128)S(1)}, f32[16,4,8,256]{3,2,1,0:T(8,128)S(1)}, u32[]{:S(2)}, u32[]{:S(2)}) %collective-permute-start.27) | collective-permute-done | bytes 524320 | tf_op jit(solution)/shard_map/ppermute | solution.py:43
  75.7 0.1 add.55
  75.8 16.6 %all_to_all.15 = f32[16,4,8,256]{3,2,1,0:T(8,128)S(1)} all-to-all(f32[16,4,8,256]{3,2,1,0:T(8,128)S(1)} %add.55), channel_id=1, replica_groups=mesh['y_lo'=2,'z'=8,'y_hi'=2,'x'=4,'core'=2] {'y_lo','y_hi','x'}, dimensions={0} | all-to-all | bytes 1048576 | tf_op jit(solution)/shard_map/all_to_all | solution.py:279
  92.5 14.7 %all_to_all.16 = f32[8,4,8,256]{3,2,1,0:T(8,128)S(1)} all-to-all(f32[8,4,8,256]{3,2,1,0:T(8,128)S(1)} %broadcast_in_dim.39), channel_id=1, replica_groups=mesh['y_lo'=2,'z'=8,'y_hi'=2,'x'=4,'core'=2] {'z'}, dimensions={0} | all-to-all | bytes 524288 | tf_op jit(solution)/shard_map/all_to_all | solution.py:280
  107.2 0.8 broadcast_in_dim.40
  108.1 4.8 %all-to-all-start.2 = ((f32[16,4,8,256]{3,2,1,0:T(8,128)}), f32[16,4,8,256]{3,2,1,0:T(8,128)S(1)}, u32[]{:S(2)}, u32[]{:S(2)}) async-start(f32[16,4,8,256]{3,2,1,0:T(8,128)} %broadcast_in_dim.40), calls=%async_computation.2 | async-start | bytes 1048576 | tf_op jit(solution)/shard_map/all_to_all | solution.py:282
  112.9 1.5 %collective-permute-start.23 = (f32[2,4,48,256]{3,2,1,0:T(8,128)S(1)}, f32[2,4,48,256]{3,2,1,0:T(8,128)S(1)}, u32[]{:S(2)}, u32[]{:S(2)}) collective-permute-start(f32[2,4,48,256]{3,2,1,0:T(8,128)S(1)} %get-tuple-element.23), channel_id=1, source_target_pairs={{0,2},{2,4},{4,6},{6,0},{1,3},{3,5},{5,7},{7,1},{8,10},{10,12},{12... | collective-permute-start | bytes 1179656 | tf_op jit(solution)/shard_map/ppermute | solution.py:51
  114.4 0.8 collective-permute-start.24
  115.2 2.4 %collective-permute-start.25 = (f32[2,4,48,256]{3,2,1,0:T(8,128)S(1)}, f32[2,4,48,256]{3,2,1,0:T(8,128)S(1)}, u32[]{:S(2)}, u32[]{:S(2)}) collective-permute-start(f32[2,4,48,256]{3,2,1,0:T(8,128)S(1)} %get-tuple-element.25), channel_id=1, source_target_pairs={{0,6},{2,0},{4,2},{6,4},{1,7},{3,1},{5,3},{7,5},{8,14},{10,8},{12,... | collective-permute-start | bytes 1179656 | tf_op jit(solution)/shard_map/ppermute | solution.py:51
  117.7 11.1 %collective-permute-done.23.refs_1_ = f32[2,4,48,256]{3,2,1,0:T(8,128)S(1)} collective-permute-done((f32[2,4,48,256]{3,2,1,0:T(8,128)S(1)}, f32[2,4,48,256]{3,2,1,0:T(8,128)S(1)}, u32[]{:S(2)}, u32[]{:S(2)}) %collective-permute-start.23) | collective-permute-done | bytes 393248 | tf_op jit(solution)/shard_map/ppermute | solution.py:51
  128.8 2.0 %collective-permute-done.24.refs_2_ = f32[2,4,48,256]{3,2,1,0:T(8,128)S(1)} collective-permute-done((f32[2,4,48,256]{3,2,1,0:T(8,128)S(1)}, f32[2,4,48,256]{3,2,1,0:T(8,128)S(1)}, u32[]{:S(2)}, u32[]{:S(2)}) %collective-permute-start.24) | collective-permute-done | bytes 393248 | tf_op jit(solution)/shard_map/ppermute | solution.py:51
  130.7 4.3 %collective-permute-done.25.refs_3_ = f32[2,4,48,256]{3,2,1,0:T(8,128)S(1)} collective-permute-done((f32[2,4,48,256]{3,2,1,0:T(8,128)S(1)}, f32[2,4,48,256]{3,2,1,0:T(8,128)S(1)}, u32[]{:S(2)}, u32[]{:S(2)}) %collective-permute-start.25) | collective-permute-done | bytes 393248 | tf_op jit(solution)/shard_map/ppermute | solution.py:51
  135.0 0.1 shard_map.76
  135.1 0.1 collective-permute-start.28
  135.2 3.1 %collective-permute-start.26 = (f32[4,48,256]{2,1,0:T(8,128)S(1)}, f32[4,48,256]{2,1,0:T(8,128)S(1)}, u32[]{:S(2)}, u32[]{:S(2)}) collective-permute-start(f32[4,48,256]{2,1,0:T(8,128)S(1)} %slice_bitcast_fusion), channel_id=1, source_target_pairs={{0,8},{8,0},{1,9},{9,1},{2,10},{10,2},{3,11},{11,3},{4,12},{12,4},... | collective-permute-start | bytes 589832 | tf_op jit(solution)/shard_map/ppermute | solution.py:47
  138.3 5.8 %collective-permute-done.26 = f32[4,48,256]{2,1,0:T(8,128)S(1)} collective-permute-done((f32[4,48,256]{2,1,0:T(8,128)S(1)}, f32[4,48,256]{2,1,0:T(8,128)S(1)}, u32[]{:S(2)}, u32[]{:S(2)}) %collective-permute-start.26) | collective-permute-done | bytes 196640 | tf_op jit(solution)/shard_map/ppermute | solution.py:47
  144.1 0.7 fusion
  144.8 1.7 %shard_map.77 = f32[4,256,256]{2,1,0:T(8,128)} custom-call(s32[16]{0:T(128)S(1)} %concatenate.3.tab, f32[16,4,8,256]{3,2,1,0:T(8,128)S(1)} %all-to-all-done.2.own, f32[16,4,8,256]{3,2,1,0:T(8,128)S(1)} %collective-permute-done.28.other, f32[4,256,256]{2,1,0:T(8,128)S(1)} %copy-done.3), custom_call_target="tpu_custom_call" | custom-call | bytes 4194304 | tf_op jit(solution)/shard_map/pallas_call | solution.py:283
  (34 shorter events, 0.2 us)
Async XLA Ops:
  0.6 20.1 %collective-permute-start = (f32[4,48,256]{2,1,0:T(8,128)}, f32[4,48,256]{2,1,0:T(8,128)S(1)}, u32[]{:S(2)}, u32[]{:S(2)}) collective-permute-start(f32[4,48,256]{2,1,0:T(8,128)} %bitcast.24), channel_id=1, source_target_pairs={{0,0},{1,64},{2,16},{3,96},{4,32},{5,112},{6,48},{7,80},{8,128},{9... | collective-permute-start | bytes 589832 | tf_op jit(solution)/shard_map/ppermute | solution.py:31
  4.6 1.2 copy-start
  5.8 0.9 copy-start.4
  6.7 0.7 copy-start.5
  9.3 16.8 %collective-permute-start.11 = (f32[4,48,256]{2,1,0:T(8,128)S(1)}, f32[4,48,256]{2,1,0:T(8,128)S(1)}, u32[]{:S(2)}, u32[]{:S(2)}) collective-permute-start(f32[4,48,256]{2,1,0:T(8,128)S(1)} %shard_map.71), channel_id=1, source_target_pairs={{0,2},{2,4},{4,6},{6,0},{1,3},{3,5},{5,7},{7,1},{8,10},{10,12},{12... | collective-permute-start | bytes 589832 | tf_op jit(solution)/shard_map/ppermute | solution.py:51
  12.2 15.1 %collective-permute-start.10 = (f32[4,48,256]{2,1,0:T(8,128)S(1)}, f32[4,48,256]{2,1,0:T(8,128)S(1)}, u32[]{:S(2)}, u32[]{:S(2)}) collective-permute-start(f32[4,48,256]{2,1,0:T(8,128)S(1)} %shard_map.71), channel_id=1, source_target_pairs={{0,4},{2,6},{4,0},{6,2},{1,5},{3,7},{5,1},{7,3},{8,12},{10,14},{12... | collective-permute-start | bytes 589832 | tf_op jit(solution)/shard_map/ppermute | solution.py:51
  14.2 13.1 %collective-permute-start.9 = (f32[4,48,256]{2,1,0:T(8,128)S(1)}, f32[4,48,256]{2,1,0:T(8,128)S(1)}, u32[]{:S(2)}, u32[]{:S(2)}) collective-permute-start(f32[4,48,256]{2,1,0:T(8,128)S(1)} %shard_map.71), channel_id=1, source_target_pairs={{0,6},{2,0},{4,2},{6,4},{1,7},{3,1},{5,3},{7,5},{8,14},{10,8},{12,... | collective-permute-start | bytes 589832 | tf_op jit(solution)/shard_map/ppermute | solution.py:51
  16.7 1.7 %copy-start.2 = (f32[3,1,256,3,1,256]{5,4,3,2,1,0:T(1,128)S(1)}, f32[3,1,256,3,1,256]{5,4,3,2,1,0:T(1,128)}, u32[]{:S(2)}) copy-start(f32[3,1,256,3,1,256]{5,4,3,2,1,0:T(1,128)} %param.5) | copy-start | bytes 7077892
  18.4 2.3 %copy-start.1 = (f32[4,256,256]{2,1,0:T(8,128)S(1)}, f32[4,256,256]{2,1,0:T(8,128)}, u32[]{:S(2)}) copy-start(f32[4,256,256]{2,1,0:T(8,128)} %refs_2_.1) | copy-start | bytes 3145732
  22.0 7.7 %collective-permute-start.13 = (f32[4,48,256]{2,1,0:T(8,128)S(1)}, f32[4,48,256]{2,1,0:T(8,128)S(1)}, u32[]{:S(2)}, u32[]{:S(2)}) collective-permute-start(f32[4,48,256]{2,1,0:T(8,128)S(1)} %shard_map.69.refs_0_), channel_id=1, source_target_pairs={{0,128},{128,0},{1,129},{129,1},{2,130},{130,2},{3,131},{131,3},{4... | collective-permute-start | bytes 589832 | tf_op jit(solution)/shard_map/ppermute | solution.py:35
  24.7 8.0 %collective-permute-start.4 = (f32[4,48,256]{2,1,0:T(8,128)S(1)}, f32[4,48,256]{2,1,0:T(8,128)S(1)}, u32[]{:S(2)}, u32[]{:S(2)}) collective-permute-start(f32[4,48,256]{2,1,0:T(8,128)S(1)} %shard_map.69.refs_0_), channel_id=1, source_target_pairs={{0,112},{16,0},{32,16},{48,32},{64,48},{80,64},{96,80},{112,96},{1... | collective-permute-start | bytes 589832 | tf_op jit(solution)/shard_map/ppermute | solution.py:39
  26.1 9.9 %collective-permute-start.1 = (f32[4,48,256]{2,1,0:T(8,128)S(1)}, f32[4,48,256]{2,1,0:T(8,128)S(1)}, u32[]{:S(2)}, u32[]{:S(2)}) collective-permute-start(f32[4,48,256]{2,1,0:T(8,128)S(1)} %shard_map.69.refs_0_), channel_id=1, source_target_pairs={{0,16},{16,32},{32,48},{48,64},{64,80},{80,96},{96,112},{112,0},{1... | collective-permute-start | bytes 589832 | tf_op jit(solution)/shard_map/ppermute | solution.py:39
  27.3 37.4 %collective-permute-start.12 = (f32[4,4,48,256]{3,2,1,0:T(8,128)S(1)}, f32[4,4,48,256]{3,2,1,0:T(8,128)S(1)}, u32[]{:S(2)}, u32[]{:S(2)}) collective-permute-start(f32[4,4,48,256]{3,2,1,0:T(8,128)S(1)} %pad_maximum_fusion.refs_0_), channel_id=1, source_target_pairs={{0,8},{8,0},{1,9},{9,1},{2,10},{10,2},{3,11},{11,3},{4,12},{12,4},... | collective-permute-start | bytes 2359304 | tf_op jit(solution)/shard_map/ppermute | solution.py:47
  29.7 8.3 %collective-permute-start.17 = (f32[4,48,256]{2,1,0:T(8,128)S(1)}, f32[4,48,256]{2,1,0:T(8,128)S(1)}, u32[]{:S(2)}, u32[]{:S(2)}) collective-permute-start(f32[4,48,256]{2,1,0:T(8,128)S(1)} %collective-permute-done.13.refs_1_), channel_id=1, source_target_pairs={{0,112},{16,0},{32,16},{48,32},{64,48},{80,64},{96,80},{112,96},{1... | collective-permute-start | bytes 589832 | tf_op jit(solution)/shard_map/ppermute | solution.py:39
  32.7 9.0 %collective-permute-start.14 = (f32[4,48,256]{2,1,0:T(8,128)S(1)}, f32[4,48,256]{2,1,0:T(8,128)S(1)}, u32[]{:S(2)}, u32[]{:S(2)}) collective-permute-start(f32[4,48,256]{2,1,0:T(8,128)S(1)} %collective-permute-done.13.refs_1_), channel_id=1, source_target_pairs={{0,16},{16,32},{32,48},{48,64},{64,80},{80,96},{96,112},{112,0},{1... | collective-permute-start | bytes 589832 | tf_op jit(solution)/shard_map/ppermute | solution.py:39
  32.7 9.5 %collective-permute-start.5 = (f32[4,48,256]{2,1,0:T(8,128)S(1)}, f32[4,48,256]{2,1,0:T(8,128)S(1)}, u32[]{:S(2)}, u32[]{:S(2)}) collective-permute-start(f32[4,48,256]{2,1,0:T(8,128)S(1)} %collective-permute-done.4.refs_4_), channel_id=1, source_target_pairs={{0,112},{16,0},{32,16},{48,32},{64,48},{80,64},{96,80},{112,96},{1... | collective-permute-start | bytes 589832 | tf_op jit(solution)/shard_map/ppermute | solution.py:39
  36.0 10.0 %collective-permute-start.2 = (f32[4,48,256]{2,1,0:T(8,128)S(1)}, f32[4,48,256]{2,1,0:T(8,128)S(1)}, u32[]{:S(2)}, u32[]{:S(2)}) collective-permute-start(f32[4,48,256]{2,1,0:T(8,128)S(1)} %collective-permute-done.1.refs_1_), channel_id=1, source_target_pairs={{0,16},{16,32},{32,48},{48,64},{64,80},{80,96},{96,112},{112,0},{1... | collective-permute-start | bytes 589832 | tf_op jit(solution)/shard_map/ppermute | solution.py:39
  38.0 8.7 %collective-permute-start.18 = (f32[4,48,256]{2,1,0:T(8,128)S(1)}, f32[4,48,256]{2,1,0:T(8,128)S(1)}, u32[]{:S(2)}, u32[]{:S(2)}) collective-permute-start(f32[4,48,256]{2,1,0:T(8,128)S(1)} %collective-permute-done.17.refs_5_), channel_id=1, source_target_pairs={{0,112},{16,0},{32,16},{48,32},{64,48},{80,64},{96,80},{112,96},{1... | collective-permute-start | bytes 589832 | tf_op jit(solution)/shard_map/ppermute | solution.py:39
  41.7 8.7 %collective-permute-start.15 = (f32[4,48,256]{2,1,0:T(8,128)S(1)}, f32[4,48,256]{2,1,0:T(8,128)S(1)}, u32[]{:S(2)}, u32[]{:S(2)}) collective-permute-start(f32[4,48,256]{2,1,0:T(8,128)S(1)} %collective-permute-done.14.refs_2_), channel_id=1, source_target_pairs={{0,16},{16,32},{32,48},{48,64},{64,80},{80,96},{96,112},{112,0},{1... | collective-permute-start | bytes 589832 | tf_op jit(solution)/shard_map/ppermute | solution.py:39
  42.2 9.0 %collective-permute-start.6 = (f32[4,48,256]{2,1,0:T(8,128)S(1)}, f32[4,48,256]{2,1,0:T(8,128)S(1)}, u32[]{:S(2)}, u32[]{:S(2)}) collective-permute-start(f32[4,48,256]{2,1,0:T(8,128)S(1)} %collective-permute-done.5.refs_5_), channel_id=1, source_target_pairs={{0,112},{16,0},{32,16},{48,32},{64,48},{80,64},{96,80},{112,96},{1... | collective-permute-start | bytes 589832 | tf_op jit(solution)/shard_map/ppermute | solution.py:39
  45.9 9.1 %collective-permute-start.3 = (f32[4,48,256]{2,1,0:T(8,128)S(1)}, f32[4,48,256]{2,1,0:T(8,128)S(1)}, u32[]{:S(2)}, u32[]{:S(2)}) collective-permute-start(f32[4,48,256]{2,1,0:T(8,128)S(1)} %collective-permute-done.2.refs_2_), channel_id=1, source_target_pairs={{0,16},{16,32},{32,48},{48,64},{64,80},{80,96},{96,112},{112,0},{1... | collective-permute-start | bytes 589832 | tf_op jit(solution)/shard_map/ppermute | solution.py:39
  46.7 8.4 %collective-permute-start.19 = (f32[4,48,256]{2,1,0:T(8,128)S(1)}, f32[4,48,256]{2,1,0:T(8,128)S(1)}, u32[]{:S(2)}, u32[]{:S(2)}) collective-permute-start(f32[4,48,256]{2,1,0:T(8,128)S(1)} %collective-permute-done.18.refs_6_), channel_id=1, source_target_pairs={{0,112},{16,0},{32,16},{48,32},{64,48},{80,64},{96,80},{112,96},{1... | collective-permute-start | bytes 589832 | tf_op jit(solution)/shard_map/ppermute | solution.py:39
  50.4 8.0 %collective-permute-start.16 = (f32[4,48,256]{2,1,0:T(8,128)S(1)}, f32[4,48,256]{2,1,0:T(8,128)S(1)}, u32[]{:S(2)}, u32[]{:S(2)}) collective-permute-start(f32[4,48,256]{2,1,0:T(8,128)S(1)} %collective-permute-done.15.refs_3_), channel_id=1, source_target_pairs={{0,16},{16,32},{32,48},{48,64},{64,80},{80,96},{96,112},{112,0},{1... | collective-permute-start | bytes 589832 | tf_op jit(solution)/shard_map/ppermute | solution.py:39
  51.2 7.3 %collective-permute-start.8 = (f32[2,48,256]{2,1,0:T(8,128)S(1)}, f32[2,48,256]{2,1,0:T(8,128)S(1)}, u32[]{:S(2)}, u32[]{:S(2)}) collective-permute-start(f32[2,48,256]{2,1,0:T(8,128)S(1)} %slice.25), channel_id=1, source_target_pairs={{0,112},{16,0},{32,16},{48,32},{64,48},{80,64},{96,80},{112,96},{1... | collective-permute-start | bytes 294920 | tf_op jit(solution)/shard_map/ppermute | solution.py:39
  55.0 6.0 %collective-permute-start.7 = (f32[2,48,256]{2,1,0:T(8,128)S(1)}, f32[2,48,256]{2,1,0:T(8,128)S(1)}, u32[]{:S(2)}, u32[]{:S(2)}) collective-permute-start(f32[2,48,256]{2,1,0:T(8,128)S(1)} %slice.24), channel_id=1, source_target_pairs={{0,16},{16,32},{32,48},{48,64},{64,80},{80,96},{96,112},{112,0},{1... | collective-permute-start | bytes 294920 | tf_op jit(solution)/shard_map/ppermute | solution.py:39
  55.1 10.3 %collective-permute-start.21 = (f32[2,48,256]{2,1,0:T(8,128)S(1)}, f32[2,48,256]{2,1,0:T(8,128)S(1)}, u32[]{:S(2)}, u32[]{:S(2)}) collective-permute-start(f32[2,48,256]{2,1,0:T(8,128)S(1)} %slice.27), channel_id=1, source_target_pairs={{0,112},{16,0},{32,16},{48,32},{64,48},{80,64},{96,80},{112,96},{1... | collective-permute-start | bytes 294920 | tf_op jit(solution)/shard_map/ppermute | solution.py:39
  58.5 7.0 %collective-permute-start.20 = (f32[2,48,256]{2,1,0:T(8,128)S(1)}, f32[2,48,256]{2,1,0:T(8,128)S(1)}, u32[]{:S(2)}, u32[]{:S(2)}) collective-permute-start(f32[2,48,256]{2,1,0:T(8,128)S(1)} %slice.26), channel_id=1, source_target_pairs={{0,16},{16,32},{32,48},{48,64},{64,80},{80,96},{96,112},{112,0},{1... | collective-permute-start | bytes 294920 | tf_op jit(solution)/shard_map/ppermute | solution.py:39
  68.1 3.5 %collective-permute-start.22 = (f32[8,4,48,256]{3,2,1,0:T(8,128)S(1)}, f32[8,4,48,256]{3,2,1,0:T(8,128)S(1)}, u32[]{:S(2)}, u32[]{:S(2)}) collective-permute-start(f32[8,4,48,256]{3,2,1,0:T(8,128)S(1)} %shard_map.74), channel_id=1, source_target_pairs={{0,1},{1,0},{2,3},{3,2},{4,5},{5,4},{6,7},{7,6},{8,9},{9,8},{10,11... | collective-permute-start | bytes 4718600 | tf_op jit(solution)/shard_map/ppermute | solution.py:43
  73.7 2.0 %collective-permute-start.27 = (f32[16,4,8,256]{3,2,1,0:T(8,128)S(1)}, f32[16,4,8,256]{3,2,1,0:T(8,128)S(1)}, u32[]{:S(2)}, u32[]{:S(2)}) collective-permute-start(f32[16,4,8,256]{3,2,1,0:T(8,128)S(1)} %get-tuple-element.27), channel_id=1, source_target_pairs={{0,1},{1,0},{2,3},{3,2},{4,5},{5,4},{6,7},{7,6},{8,9},{9,8},{10,11... | collective-permute-start | bytes 1572872 | tf_op jit(solution)/shard_map/ppermute | solution.py:43
  108.1 27.0 %all-to-all-start.2 = ((f32[16,4,8,256]{3,2,1,0:T(8,128)}), f32[16,4,8,256]{3,2,1,0:T(8,128)S(1)}, u32[]{:S(2)}, u32[]{:S(2)}) async-start(f32[16,4,8,256]{3,2,1,0:T(8,128)} %broadcast_in_dim.40), calls=%async_computation.2 | async-start | bytes 1048576 | tf_op jit(solution)/shard_map/all_to_all | solution.py:282
  112.9 31.9 %copy-start.3 = (f32[4,256,256]{2,1,0:T(8,128)S(1)}, f32[4,256,256]{2,1,0:T(8,128)}, u32[]{:S(2)}) copy-start(f32[4,256,256]{2,1,0:T(8,128)} %dinv.1) | copy-start | bytes 3145732
  112.9 15.9 %collective-permute-start.23 = (f32[2,4,48,256]{3,2,1,0:T(8,128)S(1)}, f32[2,4,48,256]{3,2,1,0:T(8,128)S(1)}, u32[]{:S(2)}, u32[]{:S(2)}) collective-permute-start(f32[2,4,48,256]{3,2,1,0:T(8,128)S(1)} %get-tuple-element.23), channel_id=1, source_target_pairs={{0,2},{2,4},{4,6},{6,0},{1,3},{3,5},{5,7},{7,1},{8,10},{10,12},{12... | collective-permute-start | bytes 1179656 | tf_op jit(solution)/shard_map/ppermute | solution.py:51
  114.4 16.3 %collective-permute-start.24 = (f32[2,4,48,256]{3,2,1,0:T(8,128)S(1)}, f32[2,4,48,256]{3,2,1,0:T(8,128)S(1)}, u32[]{:S(2)}, u32[]{:S(2)}) collective-permute-start(f32[2,4,48,256]{3,2,1,0:T(8,128)S(1)} %get-tuple-element.24), channel_id=1, source_target_pairs={{0,4},{2,6},{4,0},{6,2},{1,5},{3,7},{5,1},{7,3},{8,12},{10,14},{12... | collective-permute-start | bytes 1179656 | tf_op jit(solution)/shard_map/ppermute | solution.py:51
  115.2 19.8 %collective-permute-start.25 = (f32[2,4,48,256]{3,2,1,0:T(8,128)S(1)}, f32[2,4,48,256]{3,2,1,0:T(8,128)S(1)}, u32[]{:S(2)}, u32[]{:S(2)}) collective-permute-start(f32[2,4,48,256]{3,2,1,0:T(8,128)S(1)} %get-tuple-element.25), channel_id=1, source_target_pairs={{0,6},{2,0},{4,2},{6,4},{1,7},{3,1},{5,3},{7,5},{8,14},{10,8},{12,... | collective-permute-start | bytes 1179656 | tf_op jit(solution)/shard_map/ppermute | solution.py:51
  135.1 9.7 %collective-permute-start.28 = (f32[16,4,8,256]{3,2,1,0:T(8,128)S(1)}, f32[16,4,8,256]{3,2,1,0:T(8,128)S(1)}, u32[]{:S(2)}, u32[]{:S(2)}) collective-permute-start(f32[16,4,8,256]{3,2,1,0:T(8,128)S(1)} %all-to-all-done.2.own), channel_id=1, source_target_pairs={{0,1},{1,0},{2,3},{3,2},{4,5},{5,4},{6,7},{7,6},{8,9},{9,8},{10,11... | collective-permute-start | bytes 1572872 | tf_op jit(solution)/shard_map/ppermute | solution.py:43
  135.2 8.9 %collective-permute-start.26 = (f32[4,48,256]{2,1,0:T(8,128)S(1)}, f32[4,48,256]{2,1,0:T(8,128)S(1)}, u32[]{:S(2)}, u32[]{:S(2)}) collective-permute-start(f32[4,48,256]{2,1,0:T(8,128)S(1)} %slice_bitcast_fusion), channel_id=1, source_target_pairs={{0,8},{8,0},{1,9},{9,1},{2,10},{10,2},{3,11},{11,3},{4,12},{12,4},... | collective-permute-start | bytes 589832 | tf_op jit(solution)/shard_map/ppermute | solution.py:47

commit v3 on v2

--- a/solution.py
+++ b/solution.py
@@ -16,6 +16,7 @@
 PLANE = ("y_lo", "y_hi", "x")
 LANDING = (0, 4, 1, 6, 2, 7, 3, 5)
 SOURCE = tuple(LANDING.index(d) for d in range(8))
+STEPS = (0, 1, 2, 3, -1, -2, -3, 4)
 SMEM = pl.BlockSpec(memory_space=pltpu.SMEM)
 VMEM = pl.BlockSpec(memory_space=pltpu.VMEM)
 HBM = pl.BlockSpec(memory_space=pltpu.MemorySpace.HBM)
@@ -63,6 +64,10 @@
     )
 
 
+def in_hbm(v):
+    return pltpu.with_memory_space_constraint(v, pltpu.MemorySpace.HBM)
+
+
 def shape(*dims, dtype=F32):
     return jax.ShapeDtypeStruct(dims, dtype)
 
@@ -111,43 +116,28 @@
                     block = a[pl.ds(((i * 256 + start) * 3 + j) * 2 + half, 16, stride=6), :]
                     h, l = split_two(-block)
                     for term, part in enumerate((h, l, h)):
-                        col = term * 384 + j * 128
-                        out[half, at, col : col + 128] = part
-
-
-def product_body(flip, sides, tab, matrix, *refs):
-    n = len(sides)
-    before, pieces = (refs[:n], refs[n : n + 9]) if flip else (None, refs[:9])
-    outs, held = refs[-n - 1 : -1], refs[-1]
-    half = (tab[1] + flip) % 2
-
-    def put(block, d):
-        start = pl.multiple_of(tab[8 + d % 8], 16)
-        h, l = split_two(block)
-        for i in range(3):
-            for term, part in enumerate((l, h, h)):
-                held[pl.ds(term * 384 + i * 128 + start, 16), :] = part[i * 16 : i * 16 + 16]
+                        col = term * 768 + half * 384 + j * 128
+                        out[at, col : col + 128] = part
+
+
+def product_body(side, tab, matrix, *refs):
+    pieces, out, held = refs[:16], refs[16], refs[17]
 
     @pl.loop(0, 4)
     def _(s):
-        for ref, d in zip(pieces[:7], (0, 1, 2, 3, -1, -2, -3)):
-            put(ref[s], d)
-
-        @pl.when(s < 2)
-        def _():
-            put(pieces[7][s % 2], 4)
-
-        @pl.when(s >= 2)
-        def _():
-            put(pieces[8][s % 2], 4)
-
-        for n, c in enumerate(sides):
-            value = jnp.dot(
-                matrix[half, c * 384 : c * 384 + 384, :], held[...], preferred_element_type=F32
-            )
-            for k in range(8):
-                part = value[k * 48 : k * 48 + 48]
-                outs[n][k, s] = part if before is None else before[n][k, s] + part
+        for n, ref in enumerate(pieces):
+            half = (tab[1] + n // 8) % 2
+            start = pl.multiple_of(half * 384 + tab[8 + STEPS[n % 8] % 8], 16)
+            h, l = split_two(ref[s])
+            for i in range(3):
+                for term, part in enumerate((l, h, h)):
+                    at = pl.ds(term * 768 + i * 128 + start, 16)
+                    held[at, :] = part[i * 16 : i * 16 + 16]
+        value = jnp.dot(
+            matrix[side * 384 : side * 384 + 384, :], held[...], preferred_element_type=F32
+        )
+        for k in range(8):
+            out[k, s] = value[k * 48 : k * 48 + 48]
 
 
 def spread_body(*refs):
@@ -181,11 +171,9 @@
                 out[e, s] = value[pl.ds(pl.multiple_of(base + e * 8, 8), 8), :]
 
 
-def sum_body(*refs):
-    value = refs[0][...]
-    for r in refs[1:-1]:
-        value = value + r[...]
-    refs[-1][...] = value
+def sum_body(a, b, c, d, mine, yours):
+    for k, out in enumerate((mine, yours)):
+        out[...] = (a[k] + b[k]) + (c[k] + d[k])
 
 
 def last_body(tab, own, other, dinv, out):
@@ -219,14 +207,14 @@
             pltpu.VMEM((4, 256, 256), F32),
             DMA, DMA, DMA,
         ],
-    )(tab, present, panel, diag_inv)
+    )(tab, in_hbm(present), in_hbm(panel), in_hbm(diag_inv))
     near = jnp.stack([lhat] + [shift_x(lhat, -d) for d in (1, 2, 3)])
     matrix = call(
         matrix_body,
-        shape(2, 768, 1152, dtype=BF16),
+        shape(768, 2304, dtype=BF16),
         [SMEM, HBM],
         [pltpu.VMEM((4608, 128), F32), DMA, DMA, DMA],
-    )(tab, ainv.reshape(4608, 128))
+    )(tab, in_hbm(ainv.reshape(4608, 128)))
     arrived, matrix = lax.optimization_barrier((arrived, matrix))
     own = call(
         functools.partial(panel_body, 6), shape(4, 48, 256), [SMEM, SMEM, VMEM, VMEM]
@@ -239,29 +227,29 @@
         [pltpu.VMEM((384, 256), F32)],
     )(near, far)
 
-    chains = []
-    for first in (own, swap_y(own)):
-        a1, b1 = shift_z(first, 1), shift_z(first, -1)
-        a2, b2 = shift_z(a1, 1), shift_z(b1, -1)
-        a3, b3 = shift_z(a2, 1), shift_z(b2, -1)
-        a4, b4 = shift_z(a3[:2], 1), shift_z(b3[2:], -1)
-        chains.append((first, a1, a2, a3, b1, b2, b3, a4, b4))
-
-    def product(flip, sides, *before):
+    pieces = []
+    for flip, first in enumerate((own, swap_y(own))):
+        ahead, back = [first], [first]
+        for _ in range(3):
+            ahead.append(shift_z(ahead[-1], 1))
+            back.append(shift_z(back[-1], -1))
+        last = shift_z(back[-1], -1) if flip else shift_z(ahead[-1], 1)
+        pieces += ahead + back[1:] + [last]
+
+    def product(side):
         return call(
-            functools.partial(product_body, flip, sides),
-            [shape(8, 4, 48, 256)] * len(sides),
-            [SMEM] + [VMEM] * (1 + len(before) + 9),
-            [pltpu.VMEM((1152, 256), BF16)],
-            flops=3 * 768 * 384 * 1024 * len(sides),
+            functools.partial(product_body, side),
+            shape(8, 4, 48, 256),
+            [SMEM] + [VMEM] * 17,
+            [pltpu.VMEM((2304, 256), BF16)],
+            flops=6 * 384 * 768 * 1024,
             limit=12,
-        )(tab, matrix, *before, *chains[flip])
-
-    keep, send = product(0, (0, 1))
-    keep, send, spread = lax.optimization_barrier((keep, send, spread))
-    (send,) = product(1, (1,), send)
+        )(tab, matrix, *pieces)
+
+    send = product(1)
+    send, spread = lax.optimization_barrier((send, spread))
     other = swap_core(send)
-    (keep,) = product(1, (0,), keep)
+    keep = product(0)
     *parts, mine, yours = call(
         pair_body,
         [shape(2, 4, 48, 256)] * 4 + [shape(16, 4, 8, 256)] * 2,
@@ -271,15 +259,16 @@
         limit=12,
     )(tab, keep, other, spread)
     parts = [parts[0]] + [shift_x(parts[k], k) for k in (1, 2, 3)]
-    parts = call(sum_body, shape(2, 4, 48, 256), [VMEM] * 4)(*parts)
-    part = flip_y(parts[1])
-    shares = parts[0] + part
+    part, far = call(sum_body, [shape(4, 48, 256)] * 2, [VMEM] * 4)(*parts)
+    far = flip_y(far)
 
     term = mine + swap_core(yours)
     total = jnp.sum(lax.all_to_all(term, PLANE, 0, 0), axis=0)
     total = lax.all_to_all(jnp.broadcast_to(total[None], (8, 4, 8, 256)), "z", 0, 0)
     total = jnp.sum(total, axis=0)
     total = lax.all_to_all(jnp.broadcast_to(total[None], (16, 4, 8, 256)), PLANE, 0, 0)
+    total, far = lax.optimization_barrier((total, far))
+    shares = part + far
     diag = call(last_body, shape(4, 256, 256), [SMEM] + [VMEM] * 3)(
         tab, total, swap_core(total), dinv
     )

time: 149 us -> 134 us (0.90)
  the two profiles are of different devices: /device:TPU:2 before, /device:TPU:1 now
where the time goes in v3:
time: 134 us
  starting transfers between devices  54.3 us (41%)
  waiting for transfers between devices  38.1 us (28%)
  Pallas kernels  20.3 us (15%)
  blocking collectives  17.8 us (13%)
  local copies, waits for them, and re-layouts  1.67 us (1%)
    all_to_all x1, blocking collectives, process(): total = jnp.sum(lax.all_to_all(term, PLANE, 0, 0), axis=0)  17.8 us
    ppermute x14, starting transfers between devices, shift_z(): return lax.ppermute(v, 'z', [(p, (p + d) % 8) for p in range(8)])  17 us
    ppermute x14, waiting for transfers between devices, shift_z(): return lax.ppermute(v, 'z', [(p, (p + d) % 8) for p in range(8)])  12.8 us
    ppermute x1, starting transfers between devices, to_columns(): return lax.ppermute(v, AXES, pairs)  10.2 us
    ppermute x6, waiting for transfers between devices, shift_x(): return lax.ppermute(v, 'x', [(p, (p + d) % 4) for p in range(4)])  8.45 us
    pallas_call x2, Pallas kernels, product(): call(functools.partial(product_body, side), shape(8, 4, 48, 256), [SMEM]...  7.57 us
    ppermute x3, starting transfers between devices, swap_core(): return lax.ppermute(v, 'core', [(0, 1), (1, 0)])  7.43 us
    ppermute x2, waiting for transfers between devices, flip_y(): return lax.ppermute(v, 'y_hi', [(0, 1), (1, 0)])  7.25 us
  transfers between devices with their start and end apart: 29, of which 18 were waited for; matrix products, arithmetic and copies ran while one was open for 1% of the time, Pallas kernels for 9%

profile of v3, /device:TPU:1, one launch (start us, length us, event | category | flops | bytes accessed | tf_op | source)
XLA Modules:
  0.0 133.9 jit_solution(7000132221887650518)
XLA Ops:
  0.6 10.2 %collective-permute-start = (f32[4,48,256]{2,1,0:T(8,128)}, f32[4,48,256]{2,1,0:T(8,128)S(1)}, u32[]{:S(2)}, u32[]{:S(2)}) collective-permute-start(f32[4,48,256]{2,1,0:T(8,128)} %bitcast.22), channel_id=1, source_target_pairs={{0,0},{1,64},{2,16},{3,96},{4,32},{5,112},{6,48},{7,80},{8,128},{9... | collective-permute-start | bytes 589832 | tf_op jit(solution)/shard_map/ppermute | solution.py:32
  10.9 0.1 concatenate.3.tab
  11.0 2.6 %shard_map.72 = f32[4,48,256]{2,1,0:T(8,128)S(1)} custom-call(s32[16]{0:T(128)S(1)} %concatenate.3.tab, s32[4,48]{1,0:T(4,128)} %refs_0_.1, f32[4,48,256]{2,1,0:T(8,128)} %bitcast.23, f32[4,256,256]{2,1,0:T(8,128)} %refs_2_.1), custom_call_target="tpu_custom_call" | custom-call | bytes 4194304 | tf_op jit(solution)/shard_map/pallas_call | solution.py:200
  13.6 0.4 collective-permute-start.18
  14.0 2.8 %collective-permute-start.17 = (f32[4,48,256]{2,1,0:T(8,128)S(1)}, f32[4,48,256]{2,1,0:T(8,128)S(1)}, u32[]{:S(2)}, u32[]{:S(2)}) collective-permute-start(f32[4,48,256]{2,1,0:T(8,128)S(1)} %shard_map.72), channel_id=1, source_target_pairs={{0,4},{2,6},{4,0},{6,2},{1,5},{3,7},{5,1},{7,3},{8,12},{10,14},{12... | collective-permute-start | bytes 589832 | tf_op jit(solution)/shard_map/ppermute | solution.py:52
  16.8 0.3 collective-permute-start.16
  17.1 3.2 %shard_map.68.matrix = bf16[768,2304]{1,0:T(8,128)(2,1)S(1)} custom-call(s32[16]{0:T(128)S(1)} %concatenate.3.tab, f32[4608,128]{1,0:T(8,128)} %bitcast.17), custom_call_target="tpu_custom_call" | custom-call | bytes 4194304 | tf_op jit(solution)/shard_map/pallas_call | solution.py:212
  20.4 1.3 shard_map.69.refs_0_
  21.7 2.4 %collective-permute-start.8 = (f32[4,48,256]{2,1,0:T(8,128)S(1)}, f32[4,48,256]{2,1,0:T(8,128)S(1)}, u32[]{:S(2)}, u32[]{:S(2)}) collective-permute-start(f32[4,48,256]{2,1,0:T(8,128)S(1)} %shard_map.69.refs_0_), channel_id=1, source_target_pairs={{0,128},{128,0},{1,129},{129,1},{2,130},{130,2},{3,131},{131,3},{4... | collective-permute-start | bytes 589832 | tf_op jit(solution)/shard_map/ppermute | solution.py:36
  24.1 1.4 %collective-permute-done.17 = f32[4,48,256]{2,1,0:T(8,128)S(1)} collective-permute-done((f32[4,48,256]{2,1,0:T(8,128)S(1)}, f32[4,48,256]{2,1,0:T(8,128)S(1)}, u32[]{:S(2)}, u32[]{:S(2)}) %collective-permute-start.17) | collective-permute-done | bytes 196640 | tf_op jit(solution)/shard_map/ppermute | solution.py:52
  25.5 0.1 pad_maximum_fusion.refs_0_
  25.6 3.0 %collective-permute-start.19 = (f32[4,4,48,256]{3,2,1,0:T(8,128)S(1)}, f32[4,4,48,256]{3,2,1,0:T(8,128)S(1)}, u32[]{:S(2)}, u32[]{:S(2)}) collective-permute-start(f32[4,4,48,256]{3,2,1,0:T(8,128)S(1)} %pad_maximum_fusion.refs_0_), channel_id=1, source_target_pairs={{0,8},{8,0},{1,9},{9,1},{2,10},{10,2},{3,11},{11,3},{4,12},{12,4},... | collective-permute-start | bytes 2359304 | tf_op jit(solution)/shard_map/ppermute | solution.py:48
  28.6 2.2 %collective-permute-start.12 = (f32[4,48,256]{2,1,0:T(8,128)S(1)}, f32[4,48,256]{2,1,0:T(8,128)S(1)}, u32[]{:S(2)}, u32[]{:S(2)}) collective-permute-start(f32[4,48,256]{2,1,0:T(8,128)S(1)} %collective-permute-done.8.refs_8_), channel_id=1, source_target_pairs={{0,112},{16,0},{32,16},{48,32},{64,48},{80,64},{96,80},{112,96},{1... | collective-permute-start | bytes 589832 | tf_op jit(solution)/shard_map/ppermute | solution.py:40
  30.8 0.7 collective-permute-start.4
  31.5 0.1 collective-permute-done.1.refs_1_
  31.6 0.7 collective-permute-start.2
  32.3 0.0 collective-permute-start.9
  32.3 2.2 %collective-permute-done.12.refs_12_ = f32[4,48,256]{2,1,0:T(8,128)S(1)} collective-permute-done((f32[4,48,256]{2,1,0:T(8,128)S(1)}, f32[4,48,256]{2,1,0:T(8,128)S(1)}, u32[]{:S(2)}, u32[]{:S(2)}) %collective-permute-start.12) | collective-permute-done | bytes 196640 | tf_op jit(solution)/shard_map/ppermute | solution.py:40
  34.5 3.0 %collective-permute-start.13 = (f32[4,48,256]{2,1,0:T(8,128)S(1)}, f32[4,48,256]{2,1,0:T(8,128)S(1)}, u32[]{:S(2)}, u32[]{:S(2)}) collective-permute-start(f32[4,48,256]{2,1,0:T(8,128)S(1)} %collective-permute-done.12.refs_12_), channel_id=1, source_target_pairs={{0,112},{16,0},{32,16},{48,32},{64,48},{80,64},{96,80},{112,96},{1... | collective-permute-start | bytes 589832 | tf_op jit(solution)/shard_map/ppermute | solution.py:40
  37.5 1.2 collective-permute-done.4.refs_4_
  38.7 3.0 %collective-permute-start.5 = (f32[4,48,256]{2,1,0:T(8,128)S(1)}, f32[4,48,256]{2,1,0:T(8,128)S(1)}, u32[]{:S(2)}, u32[]{:S(2)}) collective-permute-start(f32[4,48,256]{2,1,0:T(8,128)S(1)} %collective-permute-done.4.refs_4_), channel_id=1, source_target_pairs={{0,112},{16,0},{32,16},{48,32},{64,48},{80,64},{96,80},{112,96},{1... | collective-permute-start | bytes 589832 | tf_op jit(solution)/shard_map/ppermute | solution.py:40
  41.8 0.0 collective-permute-done.9.refs_9_
  41.8 0.1 collective-permute-start.10
  41.9 1.1 collective-permute-done.13.refs_13_
  42.9 2.5 %collective-permute-start.14 = (f32[4,48,256]{2,1,0:T(8,128)S(1)}, f32[4,48,256]{2,1,0:T(8,128)S(1)}, u32[]{:S(2)}, u32[]{:S(2)}) collective-permute-start(f32[4,48,256]{2,1,0:T(8,128)S(1)} %collective-permute-done.13.refs_13_), channel_id=1, source_target_pairs={{0,112},{16,0},{32,16},{48,32},{64,48},{80,64},{96,80},{112,96},{1... | collective-permute-start | bytes 589832 | tf_op jit(solution)/shard_map/ppermute | solution.py:40
  45.4 1.7 %collective-permute-done.5.refs_5_ = f32[4,48,256]{2,1,0:T(8,128)S(1)} collective-permute-done((f32[4,48,256]{2,1,0:T(8,128)S(1)}, f32[4,48,256]{2,1,0:T(8,128)S(1)}, u32[]{:S(2)}, u32[]{:S(2)}) %collective-permute-start.5) | collective-permute-done | bytes 196640 | tf_op jit(solution)/shard_map/ppermute | solution.py:40
  47.1 2.5 %collective-permute-start.6 = (f32[4,48,256]{2,1,0:T(8,128)S(1)}, f32[4,48,256]{2,1,0:T(8,128)S(1)}, u32[]{:S(2)}, u32[]{:S(2)}) collective-permute-start(f32[4,48,256]{2,1,0:T(8,128)S(1)} %collective-permute-done.5.refs_5_), channel_id=1, source_target_pairs={{0,112},{16,0},{32,16},{48,32},{64,48},{80,64},{96,80},{112,96},{1... | collective-permute-start | bytes 589832 | tf_op jit(solution)/shard_map/ppermute | solution.py:40
  49.6 0.0 collective-permute-done.3.refs_3_
  49.6 0.0 collective-permute-start.7
  49.6 0.6 collective-permute-done.10.refs_10_
  50.2 0.1 collective-permute-start.11
  50.3 1.0 collective-permute-done.14.refs_14_
  51.3 2.2 %collective-permute-start.15 = (f32[4,48,256]{2,1,0:T(8,128)S(1)}, f32[4,48,256]{2,1,0:T(8,128)S(1)}, u32[]{:S(2)}, u32[]{:S(2)}) collective-permute-start(f32[4,48,256]{2,1,0:T(8,128)S(1)} %collective-permute-done.14.refs_14_), channel_id=1, source_target_pairs={{0,112},{16,0},{32,16},{48,32},{64,48},{80,64},{96,80},{112,96},{1... | collective-permute-start | bytes 589832 | tf_op jit(solution)/shard_map/ppermute | solution.py:40
  53.5 0.7 shard_map.73.spread
  54.2 1.0 collective-permute-done.6.refs_6_
  55.2 0.7 collective-permute-done.7.refs_7_
  55.9 2.1 %collective-permute-done.11.refs_11_ = f32[4,48,256]{2,1,0:T(8,128)S(1)} collective-permute-done((f32[4,48,256]{2,1,0:T(8,128)S(1)}, f32[4,48,256]{2,1,0:T(8,128)S(1)}, u32[]{:S(2)}, u32[]{:S(2)}) %collective-permute-start.11) | collective-permute-done | bytes 196640 | tf_op jit(solution)/shard_map/ppermute | solution.py:40
  58.0 1.1 collective-permute-done.15.refs_15_
  59.1 3.8 %shard_map.71 = f32[8,4,48,256]{3,2,1,0:T(8,128)S(1)} custom-call(s32[16]{0:T(128)S(1)} %concatenate.3.tab, bf16[768,2304]{1,0:T(8,128)(2,1)S(1)} %shard_map.68.matrix, f32[4,48,256]{2,1,0:T(8,128)S(1)} %shard_map.69.refs_0_, f32[4,48,256]{2,1,0:T(8,128)S(1)} %collective-permute-done.1.refs_1_, f32[4,48,256]{2,1,0:T(8,128)S(1)} %collective-permute-done.2.refs_2_, ...), custom_call_target="tpu_custom_call" | custom-call | flops 1811939328 | bytes 4194304 | tf_op jit(solution)/shard_map/pallas_call | solution.py:240
  62.9 4.2 %collective-permute-start.20 = (f32[8,4,48,256]{3,2,1,0:T(8,128)S(1)}, f32[8,4,48,256]{3,2,1,0:T(8,128)S(1)}, u32[]{:S(2)}, u32[]{:S(2)}) collective-permute-start(f32[8,4,48,256]{3,2,1,0:T(8,128)S(1)} %shard_map.71), channel_id=1, source_target_pairs={{0,1},{1,0},{2,3},{3,2},{4,5},{5,4},{6,7},{7,6},{8,9},{9,8},{10,11... | collective-permute-start | bytes 4718600 | tf_op jit(solution)/shard_map/ppermute | solution.py:44
  67.1 3.8 %shard_map.70.keep = f32[8,4,48,256]{3,2,1,0:T(8,128)S(1)} custom-call(s32[16]{0:T(128)S(1)} %concatenate.3.tab, bf16[768,2304]{1,0:T(8,128)(2,1)S(1)} %shard_map.68.matrix, f32[4,48,256]{2,1,0:T(8,128)S(1)} %shard_map.69.refs_0_, f32[4,48,256]{2,1,0:T(8,128)S(1)} %collective-permute-done.1.refs_1_, f32[4,48,256]{2,1,0:T(8,128)S(1)} %collective-permute-done.2.refs_2_, ...), custom_call_target="tpu_custom_call" | custom-call | flops 1811939328 | bytes 4194304 | tf_op jit(solution)/shard_map/pallas_call | solution.py:240
  70.9 3.2 %shard_map.74 = (f32[2,4,48,256]{3,2,1,0:T(8,128)S(1)}, f32[2,4,48,256]{3,2,1,0:T(8,128)}, f32[2,4,48,256]{3,2,1,0:T(8,128)}, f32[2,4,48,256]{3,2,1,0:T(8,128)},...) custom-call(s32[16]{0:T(128)S(1)} %concatenate.3.tab, f32[8,4,48,256]{3,2,1,0:T(8,128)S(1)} %shard_map.70.keep, ...), custom_call_target="tpu_custom_call" | custom-call | flops 603979776 | bytes 4194304 | tf_op jit(solution)/shard_map/pallas_call | solution.py:253
  74.0 0.0 collective-permute-start.24
  74.1 1.9 %collective-permute-done.24 = f32[16,4,8,256]{3,2,1,0:T(8,128)S(1)} collective-permute-done((f32[16,4,8,256]{3,2,1,0:T(8,128)S(1)}, f32[16,4,8,256]{3,2,1,0:T(8,128)S(1)}, u32[]{:S(2)}, u32[]{:S(2)}) %collective-permute-start.24) | collective-permute-done | bytes 524320 | tf_op jit(solution)/shard_map/ppermute | solution.py:44
  75.9 0.1 add.54
  76.0 17.8 %all_to_all.15 = f32[16,4,8,256]{3,2,1,0:T(8,128)S(1)} all-to-all(f32[16,4,8,256]{3,2,1,0:T(8,128)S(1)} %add.54), channel_id=1, replica_groups=mesh['y_lo'=2,'z'=8,'y_hi'=2,'x'=4,'core'=2] {'y_lo','y_hi','x'}, dimensions={0} | all-to-all | bytes 1048576 | tf_op jit(solution)/shard_map/all_to_all | solution.py:266
  93.9 0.7 broadcast_in_dim.39
  94.6 3.7 %all-to-all-start.1 = ((f32[8,4,8,256]{3,2,1,0:T(8,128)}), f32[8,4,8,256]{3,2,1,0:T(8,128)S(1)}, u32[]{:S(2)}, u32[]{:S(2)}) async-start(f32[8,4,8,256]{3,2,1,0:T(8,128)} %broadcast_in_dim.39), calls=%async_computation.1 | async-start | bytes 524288 | tf_op jit(solution)/shard_map/all_to_all | solution.py:267
  98.3 0.2 collective-permute-start.21
  98.5 1.2 collective-permute-start.22
  99.7 1.7 %collective-permute-start.23 = (f32[2,4,48,256]{3,2,1,0:T(8,128)}, f32[2,4,48,256]{3,2,1,0:T(8,128)S(1)}, u32[]{:S(2)}, u32[]{:S(2)}) collective-permute-start(f32[2,4,48,256]{3,2,1,0:T(8,128)} %get-tuple-element.23), channel_id=1, source_target_pairs={{0,6},{2,0},{4,2},{6,4},{1,7},{3,1},{5,3},{7,5},{8,14},{10,8},{12,... | collective-permute-start | bytes 1179656 | tf_op jit(solution)/shard_map/ppermute | solution.py:52
  101.4 6.9 %all-to-all-done.1 = f32[8,4,8,256]{3,2,1,0:T(8,128)S(1)} async-done(((f32[8,4,8,256]{3,2,1,0:T(8,128)}), f32[8,4,8,256]{3,2,1,0:T(8,128)S(1)}, u32[]{:S(2)}, u32[]{:S(2)}) %all-to-all-start.1) | async-done | bytes 262176 | tf_op jit(solution)/shard_map/all_to_all | solution.py:267
  108.3 0.8 broadcast_in_dim.40
  109.1 3.6 %all-to-all-start.2 = ((f32[16,4,8,256]{3,2,1,0:T(8,128)}), f32[16,4,8,256]{3,2,1,0:T(8,128)S(1)}, u32[]{:S(2)}, u32[]{:S(2)}) async-start(f32[16,4,8,256]{3,2,1,0:T(8,128)} %broadcast_in_dim.40), calls=%async_computation.2 | async-start | bytes 1048576 | tf_op jit(solution)/shard_map/all_to_all | solution.py:269
  112.7 0.0 collective-permute-done.21.b
  112.7 2.9 %collective-permute-done.22.c = f32[2,4,48,256]{3,2,1,0:T(8,128)S(1)} collective-permute-done((f32[2,4,48,256]{3,2,1,0:T(8,128)}, f32[2,4,48,256]{3,2,1,0:T(8,128)S(1)}, u32[]{:S(2)}, u32[]{:S(2)}) %collective-permute-start.22) | collective-permute-done | bytes 393248 | tf_op jit(solution)/shard_map/ppermute | solution.py:52
  115.7 4.1 %collective-permute-done.23.d = f32[2,4,48,256]{3,2,1,0:T(8,128)S(1)} collective-permute-done((f32[2,4,48,256]{3,2,1,0:T(8,128)}, f32[2,4,48,256]{3,2,1,0:T(8,128)S(1)}, u32[]{:S(2)}, u32[]{:S(2)}) %collective-permute-start.23) | collective-permute-done | bytes 393248 | tf_op jit(solution)/shard_map/ppermute | solution.py:52
  119.8 0.1 shard_map.75
  119.8 0.4 collective-permute-start.25
  120.2 7.2 %collective-permute-done.25 = f32[4,48,256]{2,1,0:T(8,128)S(1)} collective-permute-done((f32[4,48,256]{2,1,0:T(8,128)S(1)}, f32[4,48,256]{2,1,0:T(8,128)S(1)}, u32[]{:S(2)}, u32[]{:S(2)}) %collective-permute-start.25) | collective-permute-done | bytes 196640 | tf_op jit(solution)/shard_map/ppermute | solution.py:48
  127.5 3.2 %collective-permute-start.26 = (f32[16,4,8,256]{3,2,1,0:T(8,128)S(1)}, f32[16,4,8,256]{3,2,1,0:T(8,128)S(1)}, u32[]{:S(2)}, u32[]{:S(2)}) collective-permute-start(f32[16,4,8,256]{3,2,1,0:T(8,128)S(1)} %all-to-all-done.2.own), channel_id=1, source_target_pairs={{0,1},{1,0},{2,3},{3,2},{4,5},{5,4},{6,7},{7,6},{8,9},{9,8},{10,11... | collective-permute-start | bytes 1572872 | tf_op jit(solution)/shard_map/ppermute | solution.py:44
  130.7 0.7 add.55
  131.4 0.8 collective-permute-done.26.other
  132.2 1.6 %shard_map.76 = f32[4,256,256]{2,1,0:T(8,128)} custom-call(s32[16]{0:T(128)S(1)} %concatenate.3.tab, f32[16,4,8,256]{3,2,1,0:T(8,128)S(1)} %all-to-all-done.2.own, f32[16,4,8,256]{3,2,1,0:T(8,128)S(1)} %collective-permute-done.26.other, f32[4,256,256]{2,1,0:T(8,128)S(1)} %copy-done.1), custom_call_target="tpu_custom_call" | custom-call | bytes 4194304 | tf_op jit(solution)/shard_map/pallas_call | solution.py:272
  (19 shorter events, 0.1 us)
Async XLA Ops:
  0.6 19.7 %collective-permute-start = (f32[4,48,256]{2,1,0:T(8,128)}, f32[4,48,256]{2,1,0:T(8,128)S(1)}, u32[]{:S(2)}, u32[]{:S(2)}) collective-permute-start(f32[4,48,256]{2,1,0:T(8,128)} %bitcast.22), channel_id=1, source_target_pairs={{0,0},{1,64},{2,16},{3,96},{4,32},{5,112},{6,48},{7,80},{8,128},{9... | collective-permute-start | bytes 589832 | tf_op jit(solution)/shard_map/ppermute | solution.py:32
  13.6 10.5 %collective-permute-start.18 = (f32[4,48,256]{2,1,0:T(8,128)S(1)}, f32[4,48,256]{2,1,0:T(8,128)S(1)}, u32[]{:S(2)}, u32[]{:S(2)}) collective-permute-start(f32[4,48,256]{2,1,0:T(8,128)S(1)} %shard_map.72), channel_id=1, source_target_pairs={{0,2},{2,4},{4,6},{6,0},{1,3},{3,5},{5,7},{7,1},{8,10},{10,12},{12... | collective-permute-start | bytes 589832 | tf_op jit(solution)/shard_map/ppermute | solution.py:52
  14.0 11.5 %collective-permute-start.17 = (f32[4,48,256]{2,1,0:T(8,128)S(1)}, f32[4,48,256]{2,1,0:T(8,128)S(1)}, u32[]{:S(2)}, u32[]{:S(2)}) collective-permute-start(f32[4,48,256]{2,1,0:T(8,128)S(1)} %shard_map.72), channel_id=1, source_target_pairs={{0,4},{2,6},{4,0},{6,2},{1,5},{3,7},{5,1},{7,3},{8,12},{10,14},{12... | collective-permute-start | bytes 589832 | tf_op jit(solution)/shard_map/ppermute | solution.py:52
  16.8 8.7 %collective-permute-start.16 = (f32[4,48,256]{2,1,0:T(8,128)S(1)}, f32[4,48,256]{2,1,0:T(8,128)S(1)}, u32[]{:S(2)}, u32[]{:S(2)}) collective-permute-start(f32[4,48,256]{2,1,0:T(8,128)S(1)} %shard_map.72), channel_id=1, source_target_pairs={{0,6},{2,0},{4,2},{6,4},{1,7},{3,1},{5,3},{7,5},{8,14},{10,8},{12,... | collective-permute-start | bytes 589832 | tf_op jit(solution)/shard_map/ppermute | solution.py:52
  17.1 3.3 %copy-start = (f32[4,256,256]{2,1,0:T(8,128)S(1)}, f32[4,256,256]{2,1,0:T(8,128)}, u32[]{:S(2)}) copy-start(f32[4,256,256]{2,1,0:T(8,128)} %refs_2_.1) | copy-start | bytes 3145732
  17.1 3.3 %copy-start.2 = (s32[4,48]{1,0:T(4,128)S(1)}, s32[4,48]{1,0:T(4,128)}, u32[]{:S(2)}) copy-start(s32[4,48]{1,0:T(4,128)} %refs_0_.1) | copy-start | bytes 2308
  21.7 6.9 %collective-permute-start.8 = (f32[4,48,256]{2,1,0:T(8,128)S(1)}, f32[4,48,256]{2,1,0:T(8,128)S(1)}, u32[]{:S(2)}, u32[]{:S(2)}) collective-permute-start(f32[4,48,256]{2,1,0:T(8,128)S(1)} %shard_map.69.refs_0_), channel_id=1, source_target_pairs={{0,128},{128,0},{1,129},{129,1},{2,130},{130,2},{3,131},{131,3},{4... | collective-permute-start | bytes 589832 | tf_op jit(solution)/shard_map/ppermute | solution.py:36
  24.1 7.5 %collective-permute-start.1 = (f32[4,48,256]{2,1,0:T(8,128)S(1)}, f32[4,48,256]{2,1,0:T(8,128)S(1)}, u32[]{:S(2)}, u32[]{:S(2)}) collective-permute-start(f32[4,48,256]{2,1,0:T(8,128)S(1)} %shard_map.69.refs_0_), channel_id=1, source_target_pairs={{0,16},{16,32},{32,48},{48,64},{64,80},{80,96},{96,112},{112,0},{1... | collective-permute-start | bytes 589832 | tf_op jit(solution)/shard_map/ppermute | solution.py:40
  25.6 28.0 %collective-permute-start.19 = (f32[4,4,48,256]{3,2,1,0:T(8,128)S(1)}, f32[4,4,48,256]{3,2,1,0:T(8,128)S(1)}, u32[]{:S(2)}, u32[]{:S(2)}) collective-permute-start(f32[4,4,48,256]{3,2,1,0:T(8,128)S(1)} %pad_maximum_fusion.refs_0_), channel_id=1, source_target_pairs={{0,8},{8,0},{1,9},{9,1},{2,10},{10,2},{3,11},{11,3},{4,12},{12,4},... | collective-permute-start | bytes 2359304 | tf_op jit(solution)/shard_map/ppermute | solution.py:48
  28.6 5.9 %collective-permute-start.12 = (f32[4,48,256]{2,1,0:T(8,128)S(1)}, f32[4,48,256]{2,1,0:T(8,128)S(1)}, u32[]{:S(2)}, u32[]{:S(2)}) collective-permute-start(f32[4,48,256]{2,1,0:T(8,128)S(1)} %collective-permute-done.8.refs_8_), channel_id=1, source_target_pairs={{0,112},{16,0},{32,16},{48,32},{64,48},{80,64},{96,80},{112,96},{1... | collective-permute-start | bytes 589832 | tf_op jit(solution)/shard_map/ppermute | solution.py:40
  30.8 7.9 %collective-permute-start.4 = (f32[4,48,256]{2,1,0:T(8,128)S(1)}, f32[4,48,256]{2,1,0:T(8,128)S(1)}, u32[]{:S(2)}, u32[]{:S(2)}) collective-permute-start(f32[4,48,256]{2,1,0:T(8,128)S(1)} %shard_map.69.refs_0_), channel_id=1, source_target_pairs={{0,112},{16,0},{32,16},{48,32},{64,48},{80,64},{96,80},{112,96},{1... | collective-permute-start | bytes 589832 | tf_op jit(solution)/shard_map/ppermute | solution.py:40
  31.6 10.2 %collective-permute-start.2 = (f32[4,48,256]{2,1,0:T(8,128)S(1)}, f32[4,48,256]{2,1,0:T(8,128)S(1)}, u32[]{:S(2)}, u32[]{:S(2)}) collective-permute-start(f32[4,48,256]{2,1,0:T(8,128)S(1)} %collective-permute-done.1.refs_1_), channel_id=1, source_target_pairs={{0,16},{16,32},{32,48},{48,64},{64,80},{80,96},{96,112},{112,0},{1... | collective-permute-start | bytes 589832 | tf_op jit(solution)/shard_map/ppermute | solution.py:40
  32.3 9.5 %collective-permute-start.9 = (f32[4,48,256]{2,1,0:T(8,128)S(1)}, f32[4,48,256]{2,1,0:T(8,128)S(1)}, u32[]{:S(2)}, u32[]{:S(2)}) collective-permute-start(f32[4,48,256]{2,1,0:T(8,128)S(1)} %collective-permute-done.8.refs_8_), channel_id=1, source_target_pairs={{0,16},{16,32},{32,48},{48,64},{64,80},{80,96},{96,112},{112,0},{1... | collective-permute-start | bytes 589832 | tf_op jit(solution)/shard_map/ppermute | solution.py:40
  34.5 8.4 %collective-permute-start.13 = (f32[4,48,256]{2,1,0:T(8,128)S(1)}, f32[4,48,256]{2,1,0:T(8,128)S(1)}, u32[]{:S(2)}, u32[]{:S(2)}) collective-permute-start(f32[4,48,256]{2,1,0:T(8,128)S(1)} %collective-permute-done.12.refs_12_), channel_id=1, source_target_pairs={{0,112},{16,0},{32,16},{48,32},{64,48},{80,64},{96,80},{112,96},{1... | collective-permute-start | bytes 589832 | tf_op jit(solution)/shard_map/ppermute | solution.py:40
  38.7 8.4 %collective-permute-start.5 = (f32[4,48,256]{2,1,0:T(8,128)S(1)}, f32[4,48,256]{2,1,0:T(8,128)S(1)}, u32[]{:S(2)}, u32[]{:S(2)}) collective-permute-start(f32[4,48,256]{2,1,0:T(8,128)S(1)} %collective-permute-done.4.refs_4_), channel_id=1, source_target_pairs={{0,112},{16,0},{32,16},{48,32},{64,48},{80,64},{96,80},{112,96},{1... | collective-permute-start | bytes 589832 | tf_op jit(solution)/shard_map/ppermute | solution.py:40
  41.8 7.9 %collective-permute-start.3 = (f32[4,48,256]{2,1,0:T(8,128)S(1)}, f32[4,48,256]{2,1,0:T(8,128)S(1)}, u32[]{:S(2)}, u32[]{:S(2)}) collective-permute-start(f32[4,48,256]{2,1,0:T(8,128)S(1)} %collective-permute-done.2.refs_2_), channel_id=1, source_target_pairs={{0,16},{16,32},{32,48},{48,64},{64,80},{80,96},{96,112},{112,0},{1... | collective-permute-start | bytes 589832 | tf_op jit(solution)/shard_map/ppermute | solution.py:40
  41.8 8.4 %collective-permute-start.10 = (f32[4,48,256]{2,1,0:T(8,128)S(1)}, f32[4,48,256]{2,1,0:T(8,128)S(1)}, u32[]{:S(2)}, u32[]{:S(2)}) collective-permute-start(f32[4,48,256]{2,1,0:T(8,128)S(1)} %collective-permute-done.9.refs_9_), channel_id=1, source_target_pairs={{0,16},{16,32},{32,48},{48,64},{64,80},{80,96},{96,112},{112,0},{1... | collective-permute-start | bytes 589832 | tf_op jit(solution)/shard_map/ppermute | solution.py:40
  42.9 8.3 %collective-permute-start.14 = (f32[4,48,256]{2,1,0:T(8,128)S(1)}, f32[4,48,256]{2,1,0:T(8,128)S(1)}, u32[]{:S(2)}, u32[]{:S(2)}) collective-permute-start(f32[4,48,256]{2,1,0:T(8,128)S(1)} %collective-permute-done.13.refs_13_), channel_id=1, source_target_pairs={{0,112},{16,0},{32,16},{48,32},{64,48},{80,64},{96,80},{112,96},{1... | collective-permute-start | bytes 589832 | tf_op jit(solution)/shard_map/ppermute | solution.py:40
  47.1 8.1 %collective-permute-start.6 = (f32[4,48,256]{2,1,0:T(8,128)S(1)}, f32[4,48,256]{2,1,0:T(8,128)S(1)}, u32[]{:S(2)}, u32[]{:S(2)}) collective-permute-start(f32[4,48,256]{2,1,0:T(8,128)S(1)} %collective-permute-done.5.refs_5_), channel_id=1, source_target_pairs={{0,112},{16,0},{32,16},{48,32},{64,48},{80,64},{96,80},{112,96},{1... | collective-permute-start | bytes 589832 | tf_op jit(solution)/shard_map/ppermute | solution.py:40
  49.6 6.3 %collective-permute-start.7 = (f32[4,48,256]{2,1,0:T(8,128)S(1)}, f32[4,48,256]{2,1,0:T(8,128)S(1)}, u32[]{:S(2)}, u32[]{:S(2)}) collective-permute-start(f32[4,48,256]{2,1,0:T(8,128)S(1)} %collective-permute-done.3.refs_3_), channel_id=1, source_target_pairs={{0,16},{16,32},{32,48},{48,64},{64,80},{80,96},{96,112},{112,0},{1... | collective-permute-start | bytes 589832 | tf_op jit(solution)/shard_map/ppermute | solution.py:40
  50.2 7.8 %collective-permute-start.11 = (f32[4,48,256]{2,1,0:T(8,128)S(1)}, f32[4,48,256]{2,1,0:T(8,128)S(1)}, u32[]{:S(2)}, u32[]{:S(2)}) collective-permute-start(f32[4,48,256]{2,1,0:T(8,128)S(1)} %collective-permute-done.10.refs_10_), channel_id=1, source_target_pairs={{0,16},{16,32},{32,48},{48,64},{64,80},{80,96},{96,112},{112,0},{1... | collective-permute-start | bytes 589832 | tf_op jit(solution)/shard_map/ppermute | solution.py:40
  51.3 7.8 %collective-permute-start.15 = (f32[4,48,256]{2,1,0:T(8,128)S(1)}, f32[4,48,256]{2,1,0:T(8,128)S(1)}, u32[]{:S(2)}, u32[]{:S(2)}) collective-permute-start(f32[4,48,256]{2,1,0:T(8,128)S(1)} %collective-permute-done.14.refs_14_), channel_id=1, source_target_pairs={{0,112},{16,0},{32,16},{48,32},{64,48},{80,64},{96,80},{112,96},{1... | collective-permute-start | bytes 589832 | tf_op jit(solution)/shard_map/ppermute | solution.py:40
  62.9 8.0 %collective-permute-start.20 = (f32[8,4,48,256]{3,2,1,0:T(8,128)S(1)}, f32[8,4,48,256]{3,2,1,0:T(8,128)S(1)}, u32[]{:S(2)}, u32[]{:S(2)}) collective-permute-start(f32[8,4,48,256]{3,2,1,0:T(8,128)S(1)} %shard_map.71), channel_id=1, source_target_pairs={{0,1},{1,0},{2,3},{3,2},{4,5},{5,4},{6,7},{7,6},{8,9},{9,8},{10,11... | collective-permute-start | bytes 4718600 | tf_op jit(solution)/shard_map/ppermute | solution.py:44
  74.0 1.9 %collective-permute-start.24 = (f32[16,4,8,256]{3,2,1,0:T(8,128)S(1)}, f32[16,4,8,256]{3,2,1,0:T(8,128)S(1)}, u32[]{:S(2)}, u32[]{:S(2)}) collective-permute-start(f32[16,4,8,256]{3,2,1,0:T(8,128)S(1)} %get-tuple-element.26), channel_id=1, source_target_pairs={{0,1},{1,0},{2,3},{3,2},{4,5},{5,4},{6,7},{7,6},{8,9},{9,8},{10,11... | collective-permute-start | bytes 1572872 | tf_op jit(solution)/shard_map/ppermute | solution.py:44
  94.6 37.6 %copy-start.1 = (f32[4,256,256]{2,1,0:T(8,128)S(1)}, f32[4,256,256]{2,1,0:T(8,128)}, u32[]{:S(2)}) copy-start(f32[4,256,256]{2,1,0:T(8,128)} %dinv.1) | copy-start | bytes 3145732
  94.6 13.7 %all-to-all-start.1 = ((f32[8,4,8,256]{3,2,1,0:T(8,128)}), f32[8,4,8,256]{3,2,1,0:T(8,128)S(1)}, u32[]{:S(2)}, u32[]{:S(2)}) async-start(f32[8,4,8,256]{3,2,1,0:T(8,128)} %broadcast_in_dim.39), calls=%async_computation.1 | async-start | bytes 524288 | tf_op jit(solution)/shard_map/all_to_all | solution.py:267
  98.3 14.4 %collective-permute-start.21 = (f32[2,4,48,256]{3,2,1,0:T(8,128)}, f32[2,4,48,256]{3,2,1,0:T(8,128)S(1)}, u32[]{:S(2)}, u32[]{:S(2)}) collective-permute-start(f32[2,4,48,256]{3,2,1,0:T(8,128)} %get-tuple-element.21), channel_id=1, source_target_pairs={{0,2},{2,4},{4,6},{6,0},{1,3},{3,5},{5,7},{7,1},{8,10},{10,12},{12... | collective-permute-start | bytes 1179656 | tf_op jit(solution)/shard_map/ppermute | solution.py:52
  98.5 17.2 %collective-permute-start.22 = (f32[2,4,48,256]{3,2,1,0:T(8,128)}, f32[2,4,48,256]{3,2,1,0:T(8,128)S(1)}, u32[]{:S(2)}, u32[]{:S(2)}) collective-permute-start(f32[2,4,48,256]{3,2,1,0:T(8,128)} %get-tuple-element.22), channel_id=1, source_target_pairs={{0,4},{2,6},{4,0},{6,2},{1,5},{3,7},{5,1},{7,3},{8,12},{10,14},{12... | collective-permute-start | bytes 1179656 | tf_op jit(solution)/shard_map/ppermute | solution.py:52
  99.7 20.1 %collective-permute-start.23 = (f32[2,4,48,256]{3,2,1,0:T(8,128)}, f32[2,4,48,256]{3,2,1,0:T(8,128)S(1)}, u32[]{:S(2)}, u32[]{:S(2)}) collective-permute-start(f32[2,4,48,256]{3,2,1,0:T(8,128)} %get-tuple-element.23), channel_id=1, source_target_pairs={{0,6},{2,0},{4,2},{6,4},{1,7},{3,1},{5,3},{7,5},{8,14},{10,8},{12,... | collective-permute-start | bytes 1179656 | tf_op jit(solution)/shard_map/ppermute | solution.py:52
  109.1 18.3 %all-to-all-start.2 = ((f32[16,4,8,256]{3,2,1,0:T(8,128)}), f32[16,4,8,256]{3,2,1,0:T(8,128)S(1)}, u32[]{:S(2)}, u32[]{:S(2)}) async-start(f32[16,4,8,256]{3,2,1,0:T(8,128)} %broadcast_in_dim.40), calls=%async_computation.2 | async-start | bytes 1048576 | tf_op jit(solution)/shard_map/all_to_all | solution.py:269
  119.8 7.6 %collective-permute-start.25 = (f32[4,48,256]{2,1,0:T(8,128)S(1)}, f32[4,48,256]{2,1,0:T(8,128)S(1)}, u32[]{:S(2)}, u32[]{:S(2)}) collective-permute-start(f32[4,48,256]{2,1,0:T(8,128)S(1)} %get-tuple-element.27), channel_id=1, source_target_pairs={{0,8},{8,0},{1,9},{9,1},{2,10},{10,2},{3,11},{11,3},{4,12},{12,4},... | collective-permute-start | bytes 589832 | tf_op jit(solution)/shard_map/ppermute | solution.py:48
  127.5 4.8 %collective-permute-start.26 = (f32[16,4,8,256]{3,2,1,0:T(8,128)S(1)}, f32[16,4,8,256]{3,2,1,0:T(8,128)S(1)}, u32[]{:S(2)}, u32[]{:S(2)}) collective-permute-start(f32[16,4,8,256]{3,2,1,0:T(8,128)S(1)} %all-to-all-done.2.own), channel_id=1, source_target_pairs={{0,1},{1,0},{2,3},{3,2},{4,5},{5,4},{6,7},{7,6},{8,9},{9,8},{10,11... | collective-permute-start | bytes 1572872 | tf_op jit(solution)/shard_map/ppermute | solution.py:44

commit v4 on v3

--- a/solution.py
+++ b/solution.py
@@ -77,23 +77,38 @@
     return high, (v - high.astype(F32)).astype(BF16)
 
 
-def fetched_body(tab, *refs):
-    sources, out, targets, sems = refs[:3], refs[3], refs[4:7], refs[7:]
-    copies = [pltpu.make_async_copy(*c) for c in zip(sources, targets, sems)]
+def panel_body(tab, present, panel, inverse, out, fetched, live, rows, *sems):
+    copies = [
+        pltpu.make_async_copy(*c)
+        for c in zip((present, panel, inverse), (live, rows, fetched), sems)
+    ]
     for c in copies:
         c.start()
-    for c in copies:
-        c.wait()
-    panel_body(0, tab, *targets, out)
-
-
-def panel_body(which, tab, present, panel, inverse, out):
-    p = tab[which]
+    copies[1].wait()
+    copies[2].wait()
+    multiply(rows, fetched, out)
+    copies[0].wait()
+    clear(tab[0], live, out)
+
+
+def own_body(tab, present, rows, inverse, out, live, sem):
+    copy = pltpu.make_async_copy(present, live, sem)
+    copy.start()
+    multiply(rows, inverse, out)
+    copy.wait()
+    clear(tab[6], live, out)
+
+
+def multiply(rows, inverse, out):
     for s in range(4):
-        value = jnp.dot(panel[s], inverse[s], precision=HIGHEST, preferred_element_type=F32)
+        out[s] = jnp.dot(rows[s], inverse[s], precision=HIGHEST, preferred_element_type=F32)
+
+
+def clear(p, live, out):
+    for s in range(4):
         for i in range(3):
-            live = present[s, i * 16 + p].astype(F32)
-            out[s, i * 16 : i * 16 + 16] = value[i * 16 : i * 16 + 16] * live
+            at = slice(i * 16, i * 16 + 16)
+            out[s, at] = out[s, at] * live[s, i * 16 + p].astype(F32)
 
 
 def matrix_body(tab, source, out, a, *sems):
@@ -197,28 +212,36 @@
     panel = panel.reshape(4, 48, 256)
 
     arrived = to_columns(panel)
-    lhat = call(
-        fetched_body,
-        shape(4, 48, 256),
+    lhat, inverse = call(
+        panel_body,
+        [shape(4, 48, 256), shape(4, 256, 256)],
         [SMEM] + [HBM] * 3,
-        [
-            pltpu.SMEM((4, 48), jnp.int32),
-            pltpu.VMEM((4, 48, 256), F32),
-            pltpu.VMEM((4, 256, 256), F32),
-            DMA, DMA, DMA,
-        ],
+        [pltpu.SMEM((4, 48), jnp.int32), pltpu.VMEM((4, 48, 256), F32), DMA, DMA, DMA],
     )(tab, in_hbm(present), in_hbm(panel), in_hbm(diag_inv))
-    near = jnp.stack([lhat] + [shift_x(lhat, -d) for d in (1, 2, 3)])
+    near = [lhat] + [shift_x(lhat, -d) for d in (1, 2, 3)]
     matrix = call(
         matrix_body,
         shape(768, 2304, dtype=BF16),
         [SMEM, HBM],
         [pltpu.VMEM((4608, 128), F32), DMA, DMA, DMA],
     )(tab, in_hbm(ainv.reshape(4608, 128)))
-    arrived, matrix = lax.optimization_barrier((arrived, matrix))
     own = call(
-        functools.partial(panel_body, 6), shape(4, 48, 256), [SMEM, SMEM, VMEM, VMEM]
-    )(tab, present, arrived, diag_inv)
+        own_body,
+        shape(4, 48, 256),
+        [SMEM, HBM, VMEM, VMEM],
+        [pltpu.SMEM((4, 48), jnp.int32), DMA],
+    )(tab, in_hbm(present), arrived, inverse)
+    pieces = []
+    mate = swap_y(own)
+    for flip, first in enumerate((own, mate)):
+        ahead, back = [first], [first]
+        for _ in range(3):
+            ahead.append(shift_z(ahead[-1], 1))
+            back.append(shift_z(back[-1], -1))
+        last = shift_z(back[-1], -1) if flip else shift_z(ahead[-1], 1)
+        pieces += ahead + back[1:] + [last]
+
+    near = jnp.stack(near)
     far = flip_y(near)
     spread = call(
         spread_body,
@@ -226,15 +249,6 @@
         [VMEM] * 2,
         [pltpu.VMEM((384, 256), F32)],
     )(near, far)
-
-    pieces = []
-    for flip, first in enumerate((own, swap_y(own))):
-        ahead, back = [first], [first]
-        for _ in range(3):
-            ahead.append(shift_z(ahead[-1], 1))
-            back.append(shift_z(back[-1], -1))
-        last = shift_z(back[-1], -1) if flip else shift_z(ahead[-1], 1)
-        pieces += ahead + back[1:] + [last]
 
     def product(side):
         return call(
@@ -267,7 +281,6 @@
     total = lax.all_to_all(jnp.broadcast_to(total[None], (8, 4, 8, 256)), "z", 0, 0)
     total = jnp.sum(total, axis=0)
     total = lax.all_to_all(jnp.broadcast_to(total[None], (16, 4, 8, 256)), PLANE, 0, 0)
-    total, far = lax.optimization_barrier((total, far))
     shares = part + far
     diag = call(last_body, shape(4, 256, 256), [SMEM] + [VMEM] * 3)(
         tab, total, swap_core(total), dinv

time: 134 us -> 147 us (1.097)
  the two profiles are of different devices: /device:TPU:1 before, /device:TPU:2 now
where the time goes in v4:
time: 147 us; the launch traced here: 145 us
  starting transfers between devices  58.5 us (40%)
  waiting for transfers between devices  32.2 us (22%)
  blocking collectives  31.8 us (22%)
  Pallas kernels  20.2 us (14%)
    ppermute x14, starting transfers between devices, shift_z(): return lax.ppermute(v, 'z', [(p, (p + d) % 8) for p in range(8)])  27.9 us
    all_to_all x1, blocking collectives, process(): total = jnp.sum(lax.all_to_all(term, PLANE, 0, 0), axis=0)  16.8 us
    all_to_all x1, blocking collectives, process(): lax.all_to_all(jnp.broadcast_to(total[None], (8, 4, 8, 256)), 'z', 0, 0)  15 us
    ppermute x6, starting transfers between devices, shift_x(): return lax.ppermute(v, 'x', [(p, (p + d) % 4) for p in range(4)])  12.2 us
    all_to_all x1, waiting for transfers between devices, process(): lax.all_to_all(jnp.broadcast_to(total[None], (16, 4, 8, 256)), PLANE, 0, 0)  10.6 us
    ppermute x6, waiting for transfers between devices, shift_x(): return lax.ppermute(v, 'x', [(p, (p + d) % 4) for p in range(4)])  9.33 us
    pallas_call x2, Pallas kernels, product(): call(functools.partial(product_body, side), shape(8, 4, 48, 256), [SMEM]...  7.62 us
    ppermute x14, waiting for transfers between devices, shift_z(): return lax.ppermute(v, 'z', [(p, (p + d) % 8) for p in range(8)])  6.58 us
  transfers between devices with their start and end apart: 28, of which 14 were waited for; matrix products, arithmetic and copies ran while one was open for 1% of the time, Pallas kernels for 8%

profile of v4, /device:TPU:2, one launch (start us, length us, event | category | flops | bytes accessed | tf_op | source)
XLA Modules:
  0.0 145.4 jit_solution(15437963810034584133)
XLA Ops:
  0.6 3.8 %collective-permute-start = (f32[4,48,256]{2,1,0:T(8,128)}, f32[4,48,256]{2,1,0:T(8,128)S(1)}, u32[]{:S(2)}, u32[]{:S(2)}) collective-permute-start(f32[4,48,256]{2,1,0:T(8,128)} %bitcast.18), channel_id=1, source_target_pairs={{0,0},{1,64},{2,16},{3,96},{4,32},{5,112},{6,48},{7,80},{8,128},{9... | collective-permute-start | bytes 589832 | tf_op jit(solution)/shard_map/ppermute | solution.py:32
  4.5 0.1 concatenate.3.tab
  4.6 2.7 %shard_map.69 = (f32[4,48,256]{2,1,0:T(8,128)S(1)}, f32[4,256,256]{2,1,0:T(8,128)S(1)}) custom-call(s32[16]{0:T(128)S(1)} %concatenate.3.tab, s32[4,48]{1,0:T(4,128)} %present.3, f32[4,48,256]{2,1,0:T(8,128)} %bitcast.19, f32[4,256,256]{2,1,0:T(8,128)} %inverse.1), custom_call_target="tpu_custom_call" | custom-call | bytes 4194304 | tf_op jit(solution)/shard_map/pallas_call | solution.py:215
  7.2 2.9 %collective-permute-start.18 = (f32[4,48,256]{2,1,0:T(8,128)S(1)}, f32[4,48,256]{2,1,0:T(8,128)S(1)}, u32[]{:S(2)}, u32[]{:S(2)}) collective-permute-start(f32[4,48,256]{2,1,0:T(8,128)S(1)} %get-tuple-element.15), channel_id=1, source_target_pairs={{0,2},{2,4},{4,6},{6,0},{1,3},{3,5},{5,7},{7,1},{8,10},{10,12},{12... | collective-permute-start | bytes 589832 | tf_op jit(solution)/shard_map/ppermute | solution.py:52
  10.1 2.1 %collective-permute-start.17 = (f32[4,48,256]{2,1,0:T(8,128)S(1)}, f32[4,48,256]{2,1,0:T(8,128)S(1)}, u32[]{:S(2)}, u32[]{:S(2)}) collective-permute-start(f32[4,48,256]{2,1,0:T(8,128)S(1)} %get-tuple-element.15), channel_id=1, source_target_pairs={{0,4},{2,6},{4,0},{6,2},{1,5},{3,7},{5,1},{7,3},{8,12},{10,14},{12... | collective-permute-start | bytes 589832 | tf_op jit(solution)/shard_map/ppermute | solution.py:52
  12.2 2.5 %collective-permute-start.16 = (f32[4,48,256]{2,1,0:T(8,128)S(1)}, f32[4,48,256]{2,1,0:T(8,128)S(1)}, u32[]{:S(2)}, u32[]{:S(2)}) collective-permute-start(f32[4,48,256]{2,1,0:T(8,128)S(1)} %get-tuple-element.15), channel_id=1, source_target_pairs={{0,6},{2,0},{4,2},{6,4},{1,7},{3,1},{5,3},{7,5},{8,14},{10,8},{12,... | collective-permute-start | bytes 589832 | tf_op jit(solution)/shard_map/ppermute | solution.py:52
  14.7 0.0 collective-permute-done.rows
  14.7 1.3 shard_map.70.refs_0_
  16.0 2.7 %collective-permute-start.8 = (f32[4,48,256]{2,1,0:T(8,128)S(1)}, f32[4,48,256]{2,1,0:T(8,128)S(1)}, u32[]{:S(2)}, u32[]{:S(2)}) collective-permute-start(f32[4,48,256]{2,1,0:T(8,128)S(1)} %shard_map.70.refs_0_), channel_id=1, source_target_pairs={{0,128},{128,0},{1,129},{129,1},{2,130},{130,2},{3,131},{131,3},{4... | collective-permute-start | bytes 589832 | tf_op jit(solution)/shard_map/ppermute | solution.py:36
  18.7 2.6 %collective-permute-start.1 = (f32[4,48,256]{2,1,0:T(8,128)S(1)}, f32[4,48,256]{2,1,0:T(8,128)S(1)}, u32[]{:S(2)}, u32[]{:S(2)}) collective-permute-start(f32[4,48,256]{2,1,0:T(8,128)S(1)} %shard_map.70.refs_0_), channel_id=1, source_target_pairs={{0,16},{16,32},{32,48},{48,64},{64,80},{80,96},{96,112},{112,0},{1... | collective-permute-start | bytes 589832 | tf_op jit(solution)/shard_map/ppermute | solution.py:40
  21.3 0.3 collective-permute-done.18
  21.6 0.0 collective-permute-done.17
  21.6 1.9 %collective-permute-done.16 = f32[4,48,256]{2,1,0:T(8,128)S(1)} collective-permute-done((f32[4,48,256]{2,1,0:T(8,128)S(1)}, f32[4,48,256]{2,1,0:T(8,128)S(1)}, u32[]{:S(2)}, u32[]{:S(2)}) %collective-permute-start.16) | collective-permute-done | bytes 196640 | tf_op jit(solution)/shard_map/ppermute | solution.py:52
  23.5 0.1 pad_maximum_fusion.refs_0_
  23.6 3.4 %collective-permute-start.19 = (f32[4,4,48,256]{3,2,1,0:T(8,128)S(1)}, f32[4,4,48,256]{3,2,1,0:T(8,128)S(1)}, u32[]{:S(2)}, u32[]{:S(2)}) collective-permute-start(f32[4,4,48,256]{3,2,1,0:T(8,128)S(1)} %pad_maximum_fusion.refs_0_), channel_id=1, source_target_pairs={{0,8},{8,0},{1,9},{9,1},{2,10},{10,2},{3,11},{11,3},{4,12},{12,4},... | collective-permute-start | bytes 2359304 | tf_op jit(solution)/shard_map/ppermute | solution.py:48
  27.0 0.0 collective-permute-done.8.refs_8_
  27.0 4.7 %collective-permute-start.12 = (f32[4,48,256]{2,1,0:T(8,128)S(1)}, f32[4,48,256]{2,1,0:T(8,128)S(1)}, u32[]{:S(2)}, u32[]{:S(2)}) collective-permute-start(f32[4,48,256]{2,1,0:T(8,128)S(1)} %collective-permute-done.8.refs_8_), channel_id=1, source_target_pairs={{0,112},{16,0},{32,16},{48,32},{64,48},{80,64},{96,80},{112,96},{1... | collective-permute-start | bytes 589832 | tf_op jit(solution)/shard_map/ppermute | solution.py:40
  31.6 0.8 collective-permute-start.4
  32.5 1.2 collective-permute-start.2
  33.7 0.0 collective-permute-start.9
  33.7 3.2 %collective-permute-done.12.refs_12_ = f32[4,48,256]{2,1,0:T(8,128)S(1)} collective-permute-done((f32[4,48,256]{2,1,0:T(8,128)S(1)}, f32[4,48,256]{2,1,0:T(8,128)S(1)}, u32[]{:S(2)}, u32[]{:S(2)}) %collective-permute-start.12) | collective-permute-done | bytes 196640 | tf_op jit(solution)/shard_map/ppermute | solution.py:40
  36.9 3.7 %collective-permute-start.13 = (f32[4,48,256]{2,1,0:T(8,128)S(1)}, f32[4,48,256]{2,1,0:T(8,128)S(1)}, u32[]{:S(2)}, u32[]{:S(2)}) collective-permute-start(f32[4,48,256]{2,1,0:T(8,128)S(1)} %collective-permute-done.12.refs_12_), channel_id=1, source_target_pairs={{0,112},{16,0},{32,16},{48,32},{64,48},{80,64},{96,80},{112,96},{1... | collective-permute-start | bytes 589832 | tf_op jit(solution)/shard_map/ppermute | solution.py:40
  40.6 0.5 collective-permute-done.4.refs_4_
  41.2 3.7 %collective-permute-start.5 = (f32[4,48,256]{2,1,0:T(8,128)S(1)}, f32[4,48,256]{2,1,0:T(8,128)S(1)}, u32[]{:S(2)}, u32[]{:S(2)}) collective-permute-start(f32[4,48,256]{2,1,0:T(8,128)S(1)} %collective-permute-done.4.refs_4_), channel_id=1, source_target_pairs={{0,112},{16,0},{32,16},{48,32},{64,48},{80,64},{96,80},{112,96},{1... | collective-permute-start | bytes 589832 | tf_op jit(solution)/shard_map/ppermute | solution.py:40
  44.9 0.1 collective-permute-start.10
  45.0 0.7 collective-permute-done.13.refs_13_
  45.7 3.7 %collective-permute-start.14 = (f32[4,48,256]{2,1,0:T(8,128)S(1)}, f32[4,48,256]{2,1,0:T(8,128)S(1)}, u32[]{:S(2)}, u32[]{:S(2)}) collective-permute-start(f32[4,48,256]{2,1,0:T(8,128)S(1)} %collective-permute-done.13.refs_13_), channel_id=1, source_target_pairs={{0,112},{16,0},{32,16},{48,32},{64,48},{80,64},{96,80},{112,96},{1... | collective-permute-start | bytes 589832 | tf_op jit(solution)/shard_map/ppermute | solution.py:40
  49.4 0.8 collective-permute-done.5.refs_5_
  50.1 3.7 %collective-permute-start.6 = (f32[4,48,256]{2,1,0:T(8,128)S(1)}, f32[4,48,256]{2,1,0:T(8,128)S(1)}, u32[]{:S(2)}, u32[]{:S(2)}) collective-permute-start(f32[4,48,256]{2,1,0:T(8,128)S(1)} %collective-permute-done.5.refs_5_), channel_id=1, source_target_pairs={{0,112},{16,0},{32,16},{48,32},{64,48},{80,64},{96,80},{112,96},{1... | collective-permute-start | bytes 589832 | tf_op jit(solution)/shard_map/ppermute | solution.py:40
  53.8 0.8 collective-permute-done.10.refs_10_
  54.6 0.0 collective-permute-start.11
  54.6 0.0 collective-permute-done.14.refs_14_
  54.6 3.7 %collective-permute-start.15 = (f32[4,48,256]{2,1,0:T(8,128)S(1)}, f32[4,48,256]{2,1,0:T(8,128)S(1)}, u32[]{:S(2)}, u32[]{:S(2)}) collective-permute-start(f32[4,48,256]{2,1,0:T(8,128)S(1)} %collective-permute-done.14.refs_14_), channel_id=1, source_target_pairs={{0,112},{16,0},{32,16},{48,32},{64,48},{80,64},{96,80},{112,96},{1... | collective-permute-start | bytes 589832 | tf_op jit(solution)/shard_map/ppermute | solution.py:40
  58.3 3.2 %shard_map.68.matrix = bf16[768,2304]{1,0:T(8,128)(2,1)S(1)} custom-call(s32[16]{0:T(128)S(1)} %concatenate.3.tab, f32[4608,128]{1,0:T(8,128)} %bitcast.17), custom_call_target="tpu_custom_call" | custom-call | bytes 4194304 | tf_op jit(solution)/shard_map/pallas_call | solution.py:222
  61.6 0.0 collective-permute-done.19.refs_1_
  61.6 0.7 shard_map.73.spread
  62.3 0.0 collective-permute-done.7.refs_7_
  62.3 0.5 collective-permute-done.11.refs_11_
  62.8 3.8 %shard_map.72 = f32[8,4,48,256]{3,2,1,0:T(8,128)S(1)} custom-call(s32[16]{0:T(128)S(1)} %concatenate.3.tab, bf16[768,2304]{1,0:T(8,128)(2,1)S(1)} %shard_map.68.matrix, f32[4,48,256]{2,1,0:T(8,128)S(1)} %shard_map.70.refs_0_, f32[4,48,256]{2,1,0:T(8,128)S(1)} %collective-permute-done.1.refs_1_, f32[4,48,256]{2,1,0:T(8,128)S(1)} %collective-permute-done.2.refs_2_, ...), custom_call_target="tpu_custom_call" | custom-call | flops 1811939328 | bytes 4194304 | tf_op jit(solution)/shard_map/pallas_call | solution.py:254
  66.6 0.1 collective-permute-start.20
  66.7 3.8 %shard_map.71.keep = f32[8,4,48,256]{3,2,1,0:T(8,128)S(1)} custom-call(s32[16]{0:T(128)S(1)} %concatenate.3.tab, bf16[768,2304]{1,0:T(8,128)(2,1)S(1)} %shard_map.68.matrix, f32[4,48,256]{2,1,0:T(8,128)S(1)} %shard_map.70.refs_0_, f32[4,48,256]{2,1,0:T(8,128)S(1)} %collective-permute-done.1.refs_1_, f32[4,48,256]{2,1,0:T(8,128)S(1)} %collective-permute-done.2.refs_2_, ...), custom_call_target="tpu_custom_call" | custom-call | flops 1811939328 | bytes 4194304 | tf_op jit(solution)/shard_map/pallas_call | solution.py:254
  70.6 0.0 collective-permute-done.20.other
  70.6 3.0 %shard_map.74 = (f32[2,4,48,256]{3,2,1,0:T(8,128)S(1)}, f32[2,4,48,256]{3,2,1,0:T(8,128)}, f32[2,4,48,256]{3,2,1,0:T(8,128)}, f32[2,4,48,256]{3,2,1,0:T(8,128)S(...) custom-call(s32[16]{0:T(128)S(1)} %concatenate.3.tab, f32[8,4,48,256]{3,2,1,0:T(8,128)S(1)} %shard_map.71.keep, ...), custom_call_target="tpu_custom_call" | custom-call | flops 603979776 | bytes 4194304 | tf_op jit(solution)/shard_map/pallas_call | solution.py:267
  73.6 0.5 collective-permute-start.25
  74.0 1.5 %collective-permute-done.25 = f32[16,4,8,256]{3,2,1,0:T(8,128)S(1)} collective-permute-done((f32[16,4,8,256]{3,2,1,0:T(8,128)S(1)}, f32[16,4,8,256]{3,2,1,0:T(8,128)S(1)}, u32[]{:S(2)}, u32[]{:S(2)}) %collective-permute-start.25) | collective-permute-done | bytes 524320 | tf_op jit(solution)/shard_map/ppermute | solution.py:44
  75.6 0.1 add.55
  75.7 16.8 %all_to_all.15 = f32[16,4,8,256]{3,2,1,0:T(8,128)S(1)} all-to-all(f32[16,4,8,256]{3,2,1,0:T(8,128)S(1)} %add.55), channel_id=1, replica_groups=mesh['y_lo'=2,'z'=8,'y_hi'=2,'x'=4,'core'=2] {'y_lo','y_hi','x'}, dimensions={0} | all-to-all | bytes 1048576 | tf_op jit(solution)/shard_map/all_to_all | solution.py:280
  92.5 0.0 copy-start
  92.5 15.0 %all_to_all.16 = f32[8,4,8,256]{3,2,1,0:T(8,128)S(1)} all-to-all(f32[8,4,8,256]{3,2,1,0:T(8,128)S(1)} %broadcast_in_dim.39), channel_id=1, replica_groups=mesh['y_lo'=2,'z'=8,'y_hi'=2,'x'=4,'core'=2] {'z'}, dimensions={0} | all-to-all | bytes 524288 | tf_op jit(solution)/shard_map/all_to_all | solution.py:281
  107.6 0.8 broadcast_in_dim.40
  108.4 4.9 %all-to-all-start.2 = ((f32[16,4,8,256]{3,2,1,0:T(8,128)}), f32[16,4,8,256]{3,2,1,0:T(8,128)S(1)}, u32[]{:S(2)}, u32[]{:S(2)}) async-start(f32[16,4,8,256]{3,2,1,0:T(8,128)} %broadcast_in_dim.40), calls=%async_computation.2 | async-start | bytes 1048576 | tf_op jit(solution)/shard_map/all_to_all | solution.py:283
  113.3 1.5 %collective-permute-start.21 = (f32[2,4,48,256]{3,2,1,0:T(8,128)}, f32[2,4,48,256]{3,2,1,0:T(8,128)S(1)}, u32[]{:S(2)}, u32[]{:S(2)}) collective-permute-start(f32[2,4,48,256]{3,2,1,0:T(8,128)} %get-tuple-element.19), channel_id=1, source_target_pairs={{0,2},{2,4},{4,6},{6,0},{1,3},{3,5},{5,7},{7,1},{8,10},{10,12},{12... | collective-permute-start | bytes 1179656 | tf_op jit(solution)/shard_map/ppermute | solution.py:52
  114.8 0.9 collective-permute-start.22
  115.7 2.3 %collective-permute-start.23 = (f32[2,4,48,256]{3,2,1,0:T(8,128)S(1)}, f32[2,4,48,256]{3,2,1,0:T(8,128)S(1)}, u32[]{:S(2)}, u32[]{:S(2)}) collective-permute-start(f32[2,4,48,256]{3,2,1,0:T(8,128)S(1)} %get-tuple-element.21), channel_id=1, source_target_pairs={{0,6},{2,0},{4,2},{6,4},{1,7},{3,1},{5,3},{7,5},{8,14},{10,8},{12,... | collective-permute-start | bytes 1179656 | tf_op jit(solution)/shard_map/ppermute | solution.py:52
  118.0 10.6 %all-to-all-done.2.own = f32[16,4,8,256]{3,2,1,0:T(8,128)S(1)} async-done(((f32[16,4,8,256]{3,2,1,0:T(8,128)}), f32[16,4,8,256]{3,2,1,0:T(8,128)S(1)}, u32[]{:S(2)}, u32[]{:S(2)}) %all-to-all-start.2) | async-done | bytes 524320 | tf_op jit(solution)/shard_map/all_to_all | solution.py:283
  128.6 0.6 collective-permute-done.21.b
  129.2 2.0 %collective-permute-done.22.c = f32[2,4,48,256]{3,2,1,0:T(8,128)S(1)} collective-permute-done((f32[2,4,48,256]{3,2,1,0:T(8,128)}, f32[2,4,48,256]{3,2,1,0:T(8,128)S(1)}, u32[]{:S(2)}, u32[]{:S(2)}) %collective-permute-start.22) | collective-permute-done | bytes 393248 | tf_op jit(solution)/shard_map/ppermute | solution.py:52
  131.2 4.5 %collective-permute-done.23.d = f32[2,4,48,256]{3,2,1,0:T(8,128)S(1)} collective-permute-done((f32[2,4,48,256]{3,2,1,0:T(8,128)S(1)}, f32[2,4,48,256]{3,2,1,0:T(8,128)S(1)}, u32[]{:S(2)}, u32[]{:S(2)}) %collective-permute-start.23) | collective-permute-done | bytes 393248 | tf_op jit(solution)/shard_map/ppermute | solution.py:52
  135.7 0.1 shard_map.75
  135.8 3.1 %collective-permute-start.24 = (f32[4,48,256]{2,1,0:T(8,128)S(1)}, f32[4,48,256]{2,1,0:T(8,128)S(1)}, u32[]{:S(2)}, u32[]{:S(2)}) collective-permute-start(f32[4,48,256]{2,1,0:T(8,128)S(1)} %get-tuple-element.23), channel_id=1, source_target_pairs={{0,8},{8,0},{1,9},{9,1},{2,10},{10,2},{3,11},{11,3},{4,12},{12,4},... | collective-permute-start | bytes 589832 | tf_op jit(solution)/shard_map/ppermute | solution.py:48
  138.9 4.2 %collective-permute-done.24 = f32[4,48,256]{2,1,0:T(8,128)S(1)} collective-permute-done((f32[4,48,256]{2,1,0:T(8,128)S(1)}, f32[4,48,256]{2,1,0:T(8,128)S(1)}, u32[]{:S(2)}, u32[]{:S(2)}) %collective-permute-start.24) | collective-permute-done | bytes 196640 | tf_op jit(solution)/shard_map/ppermute | solution.py:48
  143.0 0.7 add.54
  143.7 0.0 collective-permute-done.26.other
  143.8 1.7 %shard_map.76 = f32[4,256,256]{2,1,0:T(8,128)} custom-call(s32[16]{0:T(128)S(1)} %concatenate.3.tab, f32[16,4,8,256]{3,2,1,0:T(8,128)S(1)} %all-to-all-done.2.own, f32[16,4,8,256]{3,2,1,0:T(8,128)S(1)} %collective-permute-done.26.other, f32[4,256,256]{2,1,0:T(8,128)S(1)} %copy-done), custom_call_target="tpu_custom_call" | custom-call | bytes 4194304 | tf_op jit(solution)/shard_map/pallas_call | solution.py:285
  (14 shorter events, 0.1 us)
Async XLA Ops:
  0.6 14.1 %collective-permute-start = (f32[4,48,256]{2,1,0:T(8,128)}, f32[4,48,256]{2,1,0:T(8,128)S(1)}, u32[]{:S(2)}, u32[]{:S(2)}) collective-permute-start(f32[4,48,256]{2,1,0:T(8,128)} %bitcast.18), channel_id=1, source_target_pairs={{0,0},{1,64},{2,16},{3,96},{4,32},{5,112},{6,48},{7,80},{8,128},{9... | collective-permute-start | bytes 589832 | tf_op jit(solution)/shard_map/ppermute | solution.py:32
  7.2 14.4 %collective-permute-start.18 = (f32[4,48,256]{2,1,0:T(8,128)S(1)}, f32[4,48,256]{2,1,0:T(8,128)S(1)}, u32[]{:S(2)}, u32[]{:S(2)}) collective-permute-start(f32[4,48,256]{2,1,0:T(8,128)S(1)} %get-tuple-element.15), channel_id=1, source_target_pairs={{0,2},{2,4},{4,6},{6,0},{1,3},{3,5},{5,7},{7,1},{8,10},{10,12},{12... | collective-permute-start | bytes 589832 | tf_op jit(solution)/shard_map/ppermute | solution.py:52
  10.1 11.5 %collective-permute-start.17 = (f32[4,48,256]{2,1,0:T(8,128)S(1)}, f32[4,48,256]{2,1,0:T(8,128)S(1)}, u32[]{:S(2)}, u32[]{:S(2)}) collective-permute-start(f32[4,48,256]{2,1,0:T(8,128)S(1)} %get-tuple-element.15), channel_id=1, source_target_pairs={{0,4},{2,6},{4,0},{6,2},{1,5},{3,7},{5,1},{7,3},{8,12},{10,14},{12... | collective-permute-start | bytes 589832 | tf_op jit(solution)/shard_map/ppermute | solution.py:52
  12.2 11.3 %collective-permute-start.16 = (f32[4,48,256]{2,1,0:T(8,128)S(1)}, f32[4,48,256]{2,1,0:T(8,128)S(1)}, u32[]{:S(2)}, u32[]{:S(2)}) collective-permute-start(f32[4,48,256]{2,1,0:T(8,128)S(1)} %get-tuple-element.15), channel_id=1, source_target_pairs={{0,6},{2,0},{4,2},{6,4},{1,7},{3,1},{5,3},{7,5},{8,14},{10,8},{12,... | collective-permute-start | bytes 589832 | tf_op jit(solution)/shard_map/ppermute | solution.py:52
  16.0 11.0 %collective-permute-start.8 = (f32[4,48,256]{2,1,0:T(8,128)S(1)}, f32[4,48,256]{2,1,0:T(8,128)S(1)}, u32[]{:S(2)}, u32[]{:S(2)}) collective-permute-start(f32[4,48,256]{2,1,0:T(8,128)S(1)} %shard_map.70.refs_0_), channel_id=1, source_target_pairs={{0,128},{128,0},{1,129},{129,1},{2,130},{130,2},{3,131},{131,3},{4... | collective-permute-start | bytes 589832 | tf_op jit(solution)/shard_map/ppermute | solution.py:36
  18.7 13.8 %collective-permute-start.1 = (f32[4,48,256]{2,1,0:T(8,128)S(1)}, f32[4,48,256]{2,1,0:T(8,128)S(1)}, u32[]{:S(2)}, u32[]{:S(2)}) collective-permute-start(f32[4,48,256]{2,1,0:T(8,128)S(1)} %shard_map.70.refs_0_), channel_id=1, source_target_pairs={{0,16},{16,32},{32,48},{48,64},{64,80},{80,96},{96,112},{112,0},{1... | collective-permute-start | bytes 589832 | tf_op jit(solution)/shard_map/ppermute | solution.py:40
  23.6 38.0 %collective-permute-start.19 = (f32[4,4,48,256]{3,2,1,0:T(8,128)S(1)}, f32[4,4,48,256]{3,2,1,0:T(8,128)S(1)}, u32[]{:S(2)}, u32[]{:S(2)}) collective-permute-start(f32[4,4,48,256]{3,2,1,0:T(8,128)S(1)} %pad_maximum_fusion.refs_0_), channel_id=1, source_target_pairs={{0,8},{8,0},{1,9},{9,1},{2,10},{10,2},{3,11},{11,3},{4,12},{12,4},... | collective-permute-start | bytes 2359304 | tf_op jit(solution)/shard_map/ppermute | solution.py:48
  27.0 10.0 %collective-permute-start.12 = (f32[4,48,256]{2,1,0:T(8,128)S(1)}, f32[4,48,256]{2,1,0:T(8,128)S(1)}, u32[]{:S(2)}, u32[]{:S(2)}) collective-permute-start(f32[4,48,256]{2,1,0:T(8,128)S(1)} %collective-permute-done.8.refs_8_), channel_id=1, source_target_pairs={{0,112},{16,0},{32,16},{48,32},{64,48},{80,64},{96,80},{112,96},{1... | collective-permute-start | bytes 589832 | tf_op jit(solution)/shard_map/ppermute | solution.py:40
  31.6 9.5 %collective-permute-start.4 = (f32[4,48,256]{2,1,0:T(8,128)S(1)}, f32[4,48,256]{2,1,0:T(8,128)S(1)}, u32[]{:S(2)}, u32[]{:S(2)}) collective-permute-start(f32[4,48,256]{2,1,0:T(8,128)S(1)} %shard_map.70.refs_0_), channel_id=1, source_target_pairs={{0,112},{16,0},{32,16},{48,32},{64,48},{80,64},{96,80},{112,96},{1... | collective-permute-start | bytes 589832 | tf_op jit(solution)/shard_map/ppermute | solution.py:40
  32.5 12.4 %collective-permute-start.2 = (f32[4,48,256]{2,1,0:T(8,128)S(1)}, f32[4,48,256]{2,1,0:T(8,128)S(1)}, u32[]{:S(2)}, u32[]{:S(2)}) collective-permute-start(f32[4,48,256]{2,1,0:T(8,128)S(1)} %collective-permute-done.1.refs_1_), channel_id=1, source_target_pairs={{0,16},{16,32},{32,48},{48,64},{64,80},{80,96},{96,112},{112,0},{1... | collective-permute-start | bytes 589832 | tf_op jit(solution)/shard_map/ppermute | solution.py:40
  33.7 11.2 %collective-permute-start.9 = (f32[4,48,256]{2,1,0:T(8,128)S(1)}, f32[4,48,256]{2,1,0:T(8,128)S(1)}, u32[]{:S(2)}, u32[]{:S(2)}) collective-permute-start(f32[4,48,256]{2,1,0:T(8,128)S(1)} %collective-permute-done.8.refs_8_), channel_id=1, source_target_pairs={{0,16},{16,32},{32,48},{48,64},{64,80},{80,96},{96,112},{112,0},{1... | collective-permute-start | bytes 589832 | tf_op jit(solution)/shard_map/ppermute | solution.py:40
  36.9 8.7 %collective-permute-start.13 = (f32[4,48,256]{2,1,0:T(8,128)S(1)}, f32[4,48,256]{2,1,0:T(8,128)S(1)}, u32[]{:S(2)}, u32[]{:S(2)}) collective-permute-start(f32[4,48,256]{2,1,0:T(8,128)S(1)} %collective-permute-done.12.refs_12_), channel_id=1, source_target_pairs={{0,112},{16,0},{32,16},{48,32},{64,48},{80,64},{96,80},{112,96},{1... | collective-permute-start | bytes 589832 | tf_op jit(solution)/shard_map/ppermute | solution.py:40
  41.2 9.0 %collective-permute-start.5 = (f32[4,48,256]{2,1,0:T(8,128)S(1)}, f32[4,48,256]{2,1,0:T(8,128)S(1)}, u32[]{:S(2)}, u32[]{:S(2)}) collective-permute-start(f32[4,48,256]{2,1,0:T(8,128)S(1)} %collective-permute-done.4.refs_4_), channel_id=1, source_target_pairs={{0,112},{16,0},{32,16},{48,32},{64,48},{80,64},{96,80},{112,96},{1... | collective-permute-start | bytes 589832 | tf_op jit(solution)/shard_map/ppermute | solution.py:40
  44.8 9.0 %collective-permute-start.3 = (f32[4,48,256]{2,1,0:T(8,128)S(1)}, f32[4,48,256]{2,1,0:T(8,128)S(1)}, u32[]{:S(2)}, u32[]{:S(2)}) collective-permute-start(f32[4,48,256]{2,1,0:T(8,128)S(1)} %collective-permute-done.2.refs_2_), channel_id=1, source_target_pairs={{0,16},{16,32},{32,48},{48,64},{64,80},{80,96},{96,112},{112,0},{1... | collective-permute-start | bytes 589832 | tf_op jit(solution)/shard_map/ppermute | solution.py:40
  44.9 9.8 %collective-permute-start.10 = (f32[4,48,256]{2,1,0:T(8,128)S(1)}, f32[4,48,256]{2,1,0:T(8,128)S(1)}, u32[]{:S(2)}, u32[]{:S(2)}) collective-permute-start(f32[4,48,256]{2,1,0:T(8,128)S(1)} %collective-permute-done.9.refs_9_), channel_id=1, source_target_pairs={{0,16},{16,32},{32,48},{48,64},{64,80},{80,96},{96,112},{112,0},{1... | collective-permute-start | bytes 589832 | tf_op jit(solution)/shard_map/ppermute | solution.py:40
  45.7 9.0 %collective-permute-start.14 = (f32[4,48,256]{2,1,0:T(8,128)S(1)}, f32[4,48,256]{2,1,0:T(8,128)S(1)}, u32[]{:S(2)}, u32[]{:S(2)}) collective-permute-start(f32[4,48,256]{2,1,0:T(8,128)S(1)} %collective-permute-done.13.refs_13_), channel_id=1, source_target_pairs={{0,112},{16,0},{32,16},{48,32},{64,48},{80,64},{96,80},{112,96},{1... | collective-permute-start | bytes 589832 | tf_op jit(solution)/shard_map/ppermute | solution.py:40
  50.1 12.2 %collective-permute-start.6 = (f32[4,48,256]{2,1,0:T(8,128)S(1)}, f32[4,48,256]{2,1,0:T(8,128)S(1)}, u32[]{:S(2)}, u32[]{:S(2)}) collective-permute-start(f32[4,48,256]{2,1,0:T(8,128)S(1)} %collective-permute-done.5.refs_5_), channel_id=1, source_target_pairs={{0,112},{16,0},{32,16},{48,32},{64,48},{80,64},{96,80},{112,96},{1... | collective-permute-start | bytes 589832 | tf_op jit(solution)/shard_map/ppermute | solution.py:40
  53.8 8.5 %collective-permute-start.7 = (f32[4,48,256]{2,1,0:T(8,128)S(1)}, f32[4,48,256]{2,1,0:T(8,128)S(1)}, u32[]{:S(2)}, u32[]{:S(2)}) collective-permute-start(f32[4,48,256]{2,1,0:T(8,128)S(1)} %collective-permute-done.3.refs_3_), channel_id=1, source_target_pairs={{0,16},{16,32},{32,48},{48,64},{64,80},{80,96},{96,112},{112,0},{1... | collective-permute-start | bytes 589832 | tf_op jit(solution)/shard_map/ppermute | solution.py:40
  54.6 8.2 %collective-permute-start.11 = (f32[4,48,256]{2,1,0:T(8,128)S(1)}, f32[4,48,256]{2,1,0:T(8,128)S(1)}, u32[]{:S(2)}, u32[]{:S(2)}) collective-permute-start(f32[4,48,256]{2,1,0:T(8,128)S(1)} %collective-permute-done.10.refs_10_), channel_id=1, source_target_pairs={{0,16},{16,32},{32,48},{48,64},{64,80},{80,96},{96,112},{112,0},{1... | collective-permute-start | bytes 589832 | tf_op jit(solution)/shard_map/ppermute | solution.py:40
  54.6 8.2 %collective-permute-start.15 = (f32[4,48,256]{2,1,0:T(8,128)S(1)}, f32[4,48,256]{2,1,0:T(8,128)S(1)}, u32[]{:S(2)}, u32[]{:S(2)}) collective-permute-start(f32[4,48,256]{2,1,0:T(8,128)S(1)} %collective-permute-done.14.refs_14_), channel_id=1, source_target_pairs={{0,112},{16,0},{32,16},{48,32},{64,48},{80,64},{96,80},{112,96},{1... | collective-permute-start | bytes 589832 | tf_op jit(solution)/shard_map/ppermute | solution.py:40
  66.6 3.9 %collective-permute-start.20 = (f32[8,4,48,256]{3,2,1,0:T(8,128)S(1)}, f32[8,4,48,256]{3,2,1,0:T(8,128)S(1)}, u32[]{:S(2)}, u32[]{:S(2)}) collective-permute-start(f32[8,4,48,256]{3,2,1,0:T(8,128)S(1)} %shard_map.72), channel_id=1, source_target_pairs={{0,1},{1,0},{2,3},{3,2},{4,5},{5,4},{6,7},{7,6},{8,9},{9,8},{10,11... | collective-permute-start | bytes 4718600 | tf_op jit(solution)/shard_map/ppermute | solution.py:44
  73.6 2.0 %collective-permute-start.25 = (f32[16,4,8,256]{3,2,1,0:T(8,128)S(1)}, f32[16,4,8,256]{3,2,1,0:T(8,128)S(1)}, u32[]{:S(2)}, u32[]{:S(2)}) collective-permute-start(f32[16,4,8,256]{3,2,1,0:T(8,128)S(1)} %get-tuple-element.25), channel_id=1, source_target_pairs={{0,1},{1,0},{2,3},{3,2},{4,5},{5,4},{6,7},{7,6},{8,9},{9,8},{10,11... | collective-permute-start | bytes 1572872 | tf_op jit(solution)/shard_map/ppermute | solution.py:44
  92.5 51.2 %copy-start = (f32[4,256,256]{2,1,0:T(8,128)S(1)}, f32[4,256,256]{2,1,0:T(8,128)}, u32[]{:S(2)}) copy-start(f32[4,256,256]{2,1,0:T(8,128)} %dinv.1) | copy-start | bytes 3145732
  108.4 20.2 %all-to-all-start.2 = ((f32[16,4,8,256]{3,2,1,0:T(8,128)}), f32[16,4,8,256]{3,2,1,0:T(8,128)S(1)}, u32[]{:S(2)}, u32[]{:S(2)}) async-start(f32[16,4,8,256]{3,2,1,0:T(8,128)} %broadcast_in_dim.40), calls=%async_computation.2 | async-start | bytes 1048576 | tf_op jit(solution)/shard_map/all_to_all | solution.py:283
  113.3 15.9 %collective-permute-start.21 = (f32[2,4,48,256]{3,2,1,0:T(8,128)}, f32[2,4,48,256]{3,2,1,0:T(8,128)S(1)}, u32[]{:S(2)}, u32[]{:S(2)}) collective-permute-start(f32[2,4,48,256]{3,2,1,0:T(8,128)} %get-tuple-element.19), channel_id=1, source_target_pairs={{0,2},{2,4},{4,6},{6,0},{1,3},{3,5},{5,7},{7,1},{8,10},{10,12},{12... | collective-permute-start | bytes 1179656 | tf_op jit(solution)/shard_map/ppermute | solution.py:52
  114.8 16.4 %collective-permute-start.22 = (f32[2,4,48,256]{3,2,1,0:T(8,128)}, f32[2,4,48,256]{3,2,1,0:T(8,128)S(1)}, u32[]{:S(2)}, u32[]{:S(2)}) collective-permute-start(f32[2,4,48,256]{3,2,1,0:T(8,128)} %get-tuple-element.20), channel_id=1, source_target_pairs={{0,4},{2,6},{4,0},{6,2},{1,5},{3,7},{5,1},{7,3},{8,12},{10,14},{12... | collective-permute-start | bytes 1179656 | tf_op jit(solution)/shard_map/ppermute | solution.py:52
  115.7 20.0 %collective-permute-start.23 = (f32[2,4,48,256]{3,2,1,0:T(8,128)S(1)}, f32[2,4,48,256]{3,2,1,0:T(8,128)S(1)}, u32[]{:S(2)}, u32[]{:S(2)}) collective-permute-start(f32[2,4,48,256]{3,2,1,0:T(8,128)S(1)} %get-tuple-element.21), channel_id=1, source_target_pairs={{0,6},{2,0},{4,2},{6,4},{1,7},{3,1},{5,3},{7,5},{8,14},{10,8},{12,... | collective-permute-start | bytes 1179656 | tf_op jit(solution)/shard_map/ppermute | solution.py:52
  128.6 15.1 %collective-permute-start.26 = (f32[16,4,8,256]{3,2,1,0:T(8,128)S(1)}, f32[16,4,8,256]{3,2,1,0:T(8,128)S(1)}, u32[]{:S(2)}, u32[]{:S(2)}) collective-permute-start(f32[16,4,8,256]{3,2,1,0:T(8,128)S(1)} %all-to-all-done.2.own), channel_id=1, source_target_pairs={{0,1},{1,0},{2,3},{3,2},{4,5},{5,4},{6,7},{7,6},{8,9},{9,8},{10,11... | collective-permute-start | bytes 1572872 | tf_op jit(solution)/shard_map/ppermute | solution.py:44
  135.8 7.3 %collective-permute-start.24 = (f32[4,48,256]{2,1,0:T(8,128)S(1)}, f32[4,48,256]{2,1,0:T(8,128)S(1)}, u32[]{:S(2)}, u32[]{:S(2)}) collective-permute-start(f32[4,48,256]{2,1,0:T(8,128)S(1)} %get-tuple-element.23), channel_id=1, source_target_pairs={{0,8},{8,0},{1,9},{9,1},{2,10},{10,2},{3,11},{11,3},{4,12},{12,4},... | collective-permute-start | bytes 589832 | tf_op jit(solution)/shard_map/ppermute | solution.py:48

commit v5 on v4

--- a/solution.py
+++ b/solution.py
@@ -16,7 +16,7 @@
 PLANE = ("y_lo", "y_hi", "x")
 LANDING = (0, 4, 1, 6, 2, 7, 3, 5)
 SOURCE = tuple(LANDING.index(d) for d in range(8))
-STEPS = (0, 1, 2, 3, -1, -2, -3, 4)
+STEPS = (0, 1, 2, 3, -1, -2, -3)
 SMEM = pl.BlockSpec(memory_space=pltpu.SMEM)
 VMEM = pl.BlockSpec(memory_space=pltpu.VMEM)
 HBM = pl.BlockSpec(memory_space=pltpu.MemorySpace.HBM)
@@ -136,18 +136,28 @@
 
 
 def product_body(side, tab, matrix, *refs):
-    pieces, out, held = refs[:16], refs[16], refs[17]
+    pieces, out, held = refs[:18], refs[18], refs[19]
+
+    def put(block, n, d):
+        half = (tab[1] + n // 9) % 2
+        start = pl.multiple_of(half * 384 + tab[8 + d % 8], 16)
+        h, l = split_two(block)
+        for i in range(3):
+            for term, part in enumerate((l, h, h)):
+                at = pl.ds(term * 768 + i * 128 + start, 16)
+                held[at, :] = part[i * 16 : i * 16 + 16]
 
     @pl.loop(0, 4)
     def _(s):
-        for n, ref in enumerate(pieces):
-            half = (tab[1] + n // 8) % 2
-            start = pl.multiple_of(half * 384 + tab[8 + STEPS[n % 8] % 8], 16)
-            h, l = split_two(ref[s])
-            for i in range(3):
-                for term, part in enumerate((l, h, h)):
-                    at = pl.ds(term * 768 + i * 128 + start, 16)
-                    held[at, :] = part[i * 16 : i * 16 + 16]
+        for n in range(18):
+            if n % 9 < 7:
+                put(pieces[n][s], n, STEPS[n % 9])
+            else:
+
+                @pl.when(s // 2 == n % 9 - 7)
+                def _(n=n):
+                    put(pieces[n][s % 2], n, 4)
+
         value = jnp.dot(
             matrix[side * 384 : side * 384 + 384, :], held[...], preferred_element_type=F32
         )
@@ -168,14 +178,22 @@
 
 
 def pair_body(tab, keep, other, spread, *refs):
-    parts, (mine, yours, held, value) = refs[:4], refs[4:]
+    by_x, by_y, (mine, yours, held, value) = refs[:4], refs[4:6], refs[6:]
     core = tab[2]
 
     @pl.loop(0, 4)
     def _(s):
         for k in range(8):
             part = keep[k, s] + other[k, s]
-            parts[k // 2][k % 2, s] = part
+
+            @pl.when(s < 2)
+            def _(k=k, part=part):
+                by_x[k // 2][k % 2, s % 2] = part
+
+            @pl.when(s >= 2)
+            def _(k=k, part=part):
+                by_y[k % 2][k // 2, s % 2] = part
+
             h, l = split_two(part)
             for term, piece in enumerate((l, h, h)):
                 at = term * 384 + k * 48
@@ -186,9 +204,16 @@
                 out[e, s] = value[pl.ds(pl.multiple_of(base + e * 8, 8), 8), :]
 
 
-def sum_body(a, b, c, d, mine, yours):
-    for k, out in enumerate((mine, yours)):
-        out[...] = (a[k] + b[k]) + (c[k] + d[k])
+def first_body(a, b, c, d, e, f, *outs):
+    for k in range(2):
+        outs[k][...] = (a[k] + b[k]) + (c[k] + d[k])
+    for k in range(4):
+        outs[2 + k][...] = e[k] + f[k]
+
+
+def second_body(a, b, c, d, e, f, out):
+    out[0:2] = a[...] + b[...]
+    out[2:4] = (c[...] + d[...]) + (e[...] + f[...])
 
 
 def last_body(tab, own, other, dinv, out):
@@ -233,13 +258,13 @@
     )(tab, in_hbm(present), arrived, inverse)
     pieces = []
     mate = swap_y(own)
-    for flip, first in enumerate((own, mate)):
+    for first in (own, mate):
         ahead, back = [first], [first]
         for _ in range(3):
             ahead.append(shift_z(ahead[-1], 1))
             back.append(shift_z(back[-1], -1))
-        last = shift_z(back[-1], -1) if flip else shift_z(ahead[-1], 1)
-        pieces += ahead + back[1:] + [last]
+        last = [shift_z(ahead[-1][:2], 1), shift_z(back[-1][2:], -1)]
+        pieces += ahead + back[1:] + last
 
     near = jnp.stack(near)
     far = flip_y(near)
@@ -254,34 +279,37 @@
         return call(
             functools.partial(product_body, side),
             shape(8, 4, 48, 256),
-            [SMEM] + [VMEM] * 17,
+            [SMEM] + [VMEM] * 19,
             [pltpu.VMEM((2304, 256), BF16)],
             flops=6 * 384 * 768 * 1024,
             limit=12,
         )(tab, matrix, *pieces)
 
     send = product(1)
-    send, spread = lax.optimization_barrier((send, spread))
     other = swap_core(send)
     keep = product(0)
     *parts, mine, yours = call(
         pair_body,
-        [shape(2, 4, 48, 256)] * 4 + [shape(16, 4, 8, 256)] * 2,
+        [shape(2, 2, 48, 256)] * 4 + [shape(4, 2, 48, 256)] * 2 + [shape(16, 4, 8, 256)] * 2,
         [SMEM] + [VMEM] * 3,
         [pltpu.VMEM((1152, 256), BF16), pltpu.VMEM((256, 256), F32)],
         flops=6 * 256 * 384 * 1024,
         limit=12,
     )(tab, keep, other, spread)
-    parts = [parts[0]] + [shift_x(parts[k], k) for k in (1, 2, 3)]
-    part, far = call(sum_body, [shape(4, 48, 256)] * 2, [VMEM] * 4)(*parts)
-    far = flip_y(far)
+    for k in (1, 2, 3):
+        parts[k] = shift_x(parts[k], k)
+    parts[5] = flip_y(parts[5])
+    parts = list(call(first_body, [shape(2, 48, 256)] * 6, [VMEM] * 6)(*parts))
+    parts[1] = flip_y(parts[1])
+    for k in (1, 2, 3):
+        parts[2 + k] = shift_x(parts[2 + k], k)
+    shares = call(second_body, shape(4, 48, 256), [VMEM] * 6)(*parts)
 
     term = mine + swap_core(yours)
     total = jnp.sum(lax.all_to_all(term, PLANE, 0, 0), axis=0)
     total = lax.all_to_all(jnp.broadcast_to(total[None], (8, 4, 8, 256)), "z", 0, 0)
     total = jnp.sum(total, axis=0)
     total = lax.all_to_all(jnp.broadcast_to(total[None], (16, 4, 8, 256)), PLANE, 0, 0)
-    shares = part + far
     diag = call(last_body, shape(4, 256, 256), [SMEM] + [VMEM] * 3)(
         tab, total, swap_core(total), dinv
     )

time: 147 us -> 182 us (1.24)
  blocking collectives: 31.8 us -> 47.1 us
  waiting for transfers between devices: 32.2 us -> 45.4 us
  starting transfers between devices: 58.5 us -> 65.3 us
    ppermute x2 -> x3, waiting for transfers between devices: 4.18 us -> 17.7 us  [flip_y(): return lax.ppermute(v, 'y_hi', [(0, 1), (1, 0)])]
    all_to_all x0 -> x1, blocking collectives: none -> 12.8 us  [process(): lax.all_to_all(jnp.broadcast_to(total[None], (16, 4, 8, 256)), PLANE, 0, 0)]
    ppermute x6 -> x9, waiting for transfers between devices: 9.33 us -> 20 us  [shift_x(): return lax.ppermute(v, 'x', [(p, (p + d) % 4) for p in range(4)])]
    all_to_all x1 -> x0, waiting for transfers between devices: 10.6 us -> none  [process(): lax.all_to_all(jnp.broadcast_to(total[None], (16, 4, 8, 256)), PLANE, 0, 0)]
    ppermute x14 -> x16, starting transfers between devices: 27.9 us -> 37.4 us  [shift_z(): return lax.ppermute(v, 'z', [(p, (p + d) % 8) for p in range(8)])]
    all_to_all x1 -> x0, starting transfers between devices: 4.93 us -> none  [process(): lax.all_to_all(jnp.broadcast_to(total[None], (16, 4, 8, 256)), PLANE, 0, 0)]
    ppermute x14 -> x16, waiting for transfers between devices: 6.58 us -> 2.06 us  [shift_z(): return lax.ppermute(v, 'z', [(p, (p + d) % 8) for p in range(8)])]
    ppermute x1, waiting for transfers between devices: 0.01 us -> 3.73 us  [to_columns(): return lax.ppermute(v, AXES, pairs)]
  transfers between devices with their start and end apart: 28 -> 33, of which waited for: 14 -> 15; matrix products, arithmetic and copies ran while one was open for 1% -> 0% of each run, Pallas kernels for 8% -> 6%
where the time goes in v5:
time: 182 us; the launch traced here: 180 us
  starting transfers between devices  65.3 us (36%)
  blocking collectives  47.1 us (26%)
  waiting for transfers between devices  45.4 us (25%)
  Pallas kernels  20.9 us (11%)
    ppermute x16, starting transfers between devices, shift_z(): return lax.ppermute(v, 'z', [(p, (p + d) % 8) for p in range(8)])  37.4 us
    ppermute x9, waiting for transfers between devices, shift_x(): return lax.ppermute(v, 'x', [(p, (p + d) % 4) for p in range(4)])  20 us
    ppermute x3, waiting for transfers between devices, flip_y(): return lax.ppermute(v, 'y_hi', [(0, 1), (1, 0)])  17.7 us
    all_to_all x1, blocking collectives, process(): lax.all_to_all(jnp.broadcast_to(total[None], (8, 4, 8, 256)), 'z', 0, 0)  17.5 us
    all_to_all x1, blocking collectives, process(): total = jnp.sum(lax.all_to_all(term, PLANE, 0, 0), axis=0)  16.9 us
    ppermute x9, starting transfers between devices, shift_x(): return lax.ppermute(v, 'x', [(p, (p + d) % 4) for p in range(4)])  14.3 us
    all_to_all x1, blocking collectives, process(): lax.all_to_all(jnp.broadcast_to(total[None], (16, 4, 8, 256)), PLANE, 0, 0)  12.8 us
    pallas_call x2, Pallas kernels, product(): call(functools.partial(product_body, side), shape(8, 4, 48, 256), [SMEM]...  8.01 us
  transfers between devices with their start and end apart: 33, of which 15 were waited for; matrix products, arithmetic and copies ran while one was open for 0% of the time, Pallas kernels for 6%

profile of v5, /device:TPU:2, one launch (start us, length us, event | category | flops | bytes accessed | tf_op | source)
XLA Modules:
  0.0 180.1 jit_solution(15616386271238711122)
XLA Ops:
  0.6 3.8 %collective-permute-start = (f32[4,48,256]{2,1,0:T(8,128)}, f32[4,48,256]{2,1,0:T(8,128)S(1)}, u32[]{:S(2)}, u32[]{:S(2)}) collective-permute-start(f32[4,48,256]{2,1,0:T(8,128)} %bitcast.18), channel_id=1, source_target_pairs={{0,0},{1,64},{2,16},{3,96},{4,32},{5,112},{6,48},{7,80},{8,128},{9... | collective-permute-start | bytes 589832 | tf_op jit(solution)/shard_map/ppermute | solution.py:32
  4.5 0.1 concatenate.3.tab
  4.6 2.7 %shard_map.69 = (f32[4,48,256]{2,1,0:T(8,128)S(1)}, f32[4,256,256]{2,1,0:T(8,128)S(1)}) custom-call(s32[16]{0:T(128)S(1)} %concatenate.3.tab, s32[4,48]{1,0:T(4,128)} %present.3, f32[4,48,256]{2,1,0:T(8,128)} %bitcast.19, f32[4,256,256]{2,1,0:T(8,128)} %inverse.1), custom_call_target="tpu_custom_call" | custom-call | bytes 4194304 | tf_op jit(solution)/shard_map/pallas_call | solution.py:240
  7.2 3.7 %collective-permute-done.rows = f32[4,48,256]{2,1,0:T(8,128)S(1)} collective-permute-done((f32[4,48,256]{2,1,0:T(8,128)}, f32[4,48,256]{2,1,0:T(8,128)S(1)}, u32[]{:S(2)}, u32[]{:S(2)}) %collective-permute-start) | collective-permute-done | bytes 196640 | tf_op jit(solution)/shard_map/ppermute | solution.py:32
  11.0 1.3 shard_map.70.refs_0_
  12.3 2.7 %collective-permute-start.9 = (f32[4,48,256]{2,1,0:T(8,128)S(1)}, f32[4,48,256]{2,1,0:T(8,128)S(1)}, u32[]{:S(2)}, u32[]{:S(2)}) collective-permute-start(f32[4,48,256]{2,1,0:T(8,128)S(1)} %shard_map.70.refs_0_), channel_id=1, source_target_pairs={{0,128},{128,0},{1,129},{129,1},{2,130},{130,2},{3,131},{131,3},{4... | collective-permute-start | bytes 589832 | tf_op jit(solution)/shard_map/ppermute | solution.py:36
  14.9 1.4 collective-permute-start.1
  16.4 9.0 %collective-permute-start.4 = (f32[4,48,256]{2,1,0:T(8,128)S(1)}, f32[4,48,256]{2,1,0:T(8,128)S(1)}, u32[]{:S(2)}, u32[]{:S(2)}) collective-permute-start(f32[4,48,256]{2,1,0:T(8,128)S(1)} %shard_map.70.refs_0_), channel_id=1, source_target_pairs={{0,112},{16,0},{32,16},{48,32},{64,48},{80,64},{96,80},{112,96},{1... | collective-permute-start | bytes 589832 | tf_op jit(solution)/shard_map/ppermute | solution.py:40
  25.4 0.0 collective-permute-done.9.refs_9_
  25.4 0.0 collective-permute-start.10
  25.4 4.3 %collective-permute-start.13 = (f32[4,48,256]{2,1,0:T(8,128)S(1)}, f32[4,48,256]{2,1,0:T(8,128)S(1)}, u32[]{:S(2)}, u32[]{:S(2)}) collective-permute-start(f32[4,48,256]{2,1,0:T(8,128)S(1)} %collective-permute-done.9.refs_9_), channel_id=1, source_target_pairs={{0,112},{16,0},{32,16},{48,32},{64,48},{80,64},{96,80},{112,96},{1... | collective-permute-start | bytes 589832 | tf_op jit(solution)/shard_map/ppermute | solution.py:40
  29.7 0.0 collective-permute-done.1.refs_1_
  29.7 0.0 collective-permute-start.2
  29.7 0.0 collective-permute-done.4.refs_4_
  29.7 3.3 %collective-permute-start.5 = (f32[4,48,256]{2,1,0:T(8,128)S(1)}, f32[4,48,256]{2,1,0:T(8,128)S(1)}, u32[]{:S(2)}, u32[]{:S(2)}) collective-permute-start(f32[4,48,256]{2,1,0:T(8,128)S(1)} %collective-permute-done.4.refs_4_), channel_id=1, source_target_pairs={{0,112},{16,0},{32,16},{48,32},{64,48},{80,64},{96,80},{112,96},{1... | collective-permute-start | bytes 589832 | tf_op jit(solution)/shard_map/ppermute | solution.py:40
  33.0 0.7 collective-permute-done.10.refs_10_
  33.7 3.8 %collective-permute-start.14 = (f32[4,48,256]{2,1,0:T(8,128)S(1)}, f32[4,48,256]{2,1,0:T(8,128)S(1)}, u32[]{:S(2)}, u32[]{:S(2)}) collective-permute-start(f32[4,48,256]{2,1,0:T(8,128)S(1)} %collective-permute-done.13.refs_13_), channel_id=1, source_target_pairs={{0,112},{16,0},{32,16},{48,32},{64,48},{80,64},{96,80},{112,96},{1... | collective-permute-start | bytes 589832 | tf_op jit(solution)/shard_map/ppermute | solution.py:40
  37.5 0.5 collective-permute-done.2.refs_2_
  37.9 3.7 %collective-permute-start.6 = (f32[4,48,256]{2,1,0:T(8,128)S(1)}, f32[4,48,256]{2,1,0:T(8,128)S(1)}, u32[]{:S(2)}, u32[]{:S(2)}) collective-permute-start(f32[4,48,256]{2,1,0:T(8,128)S(1)} %collective-permute-done.5.refs_5_), channel_id=1, source_target_pairs={{0,112},{16,0},{32,16},{48,32},{64,48},{80,64},{96,80},{112,96},{1... | collective-permute-start | bytes 589832 | tf_op jit(solution)/shard_map/ppermute | solution.py:40
  41.7 0.5 collective-permute-done.11.refs_11_
  42.1 3.7 %collective-permute-start.15 = (f32[4,48,256]{2,1,0:T(8,128)S(1)}, f32[4,48,256]{2,1,0:T(8,128)S(1)}, u32[]{:S(2)}, u32[]{:S(2)}) collective-permute-start(f32[4,48,256]{2,1,0:T(8,128)S(1)} %collective-permute-done.14.refs_14_), channel_id=1, source_target_pairs={{0,112},{16,0},{32,16},{48,32},{64,48},{80,64},{96,80},{112,96},{1... | collective-permute-start | bytes 589832 | tf_op jit(solution)/shard_map/ppermute | solution.py:40
  45.9 0.5 collective-permute-done.3.refs_3_
  46.4 0.1 collective-permute-start.7
  46.5 4.0 %collective-permute-start.8 = (f32[2,48,256]{2,1,0:T(8,128)S(1)}, f32[2,48,256]{2,1,0:T(8,128)S(1)}, u32[]{:S(2)}, u32[]{:S(2)}) collective-permute-start(f32[2,48,256]{2,1,0:T(8,128)S(1)} %slice.17), channel_id=1, source_target_pairs={{0,112},{16,0},{32,16},{48,32},{64,48},{80,64},{96,80},{112,96},{1... | collective-permute-start | bytes 294920 | tf_op jit(solution)/shard_map/ppermute | solution.py:40
  50.5 0.1 collective-permute-start.16
  50.6 3.9 %collective-permute-start.17 = (f32[2,48,256]{2,1,0:T(8,128)S(1)}, f32[2,48,256]{2,1,0:T(8,128)S(1)}, u32[]{:S(2)}, u32[]{:S(2)}) collective-permute-start(f32[2,48,256]{2,1,0:T(8,128)S(1)} %slice.19), channel_id=1, source_target_pairs={{0,112},{16,0},{32,16},{48,32},{64,48},{80,64},{96,80},{112,96},{1... | collective-permute-start | bytes 294920 | tf_op jit(solution)/shard_map/ppermute | solution.py:40
  54.5 3.2 %shard_map.68.matrix = bf16[768,2304]{1,0:T(8,128)(2,1)S(1)} custom-call(s32[16]{0:T(128)S(1)} %concatenate.3.tab, f32[4608,128]{1,0:T(8,128)} %bitcast.17), custom_call_target="tpu_custom_call" | custom-call | bytes 4194304 | tf_op jit(solution)/shard_map/pallas_call | solution.py:247
  57.8 4.0 %shard_map.72 = f32[8,4,48,256]{3,2,1,0:T(8,128)S(1)} custom-call(s32[16]{0:T(128)S(1)} %concatenate.3.tab, bf16[768,2304]{1,0:T(8,128)(2,1)S(1)} %shard_map.68.matrix, f32[4,48,256]{2,1,0:T(8,128)S(1)} %shard_map.70.refs_0_, f32[4,48,256]{2,1,0:T(8,128)S(1)} %collective-permute-done.1.refs_1_, f32[4,48,256]{2,1,0:T(8,128)S(1)} %collective-permute-done.2.refs_2_, ...), custom_call_target="tpu_custom_call" | custom-call | flops 1811939328 | bytes 4194304 | tf_op jit(solution)/shard_map/pallas_call | solution.py:279
  61.8 0.1 collective-permute-start.18
  61.9 0.7 collective-permute-start.21
  62.6 1.5 collective-permute-start.20
  64.1 2.5 %collective-permute-start.19 = (f32[4,48,256]{2,1,0:T(8,128)S(1)}, f32[4,48,256]{2,1,0:T(8,128)S(1)}, u32[]{:S(2)}, u32[]{:S(2)}) collective-permute-start(f32[4,48,256]{2,1,0:T(8,128)S(1)} %get-tuple-element.19), channel_id=1, source_target_pairs={{0,6},{2,0},{4,2},{6,4},{1,7},{3,1},{5,3},{7,5},{8,14},{10,8},{12,... | collective-permute-start | bytes 589832 | tf_op jit(solution)/shard_map/ppermute | solution.py:52
  66.6 3.2 %collective-permute-done.21 = f32[4,48,256]{2,1,0:T(8,128)S(1)} collective-permute-done((f32[4,48,256]{2,1,0:T(8,128)S(1)}, f32[4,48,256]{2,1,0:T(8,128)S(1)}, u32[]{:S(2)}, u32[]{:S(2)}) %collective-permute-start.21) | collective-permute-done | bytes 196640 | tf_op jit(solution)/shard_map/ppermute | solution.py:52
  69.8 2.1 %collective-permute-done.20 = f32[4,48,256]{2,1,0:T(8,128)S(1)} collective-permute-done((f32[4,48,256]{2,1,0:T(8,128)S(1)}, f32[4,48,256]{2,1,0:T(8,128)S(1)}, u32[]{:S(2)}, u32[]{:S(2)}) %collective-permute-start.20) | collective-permute-done | bytes 196640 | tf_op jit(solution)/shard_map/ppermute | solution.py:52
  71.9 3.2 %collective-permute-done.19 = f32[4,48,256]{2,1,0:T(8,128)S(1)} collective-permute-done((f32[4,48,256]{2,1,0:T(8,128)S(1)}, f32[4,48,256]{2,1,0:T(8,128)S(1)}, u32[]{:S(2)}, u32[]{:S(2)}) %collective-permute-start.19) | collective-permute-done | bytes 196640 | tf_op jit(solution)/shard_map/ppermute | solution.py:52
  75.1 0.1 pad_maximum_fusion.refs_0_
  75.2 3.2 %collective-permute-start.22 = (f32[4,4,48,256]{3,2,1,0:T(8,128)S(1)}, f32[4,4,48,256]{3,2,1,0:T(8,128)S(1)}, u32[]{:S(2)}, u32[]{:S(2)}) collective-permute-start(f32[4,4,48,256]{3,2,1,0:T(8,128)S(1)} %pad_maximum_fusion.refs_0_), channel_id=1, source_target_pairs={{0,8},{8,0},{1,9},{9,1},{2,10},{10,2},{3,11},{11,3},{4,12},{12,4},... | collective-permute-start | bytes 2359304 | tf_op jit(solution)/shard_map/ppermute | solution.py:48
  78.4 17.7 %collective-permute-done.22.refs_1_ = f32[4,4,48,256]{3,2,1,0:T(8,128)S(1)} collective-permute-done((f32[4,4,48,256]{3,2,1,0:T(8,128)S(1)}, f32[4,4,48,256]{3,2,1,0:T(8,128)S(1)}, u32[]{:S(2)}, u32[]{:S(2)}) %collective-permute-start.22) | collective-permute-done | bytes 786464 | tf_op jit(solution)/shard_map/ppermute | solution.py:48
  96.1 0.7 shard_map.73.spread
  96.8 4.0 %shard_map.71.keep = f32[8,4,48,256]{3,2,1,0:T(8,128)S(1)} custom-call(s32[16]{0:T(128)S(1)} %concatenate.3.tab, bf16[768,2304]{1,0:T(8,128)(2,1)S(1)} %shard_map.68.matrix, f32[4,48,256]{2,1,0:T(8,128)S(1)} %shard_map.70.refs_0_, f32[4,48,256]{2,1,0:T(8,128)S(1)} %collective-permute-done.1.refs_1_, f32[4,48,256]{2,1,0:T(8,128)S(1)} %collective-permute-done.2.refs_2_, ...), custom_call_target="tpu_custom_call" | custom-call | flops 1811939328 | bytes 4194304 | tf_op jit(solution)/shard_map/pallas_call | solution.py:279
  100.9 2.6 %shard_map.74 = (f32[2,2,48,256]{3,2,1,0:T(8,128)S(1)}, f32[2,2,48,256]{3,2,1,0:T(8,128)S(1)}, f32[2,2,48,256]{3,2,1,0:T(8,128)S(1)}, f32[2,2,48,256]{3,2,1,0:T(...) custom-call(s32[16]{0:T(128)S(1)} %concatenate.3.tab, ...), custom_call_target="tpu_custom_call" | custom-call | flops 603979776 | bytes 4194304 | tf_op jit(solution)/shard_map/pallas_call | solution.py:291
  103.5 0.1 collective-permute-start.31
  103.6 1.9 %collective-permute-done.31 = f32[16,4,8,256]{3,2,1,0:T(8,128)S(1)} collective-permute-done((f32[16,4,8,256]{3,2,1,0:T(8,128)S(1)}, f32[16,4,8,256]{3,2,1,0:T(8,128)S(1)}, u32[]{:S(2)}, u32[]{:S(2)}) %collective-permute-start.31) | collective-permute-done | bytes 524320 | tf_op jit(solution)/shard_map/ppermute | solution.py:44
  105.5 0.1 add.51
  105.5 16.9 %all_to_all.15 = f32[16,4,8,256]{3,2,1,0:T(8,128)S(1)} all-to-all(f32[16,4,8,256]{3,2,1,0:T(8,128)S(1)} %add.51), channel_id=1, replica_groups=mesh['y_lo'=2,'z'=8,'y_hi'=2,'x'=4,'core'=2] {'y_lo','y_hi','x'}, dimensions={0} | all-to-all | bytes 1048576 | tf_op jit(solution)/shard_map/all_to_all | solution.py:309
  122.5 0.0 copy-start
  122.5 17.5 %all_to_all.16 = f32[8,4,8,256]{3,2,1,0:T(8,128)S(1)} all-to-all(f32[8,4,8,256]{3,2,1,0:T(8,128)S(1)} %broadcast_in_dim.39), channel_id=1, replica_groups=mesh['y_lo'=2,'z'=8,'y_hi'=2,'x'=4,'core'=2] {'z'}, dimensions={0} | all-to-all | bytes 524288 | tf_op jit(solution)/shard_map/all_to_all | solution.py:310
  140.0 12.8 %all_to_all.17.own = f32[16,4,8,256]{3,2,1,0:T(8,128)S(1)} all-to-all(f32[16,4,8,256]{3,2,1,0:T(8,128)S(1)} %broadcast_in_dim.40), channel_id=1, replica_groups=mesh['y_lo'=2,'z'=8,'y_hi'=2,'x'=4,'core'=2] {'y_lo','y_hi','x'}, dimensions={0} | all-to-all | bytes 1048576 | tf_op jit(solution)/shard_map/all_to_all | solution.py:312
  152.8 0.9 collective-permute-start.26
  153.6 0.5 collective-permute-start.23
  154.1 3.1 %collective-permute-start.24 = (f32[2,2,48,256]{3,2,1,0:T(8,128)S(1)}, f32[2,2,48,256]{3,2,1,0:T(8,128)S(1)}, u32[]{:S(2)}, u32[]{:S(2)}) collective-permute-start(f32[2,2,48,256]{3,2,1,0:T(8,128)S(1)} %get-tuple-element.22), channel_id=1, source_target_pairs={{0,4},{2,6},{4,0},{6,2},{1,5},{3,7},{5,1},{7,3},{8,12},{10,14},{12... | collective-permute-start | bytes 589832 | tf_op jit(solution)/shard_map/ppermute | solution.py:52
  157.2 0.5 collective-permute-start.25
  157.7 3.7 %collective-permute-done.23.b = f32[2,2,48,256]{3,2,1,0:T(8,128)S(1)} collective-permute-done((f32[2,2,48,256]{3,2,1,0:T(8,128)S(1)}, f32[2,2,48,256]{3,2,1,0:T(8,128)S(1)}, u32[]{:S(2)}, u32[]{:S(2)}) %collective-permute-start.23) | collective-permute-done | bytes 196640 | tf_op jit(solution)/shard_map/ppermute | solution.py:52
  161.4 2.0 %collective-permute-done.24.c = f32[2,2,48,256]{3,2,1,0:T(8,128)S(1)} collective-permute-done((f32[2,2,48,256]{3,2,1,0:T(8,128)S(1)}, f32[2,2,48,256]{3,2,1,0:T(8,128)S(1)}, u32[]{:S(2)}, u32[]{:S(2)}) %collective-permute-start.24) | collective-permute-done | bytes 196640 | tf_op jit(solution)/shard_map/ppermute | solution.py:52
  163.4 3.1 %collective-permute-done.25.d = f32[2,2,48,256]{3,2,1,0:T(8,128)S(1)} collective-permute-done((f32[2,2,48,256]{3,2,1,0:T(8,128)S(1)}, f32[2,2,48,256]{3,2,1,0:T(8,128)S(1)}, u32[]{:S(2)}, u32[]{:S(2)}) %collective-permute-start.25) | collective-permute-done | bytes 196640 | tf_op jit(solution)/shard_map/ppermute | solution.py:52
  166.6 0.1 shard_map.75
  166.7 2.8 %collective-permute-start.27 = (f32[2,48,256]{2,1,0:T(8,128)S(1)}, f32[2,48,256]{2,1,0:T(8,128)S(1)}, u32[]{:S(2)}, u32[]{:S(2)}) collective-permute-start(f32[2,48,256]{2,1,0:T(8,128)S(1)} %get-tuple-element.27), channel_id=1, source_target_pairs={{0,8},{8,0},{1,9},{9,1},{2,10},{10,2},{3,11},{11,3},{4,12},{12,4},... | collective-permute-start | bytes 294920 | tf_op jit(solution)/shard_map/ppermute | solution.py:48
  169.5 0.6 collective-permute-start.28
  170.1 3.0 %collective-permute-start.29 = (f32[2,48,256]{2,1,0:T(8,128)S(1)}, f32[2,48,256]{2,1,0:T(8,128)S(1)}, u32[]{:S(2)}, u32[]{:S(2)}) collective-permute-start(f32[2,48,256]{2,1,0:T(8,128)S(1)} %get-tuple-element.30), channel_id=1, source_target_pairs={{0,4},{2,6},{4,0},{6,2},{1,5},{3,7},{5,1},{7,3},{8,12},{10,14},{12... | collective-permute-start | bytes 294920 | tf_op jit(solution)/shard_map/ppermute | solution.py:52
  173.1 2.0 %collective-permute-start.30 = (f32[2,48,256]{2,1,0:T(8,128)S(1)}, f32[2,48,256]{2,1,0:T(8,128)S(1)}, u32[]{:S(2)}, u32[]{:S(2)}) collective-permute-start(f32[2,48,256]{2,1,0:T(8,128)S(1)} %get-tuple-element.31), channel_id=1, source_target_pairs={{0,6},{2,0},{4,2},{6,4},{1,7},{3,1},{5,3},{7,5},{8,14},{10,8},{12,... | collective-permute-start | bytes 294920 | tf_op jit(solution)/shard_map/ppermute | solution.py:52
  175.1 1.5 collective-permute-done.29.e
  176.6 1.1 collective-permute-done.30.f
  177.7 0.7 shard_map.76
  178.4 1.6 shard_map.77
  (29 shorter events, 0.2 us)
Async XLA Ops:
  0.6 10.3 %collective-permute-start = (f32[4,48,256]{2,1,0:T(8,128)}, f32[4,48,256]{2,1,0:T(8,128)S(1)}, u32[]{:S(2)}, u32[]{:S(2)}) collective-permute-start(f32[4,48,256]{2,1,0:T(8,128)} %bitcast.18), channel_id=1, source_target_pairs={{0,0},{1,64},{2,16},{3,96},{4,32},{5,112},{6,48},{7,80},{8,128},{9... | collective-permute-start | bytes 589832 | tf_op jit(solution)/shard_map/ppermute | solution.py:32
  12.3 13.2 %collective-permute-start.9 = (f32[4,48,256]{2,1,0:T(8,128)S(1)}, f32[4,48,256]{2,1,0:T(8,128)S(1)}, u32[]{:S(2)}, u32[]{:S(2)}) collective-permute-start(f32[4,48,256]{2,1,0:T(8,128)S(1)} %shard_map.70.refs_0_), channel_id=1, source_target_pairs={{0,128},{128,0},{1,129},{129,1},{2,130},{130,2},{3,131},{131,3},{4... | collective-permute-start | bytes 589832 | tf_op jit(solution)/shard_map/ppermute | solution.py:36
  14.9 14.8 %collective-permute-start.1 = (f32[4,48,256]{2,1,0:T(8,128)S(1)}, f32[4,48,256]{2,1,0:T(8,128)S(1)}, u32[]{:S(2)}, u32[]{:S(2)}) collective-permute-start(f32[4,48,256]{2,1,0:T(8,128)S(1)} %shard_map.70.refs_0_), channel_id=1, source_target_pairs={{0,16},{16,32},{32,48},{48,64},{64,80},{80,96},{96,112},{112,0},{1... | collective-permute-start | bytes 589832 | tf_op jit(solution)/shard_map/ppermute | solution.py:40
  16.4 13.3 %collective-permute-start.4 = (f32[4,48,256]{2,1,0:T(8,128)S(1)}, f32[4,48,256]{2,1,0:T(8,128)S(1)}, u32[]{:S(2)}, u32[]{:S(2)}) collective-permute-start(f32[4,48,256]{2,1,0:T(8,128)S(1)} %shard_map.70.refs_0_), channel_id=1, source_target_pairs={{0,112},{16,0},{32,16},{48,32},{64,48},{80,64},{96,80},{112,96},{1... | collective-permute-start | bytes 589832 | tf_op jit(solution)/shard_map/ppermute | solution.py:40
  25.4 8.2 %collective-permute-start.10 = (f32[4,48,256]{2,1,0:T(8,128)S(1)}, f32[4,48,256]{2,1,0:T(8,128)S(1)}, u32[]{:S(2)}, u32[]{:S(2)}) collective-permute-start(f32[4,48,256]{2,1,0:T(8,128)S(1)} %collective-permute-done.9.refs_9_), channel_id=1, source_target_pairs={{0,16},{16,32},{32,48},{48,64},{64,80},{80,96},{96,112},{112,0},{1... | collective-permute-start | bytes 589832 | tf_op jit(solution)/shard_map/ppermute | solution.py:40
  25.4 8.2 %collective-permute-start.13 = (f32[4,48,256]{2,1,0:T(8,128)S(1)}, f32[4,48,256]{2,1,0:T(8,128)S(1)}, u32[]{:S(2)}, u32[]{:S(2)}) collective-permute-start(f32[4,48,256]{2,1,0:T(8,128)S(1)} %collective-permute-done.9.refs_9_), channel_id=1, source_target_pairs={{0,112},{16,0},{32,16},{48,32},{64,48},{80,64},{96,80},{112,96},{1... | collective-permute-start | bytes 589832 | tf_op jit(solution)/shard_map/ppermute | solution.py:40
  29.7 8.2 %collective-permute-start.2 = (f32[4,48,256]{2,1,0:T(8,128)S(1)}, f32[4,48,256]{2,1,0:T(8,128)S(1)}, u32[]{:S(2)}, u32[]{:S(2)}) collective-permute-start(f32[4,48,256]{2,1,0:T(8,128)S(1)} %collective-permute-done.1.refs_1_), channel_id=1, source_target_pairs={{0,16},{16,32},{32,48},{48,64},{64,80},{80,96},{96,112},{112,0},{1... | collective-permute-start | bytes 589832 | tf_op jit(solution)/shard_map/ppermute | solution.py:40
  29.7 8.2 %collective-permute-start.5 = (f32[4,48,256]{2,1,0:T(8,128)S(1)}, f32[4,48,256]{2,1,0:T(8,128)S(1)}, u32[]{:S(2)}, u32[]{:S(2)}) collective-permute-start(f32[4,48,256]{2,1,0:T(8,128)S(1)} %collective-permute-done.4.refs_4_), channel_id=1, source_target_pairs={{0,112},{16,0},{32,16},{48,32},{64,48},{80,64},{96,80},{112,96},{1... | collective-permute-start | bytes 589832 | tf_op jit(solution)/shard_map/ppermute | solution.py:40
  33.7 8.5 %collective-permute-start.11 = (f32[4,48,256]{2,1,0:T(8,128)S(1)}, f32[4,48,256]{2,1,0:T(8,128)S(1)}, u32[]{:S(2)}, u32[]{:S(2)}) collective-permute-start(f32[4,48,256]{2,1,0:T(8,128)S(1)} %collective-permute-done.10.refs_10_), channel_id=1, source_target_pairs={{0,16},{16,32},{32,48},{48,64},{64,80},{80,96},{96,112},{112,0},{1... | collective-permute-start | bytes 589832 | tf_op jit(solution)/shard_map/ppermute | solution.py:40
  33.7 8.5 %collective-permute-start.14 = (f32[4,48,256]{2,1,0:T(8,128)S(1)}, f32[4,48,256]{2,1,0:T(8,128)S(1)}, u32[]{:S(2)}, u32[]{:S(2)}) collective-permute-start(f32[4,48,256]{2,1,0:T(8,128)S(1)} %collective-permute-done.13.refs_13_), channel_id=1, source_target_pairs={{0,112},{16,0},{32,16},{48,32},{64,48},{80,64},{96,80},{112,96},{1... | collective-permute-start | bytes 589832 | tf_op jit(solution)/shard_map/ppermute | solution.py:40
  37.9 8.4 %collective-permute-start.3 = (f32[4,48,256]{2,1,0:T(8,128)S(1)}, f32[4,48,256]{2,1,0:T(8,128)S(1)}, u32[]{:S(2)}, u32[]{:S(2)}) collective-permute-start(f32[4,48,256]{2,1,0:T(8,128)S(1)} %collective-permute-done.2.refs_2_), channel_id=1, source_target_pairs={{0,16},{16,32},{32,48},{48,64},{64,80},{80,96},{96,112},{112,0},{1... | collective-permute-start | bytes 589832 | tf_op jit(solution)/shard_map/ppermute | solution.py:40
  37.9 8.5 %collective-permute-start.6 = (f32[4,48,256]{2,1,0:T(8,128)S(1)}, f32[4,48,256]{2,1,0:T(8,128)S(1)}, u32[]{:S(2)}, u32[]{:S(2)}) collective-permute-start(f32[4,48,256]{2,1,0:T(8,128)S(1)} %collective-permute-done.5.refs_5_), channel_id=1, source_target_pairs={{0,112},{16,0},{32,16},{48,32},{64,48},{80,64},{96,80},{112,96},{1... | collective-permute-start | bytes 589832 | tf_op jit(solution)/shard_map/ppermute | solution.py:40
  42.1 8.3 %collective-permute-start.12 = (f32[4,48,256]{2,1,0:T(8,128)S(1)}, f32[4,48,256]{2,1,0:T(8,128)S(1)}, u32[]{:S(2)}, u32[]{:S(2)}) collective-permute-start(f32[4,48,256]{2,1,0:T(8,128)S(1)} %collective-permute-done.11.refs_11_), channel_id=1, source_target_pairs={{0,16},{16,32},{32,48},{48,64},{64,80},{80,96},{96,112},{112,0},{1... | collective-permute-start | bytes 589832 | tf_op jit(solution)/shard_map/ppermute | solution.py:40
  42.1 8.4 %collective-permute-start.15 = (f32[4,48,256]{2,1,0:T(8,128)S(1)}, f32[4,48,256]{2,1,0:T(8,128)S(1)}, u32[]{:S(2)}, u32[]{:S(2)}) collective-permute-start(f32[4,48,256]{2,1,0:T(8,128)S(1)} %collective-permute-done.14.refs_14_), channel_id=1, source_target_pairs={{0,112},{16,0},{32,16},{48,32},{64,48},{80,64},{96,80},{112,96},{1... | collective-permute-start | bytes 589832 | tf_op jit(solution)/shard_map/ppermute | solution.py:40
  46.4 11.4 %collective-permute-start.7 = (f32[2,48,256]{2,1,0:T(8,128)S(1)}, f32[2,48,256]{2,1,0:T(8,128)S(1)}, u32[]{:S(2)}, u32[]{:S(2)}) collective-permute-start(f32[2,48,256]{2,1,0:T(8,128)S(1)} %slice.16), channel_id=1, source_target_pairs={{0,16},{16,32},{32,48},{48,64},{64,80},{80,96},{96,112},{112,0},{1... | collective-permute-start | bytes 294920 | tf_op jit(solution)/shard_map/ppermute | solution.py:40
  46.5 11.3 %collective-permute-start.8 = (f32[2,48,256]{2,1,0:T(8,128)S(1)}, f32[2,48,256]{2,1,0:T(8,128)S(1)}, u32[]{:S(2)}, u32[]{:S(2)}) collective-permute-start(f32[2,48,256]{2,1,0:T(8,128)S(1)} %slice.17), channel_id=1, source_target_pairs={{0,112},{16,0},{32,16},{48,32},{64,48},{80,64},{96,80},{112,96},{1... | collective-permute-start | bytes 294920 | tf_op jit(solution)/shard_map/ppermute | solution.py:40
  50.5 7.3 %collective-permute-start.16 = (f32[2,48,256]{2,1,0:T(8,128)S(1)}, f32[2,48,256]{2,1,0:T(8,128)S(1)}, u32[]{:S(2)}, u32[]{:S(2)}) collective-permute-start(f32[2,48,256]{2,1,0:T(8,128)S(1)} %slice.18), channel_id=1, source_target_pairs={{0,16},{16,32},{32,48},{48,64},{64,80},{80,96},{96,112},{112,0},{1... | collective-permute-start | bytes 294920 | tf_op jit(solution)/shard_map/ppermute | solution.py:40
  50.6 7.2 %collective-permute-start.17 = (f32[2,48,256]{2,1,0:T(8,128)S(1)}, f32[2,48,256]{2,1,0:T(8,128)S(1)}, u32[]{:S(2)}, u32[]{:S(2)}) collective-permute-start(f32[2,48,256]{2,1,0:T(8,128)S(1)} %slice.19), channel_id=1, source_target_pairs={{0,112},{16,0},{32,16},{48,32},{64,48},{80,64},{96,80},{112,96},{1... | collective-permute-start | bytes 294920 | tf_op jit(solution)/shard_map/ppermute | solution.py:40
  61.8 39.0 %collective-permute-start.18 = (f32[8,4,48,256]{3,2,1,0:T(8,128)S(1)}, f32[8,4,48,256]{3,2,1,0:T(8,128)S(1)}, u32[]{:S(2)}, u32[]{:S(2)}) collective-permute-start(f32[8,4,48,256]{3,2,1,0:T(8,128)S(1)} %shard_map.72), channel_id=1, source_target_pairs={{0,1},{1,0},{2,3},{3,2},{4,5},{5,4},{6,7},{7,6},{8,9},{9,8},{10,11... | collective-permute-start | bytes 4718600 | tf_op jit(solution)/shard_map/ppermute | solution.py:44
  61.9 7.9 %collective-permute-start.21 = (f32[4,48,256]{2,1,0:T(8,128)S(1)}, f32[4,48,256]{2,1,0:T(8,128)S(1)}, u32[]{:S(2)}, u32[]{:S(2)}) collective-permute-start(f32[4,48,256]{2,1,0:T(8,128)S(1)} %get-tuple-element.19), channel_id=1, source_target_pairs={{0,2},{2,4},{4,6},{6,0},{1,3},{3,5},{5,7},{7,1},{8,10},{10,12},{12... | collective-permute-start | bytes 589832 | tf_op jit(solution)/shard_map/ppermute | solution.py:52
  62.6 9.3 %collective-permute-start.20 = (f32[4,48,256]{2,1,0:T(8,128)S(1)}, f32[4,48,256]{2,1,0:T(8,128)S(1)}, u32[]{:S(2)}, u32[]{:S(2)}) collective-permute-start(f32[4,48,256]{2,1,0:T(8,128)S(1)} %get-tuple-element.19), channel_id=1, source_target_pairs={{0,4},{2,6},{4,0},{6,2},{1,5},{3,7},{5,1},{7,3},{8,12},{10,14},{12... | collective-permute-start | bytes 589832 | tf_op jit(solution)/shard_map/ppermute | solution.py:52
  64.1 11.1 %collective-permute-start.19 = (f32[4,48,256]{2,1,0:T(8,128)S(1)}, f32[4,48,256]{2,1,0:T(8,128)S(1)}, u32[]{:S(2)}, u32[]{:S(2)}) collective-permute-start(f32[4,48,256]{2,1,0:T(8,128)S(1)} %get-tuple-element.19), channel_id=1, source_target_pairs={{0,6},{2,0},{4,2},{6,4},{1,7},{3,1},{5,3},{7,5},{8,14},{10,8},{12,... | collective-permute-start | bytes 589832 | tf_op jit(solution)/shard_map/ppermute | solution.py:52
  75.2 20.9 %collective-permute-start.22 = (f32[4,4,48,256]{3,2,1,0:T(8,128)S(1)}, f32[4,4,48,256]{3,2,1,0:T(8,128)S(1)}, u32[]{:S(2)}, u32[]{:S(2)}) collective-permute-start(f32[4,4,48,256]{3,2,1,0:T(8,128)S(1)} %pad_maximum_fusion.refs_0_), channel_id=1, source_target_pairs={{0,8},{8,0},{1,9},{9,1},{2,10},{10,2},{3,11},{11,3},{4,12},{12,4},... | collective-permute-start | bytes 2359304 | tf_op jit(solution)/shard_map/ppermute | solution.py:48
  103.5 2.0 %collective-permute-start.31 = (f32[16,4,8,256]{3,2,1,0:T(8,128)S(1)}, f32[16,4,8,256]{3,2,1,0:T(8,128)S(1)}, u32[]{:S(2)}, u32[]{:S(2)}) collective-permute-start(f32[16,4,8,256]{3,2,1,0:T(8,128)S(1)} %get-tuple-element.33), channel_id=1, source_target_pairs={{0,1},{1,0},{2,3},{3,2},{4,5},{5,4},{6,7},{7,6},{8,9},{9,8},{10,11... | collective-permute-start | bytes 1572872 | tf_op jit(solution)/shard_map/ppermute | solution.py:44
  122.5 55.9 %copy-start = (f32[4,256,256]{2,1,0:T(8,128)S(1)}, f32[4,256,256]{2,1,0:T(8,128)}, u32[]{:S(2)}) copy-start(f32[4,256,256]{2,1,0:T(8,128)} %dinv.1) | copy-start | bytes 3145732
  152.8 25.6 %collective-permute-start.32 = (f32[16,4,8,256]{3,2,1,0:T(8,128)S(1)}, f32[16,4,8,256]{3,2,1,0:T(8,128)S(1)}, u32[]{:S(2)}, u32[]{:S(2)}) collective-permute-start(f32[16,4,8,256]{3,2,1,0:T(8,128)S(1)} %all_to_all.17.own), channel_id=1, source_target_pairs={{0,1},{1,0},{2,3},{3,2},{4,5},{5,4},{6,7},{7,6},{8,9},{9,8},{10,11... | collective-permute-start | bytes 1572872 | tf_op jit(solution)/shard_map/ppermute | solution.py:44
  152.8 13.8 %collective-permute-start.26 = (f32[4,2,48,256]{3,2,1,0:T(8,128)S(1)}, f32[4,2,48,256]{3,2,1,0:T(8,128)S(1)}, u32[]{:S(2)}, u32[]{:S(2)}) collective-permute-start(f32[4,2,48,256]{3,2,1,0:T(8,128)S(1)} %get-tuple-element.25), channel_id=1, source_target_pairs={{0,8},{8,0},{1,9},{9,1},{2,10},{10,2},{3,11},{11,3},{4,12},{12,4},... | collective-permute-start | bytes 1179656 | tf_op jit(solution)/shard_map/ppermute | solution.py:48
  153.6 7.8 %collective-permute-start.23 = (f32[2,2,48,256]{3,2,1,0:T(8,128)S(1)}, f32[2,2,48,256]{3,2,1,0:T(8,128)S(1)}, u32[]{:S(2)}, u32[]{:S(2)}) collective-permute-start(f32[2,2,48,256]{3,2,1,0:T(8,128)S(1)} %get-tuple-element.21), channel_id=1, source_target_pairs={{0,2},{2,4},{4,6},{6,0},{1,3},{3,5},{5,7},{7,1},{8,10},{10,12},{12... | collective-permute-start | bytes 589832 | tf_op jit(solution)/shard_map/ppermute | solution.py:52
  154.1 9.3 %collective-permute-start.24 = (f32[2,2,48,256]{3,2,1,0:T(8,128)S(1)}, f32[2,2,48,256]{3,2,1,0:T(8,128)S(1)}, u32[]{:S(2)}, u32[]{:S(2)}) collective-permute-start(f32[2,2,48,256]{3,2,1,0:T(8,128)S(1)} %get-tuple-element.22), channel_id=1, source_target_pairs={{0,4},{2,6},{4,0},{6,2},{1,5},{3,7},{5,1},{7,3},{8,12},{10,14},{12... | collective-permute-start | bytes 589832 | tf_op jit(solution)/shard_map/ppermute | solution.py:52
  157.2 9.4 %collective-permute-start.25 = (f32[2,2,48,256]{3,2,1,0:T(8,128)S(1)}, f32[2,2,48,256]{3,2,1,0:T(8,128)S(1)}, u32[]{:S(2)}, u32[]{:S(2)}) collective-permute-start(f32[2,2,48,256]{3,2,1,0:T(8,128)S(1)} %get-tuple-element.23), channel_id=1, source_target_pairs={{0,6},{2,0},{4,2},{6,4},{1,7},{3,1},{5,3},{7,5},{8,14},{10,8},{12,... | collective-permute-start | bytes 589832 | tf_op jit(solution)/shard_map/ppermute | solution.py:52
  166.7 8.4 %collective-permute-start.27 = (f32[2,48,256]{2,1,0:T(8,128)S(1)}, f32[2,48,256]{2,1,0:T(8,128)S(1)}, u32[]{:S(2)}, u32[]{:S(2)}) collective-permute-start(f32[2,48,256]{2,1,0:T(8,128)S(1)} %get-tuple-element.27), channel_id=1, source_target_pairs={{0,8},{8,0},{1,9},{9,1},{2,10},{10,2},{3,11},{11,3},{4,12},{12,4},... | collective-permute-start | bytes 294920 | tf_op jit(solution)/shard_map/ppermute | solution.py:48
  169.5 5.6 %collective-permute-start.28 = (f32[2,48,256]{2,1,0:T(8,128)S(1)}, f32[2,48,256]{2,1,0:T(8,128)S(1)}, u32[]{:S(2)}, u32[]{:S(2)}) collective-permute-start(f32[2,48,256]{2,1,0:T(8,128)S(1)} %get-tuple-element.29), channel_id=1, source_target_pairs={{0,2},{2,4},{4,6},{6,0},{1,3},{3,5},{5,7},{7,1},{8,10},{10,12},{12... | collective-permute-start | bytes 294920 | tf_op jit(solution)/shard_map/ppermute | solution.py:52
  170.1 6.5 %collective-permute-start.29 = (f32[2,48,256]{2,1,0:T(8,128)S(1)}, f32[2,48,256]{2,1,0:T(8,128)S(1)}, u32[]{:S(2)}, u32[]{:S(2)}) collective-permute-start(f32[2,48,256]{2,1,0:T(8,128)S(1)} %get-tuple-element.30), channel_id=1, source_target_pairs={{0,4},{2,6},{4,0},{6,2},{1,5},{3,7},{5,1},{7,3},{8,12},{10,14},{12... | collective-permute-start | bytes 294920 | tf_op jit(solution)/shard_map/ppermute | solution.py:52
  173.1 4.6 %collective-permute-start.30 = (f32[2,48,256]{2,1,0:T(8,128)S(1)}, f32[2,48,256]{2,1,0:T(8,128)S(1)}, u32[]{:S(2)}, u32[]{:S(2)}) collective-permute-start(f32[2,48,256]{2,1,0:T(8,128)S(1)} %get-tuple-element.31), channel_id=1, source_target_pairs={{0,6},{2,0},{4,2},{6,4},{1,7},{3,1},{5,3},{7,5},{8,14},{10,8},{12,... | collective-permute-start | bytes 294920 | tf_op jit(solution)/shard_map/ppermute | solution.py:52

commit v6 on v5

--- a/solution.py
+++ b/solution.py
@@ -52,13 +52,14 @@
     return lax.ppermute(v, "x", [(p, (p + d) % 4) for p in range(4)])
 
 
-def call(body, outs, specs, scratch=(), flops=0, limit=8):
+def call(body, outs, specs, scratch=(), flops=0, limit=8, aliases=None):
     return pl.pallas_call(
         body,
         out_shape=outs,
         in_specs=specs,
         out_specs=jax.tree.map(lambda _: VMEM, outs),
         scratch_shapes=list(scratch),
+        input_output_aliases=aliases or {},
         compiler_params=pltpu.CompilerParams(vmem_limit_bytes=limit << 20),
         cost_estimate=pl.CostEstimate(flops=flops, transcendentals=0, bytes_accessed=4 << 20),
     )
@@ -111,7 +112,7 @@
             out[s, at] = out[s, at] * live[s, i * 16 + p].astype(F32)
 
 
-def matrix_body(tab, source, out, a, *sems):
+def matrix_body(tab, source, out, rest, a, *sems):
     core, x, yh = tab[2], tab[3], tab[5]
     copies = []
     for i in range(3):
@@ -133,36 +134,69 @@
                     for term, part in enumerate((h, l, h)):
                         col = term * 768 + half * 384 + j * 128
                         out[at, col : col + 128] = part
-
-
-def product_body(side, tab, matrix, *refs):
-    pieces, out, held = refs[:18], refs[18], refs[19]
-
-    def put(block, n, d):
-        half = (tab[1] + n // 9) % 2
-        start = pl.multiple_of(half * 384 + tab[8 + d % 8], 16)
-        h, l = split_two(block)
-        for i in range(3):
-            for term, part in enumerate((l, h, h)):
-                at = pl.ds(term * 768 + i * 128 + start, 16)
-                held[at, :] = part[i * 16 : i * 16 + 16]
-
-    @pl.loop(0, 4)
-    def _(s):
-        for n in range(18):
-            if n % 9 < 7:
-                put(pieces[n][s], n, STEPS[n % 9])
-            else:
-
-                @pl.when(s // 2 == n % 9 - 7)
-                def _(n=n):
-                    put(pieces[n][s % 2], n, 4)
-
+                    h, l = split_two(-pltpu.roll(block, (128 - tab[12]) % 128, 1)[:, :16])
+                    for term, part in enumerate((h, l, h)):
+                        col = term * 128 + half * 48 + j * 16
+                        rest[at, col : col + 16] = part
+            for term in range(3):
+                col = term * 128 + 96
+                rest[at, col : col + 32] = jnp.zeros((16, 32), BF16)
+
+
+def put(tab, out, s, block, flip, d):
+    start = pl.multiple_of((tab[1] + flip) % 2 * 384 + tab[8 + d % 8], 16)
+    h, l = split_two(block)
+    for i in range(3):
+        for term, part in enumerate((l, h, h)):
+            out[s, pl.ds(term * 768 + i * 128 + start, 16), :] = part[i * 16 : i * 16 + 16]
+
+
+def join_body(tab, *refs):
+    out = refs[14]
+
+    zeros = jnp.zeros((16, 256), BF16)
+    base = pl.multiple_of(tab[12], 16)
+
+    @pl.loop(0, 4)
+    def _(s):
+        for n in range(14):
+            put(tab, out, s, refs[n][s], n // 7, STEPS[n % 7])
+        for k in range(18):
+            out[s, pl.ds(k * 128 + base, 16), :] = zeros
+
+
+def multiply_side(side, s, matrix, joined, out):
+    value = jnp.dot(
+        matrix[side * 384 : side * 384 + 384, :], joined[s], preferred_element_type=F32
+    )
+    for k in range(8):
+        out[k, s] = value[k * 48 : k * 48 + 48]
+
+
+def side_body(side, matrix, joined, out):
+    @pl.loop(0, 4)
+    def _(s):
+        multiply_side(side, s, matrix, joined, out)
+
+
+def rest_body(side, tab, rest, before, a, b, c, d, out, held):
+    held[...] = jnp.zeros_like(held)
+    for s in range(4):
+        for flip, block in enumerate(((a if s < 2 else b)[s % 2], (c if s < 2 else d)[s % 2])):
+            start = pl.multiple_of((tab[1] + flip) % 2 * 48, 16)
+            h, l = split_two(block)
+            for i in range(3):
+                for term, part in enumerate((l, h, h)):
+                    at = pl.ds(term * 128 + i * 16 + start, 16)
+                    held[s, at, :] = part[i * 16 : i * 16 + 16]
+
+    @pl.loop(0, 4)
+    def _(s):
         value = jnp.dot(
-            matrix[side * 384 : side * 384 + 384, :], held[...], preferred_element_type=F32
+            rest[side * 384 : side * 384 + 384, :], held[s], preferred_element_type=F32
         )
         for k in range(8):
-            out[k, s] = value[k * 48 : k * 48 + 48]
+            out[k, s] = before[k, s] + value[k * 48 : k * 48 + 48]
 
 
 def spread_body(*refs):
@@ -177,24 +211,13 @@
             out[s, :, term * 384 : term * 384 + 384] = part
 
 
-def pair_body(tab, keep, other, spread, *refs):
-    by_x, by_y, (mine, yours, held, value) = refs[:4], refs[4:6], refs[6:]
+def pair_body(tab, keep, other, spread, mine, yours, held, value):
     core = tab[2]
 
     @pl.loop(0, 4)
     def _(s):
         for k in range(8):
-            part = keep[k, s] + other[k, s]
-
-            @pl.when(s < 2)
-            def _(k=k, part=part):
-                by_x[k // 2][k % 2, s % 2] = part
-
-            @pl.when(s >= 2)
-            def _(k=k, part=part):
-                by_y[k % 2][k // 2, s % 2] = part
-
-            h, l = split_two(part)
+            h, l = split_two(keep[k, s] + other[k, s])
             for term, piece in enumerate((l, h, h)):
                 at = term * 384 + k * 48
                 held[at : at + 48, :] = piece
@@ -202,6 +225,22 @@
         for out, base in ((mine, core * 128), (yours, 128 - core * 128)):
             for e in range(16):
                 out[e, s] = value[pl.ds(pl.multiple_of(base + e * 8, 8), 8), :]
+
+
+def parts_body(keep, other, *outs):
+    by_x, by_y = outs[:4], outs[4:]
+    for s in range(2):
+        for k in range(8):
+            by_x[k // 2][k % 2, s] = keep[k, s] + other[k, s]
+            by_y[k % 2][k // 2, s] = keep[k, s + 2] + other[k, s + 2]
+
+
+def level_body(pieces, out):
+    total = pieces[0]
+    for k in range(1, pieces.shape[0]):
+        total = total + pieces[k]
+    for k in range(out.shape[0]):
+        out[k] = total
 
 
 def first_body(a, b, c, d, e, f, *outs):
@@ -244,9 +283,9 @@
         [pltpu.SMEM((4, 48), jnp.int32), pltpu.VMEM((4, 48, 256), F32), DMA, DMA, DMA],
     )(tab, in_hbm(present), in_hbm(panel), in_hbm(diag_inv))
     near = [lhat] + [shift_x(lhat, -d) for d in (1, 2, 3)]
-    matrix = call(
+    matrix, rest = call(
         matrix_body,
-        shape(768, 2304, dtype=BF16),
+        [shape(768, 2304, dtype=BF16), shape(768, 384, dtype=BF16)],
         [SMEM, HBM],
         [pltpu.VMEM((4608, 128), F32), DMA, DMA, DMA],
     )(tab, in_hbm(ainv.reshape(4608, 128)))
@@ -275,27 +314,45 @@
         [pltpu.VMEM((384, 256), F32)],
     )(near, far)
 
-    def product(side):
-        return call(
-            functools.partial(product_body, side),
+    joined = call(
+        join_body, shape(4, 2304, 256, dtype=BF16), [SMEM] + [VMEM] * 14, limit=12
+    )(tab, *pieces[:7], *pieces[9:16])
+    halves = []
+    for side in (1, 0):
+        half = call(
+            functools.partial(side_body, side),
             shape(8, 4, 48, 256),
-            [SMEM] + [VMEM] * 19,
-            [pltpu.VMEM((2304, 256), BF16)],
+            [VMEM] * 2,
             flops=6 * 384 * 768 * 1024,
-            limit=12,
-        )(tab, matrix, *pieces)
-
-    send = product(1)
-    other = swap_core(send)
-    keep = product(0)
-    *parts, mine, yours = call(
+            limit=16,
+        )(matrix, joined)
+        if side == 0:
+            other = swap_core(halves[0])
+        halves.append(
+            call(
+                functools.partial(rest_body, side),
+                shape(8, 4, 48, 256),
+                [SMEM] + [VMEM] * 6,
+                [pltpu.VMEM((4, 384, 256), BF16)],
+                flops=6 * 384 * 96 * 1024,
+                limit=12,
+            )(tab, rest, half, *pieces[7:9], *pieces[16:18])
+        )
+    keep = halves[1]
+    mine, yours = call(
         pair_body,
-        [shape(2, 2, 48, 256)] * 4 + [shape(4, 2, 48, 256)] * 2 + [shape(16, 4, 8, 256)] * 2,
+        [shape(16, 4, 8, 256)] * 2,
         [SMEM] + [VMEM] * 3,
         [pltpu.VMEM((1152, 256), BF16), pltpu.VMEM((256, 256), F32)],
         flops=6 * 256 * 384 * 1024,
         limit=12,
     )(tab, keep, other, spread)
+    parts = call(
+        parts_body,
+        [shape(2, 2, 48, 256)] * 4 + [shape(4, 2, 48, 256)] * 2,
+        [VMEM] * 2,
+    )(keep, other)
+    parts = list(parts)
     for k in (1, 2, 3):
         parts[k] = shift_x(parts[k], k)
     parts[5] = flip_y(parts[5])
@@ -305,11 +362,13 @@
         parts[2 + k] = shift_x(parts[2 + k], k)
     shares = call(second_body, shape(4, 48, 256), [VMEM] * 6)(*parts)
 
-    term = mine + swap_core(yours)
-    total = jnp.sum(lax.all_to_all(term, PLANE, 0, 0), axis=0)
-    total = lax.all_to_all(jnp.broadcast_to(total[None], (8, 4, 8, 256)), "z", 0, 0)
-    total = jnp.sum(total, axis=0)
-    total = lax.all_to_all(jnp.broadcast_to(total[None], (16, 4, 8, 256)), PLANE, 0, 0)
+    yours = swap_core(yours)
+    term = mine + yours
+    total = lax.all_to_all(term, PLANE, 0, 0)
+    total = call(level_body, shape(8, 4, 8, 256), [VMEM])(total)
+    total = lax.all_to_all(total, "z", 0, 0)
+    total = call(level_body, shape(16, 4, 8, 256), [VMEM])(total)
+    total = lax.all_to_all(total, PLANE, 0, 0)
     diag = call(last_body, shape(4, 256, 256), [SMEM] + [VMEM] * 3)(
         tab, total, swap_core(total), dinv
     )

time: 182 us -> 189 us (1.038)
  Pallas kernels: 20.9 us -> 29.7 us
    pallas_call x4 -> x10, Pallas kernels: 13.9 us -> 22.6 us  [the longest x1 10.1 us: process(): call(matrix_body, [shape(768, 2304, dtype=BF16), shape(768, 384, dtype=BF...]
  transfers between devices with their start and end apart: 33 -> 33, of which waited for: 15 -> 14; matrix products, arithmetic and copies ran while one was open for 0% -> 0% of each run, Pallas kernels for 6% -> 12%
where the time goes in v6:
time: 189 us; the launch traced here: 187 us
  starting transfers between devices  64.7 us (34%)
  blocking collectives  47.1 us (25%)
  waiting for transfers between devices  44.7 us (24%)
  Pallas kernels  29.7 us (16%)
    ppermute x16, starting transfers between devices, shift_z(): return lax.ppermute(v, 'z', [(p, (p + d) % 8) for p in range(8)])  36.3 us
    ppermute x9, waiting for transfers between devices, shift_x(): return lax.ppermute(v, 'x', [(p, (p + d) % 4) for p in range(4)])  20 us
    all_to_all x1, blocking collectives, process(): total = lax.all_to_all(term, PLANE, 0, 0)  17.5 us
    ppermute x3, waiting for transfers between devices, flip_y(): return lax.ppermute(v, 'y_hi', [(0, 1), (1, 0)])  17.5 us
    all_to_all x1, blocking collectives, process(): total = lax.all_to_all(total, 'z', 0, 0)  16.9 us
    ppermute x9, starting transfers between devices, shift_x(): return lax.ppermute(v, 'x', [(p, (p + d) % 4) for p in range(4)])  13.9 us
    all_to_all x1, blocking collectives, process(): total = lax.all_to_all(total, PLANE, 0, 0)  12.8 us
    pallas_call x1, Pallas kernels, process(): call(matrix_body, [shape(768, 2304, dtype=BF16), shape(768, 384, dtype=BF...  10.1 us
  transfers between devices with their start and end apart: 33, of which 14 were waited for; matrix products, arithmetic and copies ran while one was open for 0% of the time, Pallas kernels for 12%

profile of v6, /device:TPU:2, one launch (start us, length us, event | category | flops | bytes accessed | tf_op | source)
XLA Modules:
  0.0 187.5 jit_solution(11175023628404641977)
XLA Ops:
  0.6 3.8 %collective-permute-start = (f32[4,48,256]{2,1,0:T(8,128)}, f32[4,48,256]{2,1,0:T(8,128)S(1)}, u32[]{:S(2)}, u32[]{:S(2)}) collective-permute-start(f32[4,48,256]{2,1,0:T(8,128)} %bitcast.18), channel_id=1, source_target_pairs={{0,0},{1,64},{2,16},{3,96},{4,32},{5,112},{6,48},{7,80},{8,128},{9... | collective-permute-start | bytes 589832 | tf_op jit(solution)/shard_map/ppermute | solution.py:32
  4.5 0.1 concatenate.3.tab
  4.6 2.7 %shard_map.69 = (f32[4,48,256]{2,1,0:T(8,128)S(1)}, f32[4,256,256]{2,1,0:T(8,128)S(1)}) custom-call(s32[16]{0:T(128)S(1)} %concatenate.3.tab, s32[4,48]{1,0:T(4,128)} %present.3, f32[4,48,256]{2,1,0:T(8,128)} %bitcast.19, f32[4,256,256]{2,1,0:T(8,128)} %inverse.1), custom_call_target="tpu_custom_call" | custom-call | bytes 4194304 | tf_op jit(solution)/shard_map/pallas_call | solution.py:279
  7.2 3.7 %collective-permute-done.rows = f32[4,48,256]{2,1,0:T(8,128)S(1)} collective-permute-done((f32[4,48,256]{2,1,0:T(8,128)}, f32[4,48,256]{2,1,0:T(8,128)S(1)}, u32[]{:S(2)}, u32[]{:S(2)}) %collective-permute-start) | collective-permute-done | bytes 196640 | tf_op jit(solution)/shard_map/ppermute | solution.py:32
  11.0 1.3 shard_map.70.refs_0_
  12.3 2.7 %collective-permute-start.7 = (f32[4,48,256]{2,1,0:T(8,128)S(1)}, f32[4,48,256]{2,1,0:T(8,128)S(1)}, u32[]{:S(2)}, u32[]{:S(2)}) collective-permute-start(f32[4,48,256]{2,1,0:T(8,128)S(1)} %shard_map.70.refs_0_), channel_id=1, source_target_pairs={{0,128},{128,0},{1,129},{129,1},{2,130},{130,2},{3,131},{131,3},{4... | collective-permute-start | bytes 589832 | tf_op jit(solution)/shard_map/ppermute | solution.py:36
  14.9 1.4 collective-permute-start.1
  16.4 9.0 %collective-permute-start.4 = (f32[4,48,256]{2,1,0:T(8,128)S(1)}, f32[4,48,256]{2,1,0:T(8,128)S(1)}, u32[]{:S(2)}, u32[]{:S(2)}) collective-permute-start(f32[4,48,256]{2,1,0:T(8,128)S(1)} %shard_map.70.refs_0_), channel_id=1, source_target_pairs={{0,112},{16,0},{32,16},{48,32},{64,48},{80,64},{96,80},{112,96},{1... | collective-permute-start | bytes 589832 | tf_op jit(solution)/shard_map/ppermute | solution.py:40
  25.4 0.0 collective-permute-done.7.refs_7_
  25.4 4.3 %collective-permute-start.11 = (f32[4,48,256]{2,1,0:T(8,128)S(1)}, f32[4,48,256]{2,1,0:T(8,128)S(1)}, u32[]{:S(2)}, u32[]{:S(2)}) collective-permute-start(f32[4,48,256]{2,1,0:T(8,128)S(1)} %collective-permute-done.7.refs_7_), channel_id=1, source_target_pairs={{0,112},{16,0},{32,16},{48,32},{64,48},{80,64},{96,80},{112,96},{1... | collective-permute-start | bytes 589832 | tf_op jit(solution)/shard_map/ppermute | solution.py:40
  29.7 3.3 %collective-permute-start.5 = (f32[4,48,256]{2,1,0:T(8,128)S(1)}, f32[4,48,256]{2,1,0:T(8,128)S(1)}, u32[]{:S(2)}, u32[]{:S(2)}) collective-permute-start(f32[4,48,256]{2,1,0:T(8,128)S(1)} %collective-permute-done.4.refs_4_), channel_id=1, source_target_pairs={{0,112},{16,0},{32,16},{48,32},{64,48},{80,64},{96,80},{112,96},{1... | collective-permute-start | bytes 589832 | tf_op jit(solution)/shard_map/ppermute | solution.py:40
  33.0 0.7 collective-permute-done.8.refs_8_
  33.7 3.8 %collective-permute-start.12 = (f32[4,48,256]{2,1,0:T(8,128)S(1)}, f32[4,48,256]{2,1,0:T(8,128)S(1)}, u32[]{:S(2)}, u32[]{:S(2)}) collective-permute-start(f32[4,48,256]{2,1,0:T(8,128)S(1)} %collective-permute-done.11.refs_11_), channel_id=1, source_target_pairs={{0,112},{16,0},{32,16},{48,32},{64,48},{80,64},{96,80},{112,96},{1... | collective-permute-start | bytes 589832 | tf_op jit(solution)/shard_map/ppermute | solution.py:40
  37.5 0.5 collective-permute-done.2.refs_2_
  37.9 3.7 %collective-permute-start.6 = (f32[4,48,256]{2,1,0:T(8,128)S(1)}, f32[4,48,256]{2,1,0:T(8,128)S(1)}, u32[]{:S(2)}, u32[]{:S(2)}) collective-permute-start(f32[4,48,256]{2,1,0:T(8,128)S(1)} %collective-permute-done.5.refs_5_), channel_id=1, source_target_pairs={{0,112},{16,0},{32,16},{48,32},{64,48},{80,64},{96,80},{112,96},{1... | collective-permute-start | bytes 589832 | tf_op jit(solution)/shard_map/ppermute | solution.py:40
  41.7 0.5 collective-permute-done.9.refs_9_
  42.1 3.7 %collective-permute-start.13 = (f32[4,48,256]{2,1,0:T(8,128)S(1)}, f32[4,48,256]{2,1,0:T(8,128)S(1)}, u32[]{:S(2)}, u32[]{:S(2)}) collective-permute-start(f32[4,48,256]{2,1,0:T(8,128)S(1)} %collective-permute-done.12.refs_12_), channel_id=1, source_target_pairs={{0,112},{16,0},{32,16},{48,32},{64,48},{80,64},{96,80},{112,96},{1... | collective-permute-start | bytes 589832 | tf_op jit(solution)/shard_map/ppermute | solution.py:40
  45.9 10.1 %shard_map.68 = (bf16[768,2304]{1,0:T(8,128)(2,1)S(1)}, bf16[768,384]{1,0:T(8,128)(2,1)S(1)}) custom-call(s32[16]{0:T(128)S(1)} %concatenate.3.tab, f32[4608,128]{1,0:T(8,128)} %bitcast.17), custom_call_target="tpu_custom_call" | custom-call | bytes 4194304 | tf_op jit(solution)/shard_map/pallas_call | solution.py:286
  56.1 0.1 collective-permute-start.14
  56.2 3.5 %collective-permute-start.15 = (f32[2,48,256]{2,1,0:T(8,128)S(1)}, f32[2,48,256]{2,1,0:T(8,128)S(1)}, u32[]{:S(2)}, u32[]{:S(2)}) collective-permute-start(f32[2,48,256]{2,1,0:T(8,128)S(1)} %slice.17), channel_id=1, source_target_pairs={{0,112},{16,0},{32,16},{48,32},{64,48},{80,64},{96,80},{112,96},{1... | collective-permute-start | bytes 294920 | tf_op jit(solution)/shard_map/ppermute | solution.py:40
  59.7 0.1 collective-permute-start.16
  59.8 3.3 %collective-permute-start.17 = (f32[2,48,256]{2,1,0:T(8,128)S(1)}, f32[2,48,256]{2,1,0:T(8,128)S(1)}, u32[]{:S(2)}, u32[]{:S(2)}) collective-permute-start(f32[2,48,256]{2,1,0:T(8,128)S(1)} %slice.19), channel_id=1, source_target_pairs={{0,112},{16,0},{32,16},{48,32},{64,48},{80,64},{96,80},{112,96},{1... | collective-permute-start | bytes 294920 | tf_op jit(solution)/shard_map/ppermute | solution.py:40
  63.1 1.7 shard_map.71.joined
  64.7 2.5 %shard_map.74.before = f32[8,4,48,256]{3,2,1,0:T(8,128)S(1)} custom-call(bf16[768,2304]{1,0:T(8,128)(2,1)S(1)} %get-tuple-element.21.matrix, bf16[4,2304,256]{2,1,0:T(8,128)(2,1)S(1)} %shard_map.71.joined), custom_call_target="tpu_custom_call" | custom-call | flops 1811939328 | bytes 4194304 | tf_op jit(solution)/shard_map/pallas_call | solution.py:322
  67.3 1.7 shard_map.75
  69.0 0.1 collective-permute-start.18
  69.1 1.3 collective-permute-start.29
  70.4 0.5 collective-permute-start.28
  70.8 2.5 %collective-permute-start.27 = (f32[4,48,256]{2,1,0:T(8,128)S(1)}, f32[4,48,256]{2,1,0:T(8,128)S(1)}, u32[]{:S(2)}, u32[]{:S(2)}) collective-permute-start(f32[4,48,256]{2,1,0:T(8,128)S(1)} %get-tuple-element.35), channel_id=1, source_target_pairs={{0,6},{2,0},{4,2},{6,4},{1,7},{3,1},{5,3},{7,5},{8,14},{10,8},{12,... | collective-permute-start | bytes 589832 | tf_op jit(solution)/shard_map/ppermute | solution.py:52
  73.4 3.6 %collective-permute-done.29 = f32[4,48,256]{2,1,0:T(8,128)S(1)} collective-permute-done((f32[4,48,256]{2,1,0:T(8,128)S(1)}, f32[4,48,256]{2,1,0:T(8,128)S(1)}, u32[]{:S(2)}, u32[]{:S(2)}) %collective-permute-start.29) | collective-permute-done | bytes 196640 | tf_op jit(solution)/shard_map/ppermute | solution.py:52
  77.0 2.7 %collective-permute-done.28 = f32[4,48,256]{2,1,0:T(8,128)S(1)} collective-permute-done((f32[4,48,256]{2,1,0:T(8,128)S(1)}, f32[4,48,256]{2,1,0:T(8,128)S(1)}, u32[]{:S(2)}, u32[]{:S(2)}) %collective-permute-start.28) | collective-permute-done | bytes 196640 | tf_op jit(solution)/shard_map/ppermute | solution.py:52
  79.7 2.2 %collective-permute-done.27 = f32[4,48,256]{2,1,0:T(8,128)S(1)} collective-permute-done((f32[4,48,256]{2,1,0:T(8,128)S(1)}, f32[4,48,256]{2,1,0:T(8,128)S(1)}, u32[]{:S(2)}, u32[]{:S(2)}) %collective-permute-start.27) | collective-permute-done | bytes 196640 | tf_op jit(solution)/shard_map/ppermute | solution.py:52
  81.9 0.1 pad_maximum_fusion.refs_0_
  82.0 3.9 %collective-permute-start.30 = (f32[4,4,48,256]{3,2,1,0:T(8,128)S(1)}, f32[4,4,48,256]{3,2,1,0:T(8,128)S(1)}, u32[]{:S(2)}, u32[]{:S(2)}) collective-permute-start(f32[4,4,48,256]{3,2,1,0:T(8,128)S(1)} %pad_maximum_fusion.refs_0_), channel_id=1, source_target_pairs={{0,8},{8,0},{1,9},{9,1},{2,10},{10,2},{3,11},{11,3},{4,12},{12,4},... | collective-permute-start | bytes 2359304 | tf_op jit(solution)/shard_map/ppermute | solution.py:48
  85.8 17.5 %collective-permute-done.30.refs_1_ = f32[4,4,48,256]{3,2,1,0:T(8,128)S(1)} collective-permute-done((f32[4,4,48,256]{3,2,1,0:T(8,128)S(1)}, f32[4,4,48,256]{3,2,1,0:T(8,128)S(1)}, u32[]{:S(2)}, u32[]{:S(2)}) %collective-permute-start.30) | collective-permute-done | bytes 786464 | tf_op jit(solution)/shard_map/ppermute | solution.py:48
  103.3 0.7 shard_map.79.spread
  104.0 2.5 %shard_map.72.before = f32[8,4,48,256]{3,2,1,0:T(8,128)S(1)} custom-call(bf16[768,2304]{1,0:T(8,128)(2,1)S(1)} %get-tuple-element.21.matrix, bf16[4,2304,256]{2,1,0:T(8,128)(2,1)S(1)} %shard_map.71.joined), custom_call_target="tpu_custom_call" | custom-call | flops 1811939328 | bytes 4194304 | tf_op jit(solution)/shard_map/pallas_call | solution.py:322
  106.5 1.7 shard_map.73.keep
  108.2 2.2 %shard_map.80 = (f32[16,4,8,256]{3,2,1,0:T(8,128)S(1)}, f32[16,4,8,256]{3,2,1,0:T(8,128)S(1)}) custom-call(s32[16]{0:T(128)S(1)} %concatenate.3.tab, f32[8,4,48,256]{3,2,1,0:T(8,128)S(1)} %shard_map.73.keep, f32[8,4,48,256]{3,2,1,0:T(8,128)S(1)} %collective-permute-done.18.other, bf16[4,256,1152]{2,1,0:T(8,128)(2,1)S(1)} %shard_map.79.spread), custom_call_target="tpu_custom_call" | custom-call | flops 603979776 | bytes 4194304 | tf_op jit(solution)/shard_map/pallas_call | solution.py:342
  110.4 0.1 collective-permute-start.31
  110.5 1.9 %collective-permute-done.31 = f32[16,4,8,256]{3,2,1,0:T(8,128)S(1)} collective-permute-done((f32[16,4,8,256]{3,2,1,0:T(8,128)S(1)}, f32[16,4,8,256]{3,2,1,0:T(8,128)S(1)}, u32[]{:S(2)}, u32[]{:S(2)}) %collective-permute-start.31) | collective-permute-done | bytes 524320 | tf_op jit(solution)/shard_map/ppermute | solution.py:44
  112.4 0.1 add.51
  112.5 17.5 %all_to_all.15.pieces = f32[16,4,8,256]{3,2,1,0:T(8,128)S(1)} all-to-all(f32[16,4,8,256]{3,2,1,0:T(8,128)S(1)} %add.51), channel_id=1, replica_groups=mesh['y_lo'=2,'z'=8,'y_hi'=2,'x'=4,'core'=2] {'y_lo','y_hi','x'}, dimensions={0} | all-to-all | bytes 1048576 | tf_op jit(solution)/shard_map/all_to_all | solution.py:367
  130.0 16.9 %all_to_all.16.pieces = f32[8,4,8,256]{3,2,1,0:T(8,128)S(1)} all-to-all(f32[8,4,8,256]{3,2,1,0:T(8,128)S(1)} %shard_map.81), channel_id=1, replica_groups=mesh['y_lo'=2,'z'=8,'y_hi'=2,'x'=4,'core'=2] {'z'}, dimensions={0} | all-to-all | bytes 524288 | tf_op jit(solution)/shard_map/all_to_all | solution.py:369
  146.9 0.1 shard_map.82
  146.9 12.8 %all_to_all.17.own = f32[16,4,8,256]{3,2,1,0:T(8,128)S(1)} all-to-all(f32[16,4,8,256]{3,2,1,0:T(8,128)S(1)} %shard_map.82), channel_id=1, replica_groups=mesh['y_lo'=2,'z'=8,'y_hi'=2,'x'=4,'core'=2] {'y_lo','y_hi','x'}, dimensions={0} | all-to-all | bytes 1048576 | tf_op jit(solution)/shard_map/all_to_all | solution.py:371
  159.7 0.2 shard_map.76
  159.8 0.0 copy-start
  159.9 0.9 collective-permute-start.22
  160.8 0.5 collective-permute-start.19
  161.3 3.1 %collective-permute-start.20 = (f32[2,2,48,256]{3,2,1,0:T(8,128)S(1)}, f32[2,2,48,256]{3,2,1,0:T(8,128)S(1)}, u32[]{:S(2)}, u32[]{:S(2)}) collective-permute-start(f32[2,2,48,256]{3,2,1,0:T(8,128)S(1)} %get-tuple-element.25), channel_id=1, source_target_pairs={{0,4},{2,6},{4,0},{6,2},{1,5},{3,7},{5,1},{7,3},{8,12},{10,14},{12... | collective-permute-start | bytes 589832 | tf_op jit(solution)/shard_map/ppermute | solution.py:52
  164.3 0.5 collective-permute-start.21
  164.8 3.7 %collective-permute-done.19.b = f32[2,2,48,256]{3,2,1,0:T(8,128)S(1)} collective-permute-done((f32[2,2,48,256]{3,2,1,0:T(8,128)S(1)}, f32[2,2,48,256]{3,2,1,0:T(8,128)S(1)}, u32[]{:S(2)}, u32[]{:S(2)}) %collective-permute-start.19) | collective-permute-done | bytes 196640 | tf_op jit(solution)/shard_map/ppermute | solution.py:52
  168.6 2.0 %collective-permute-done.20.c = f32[2,2,48,256]{3,2,1,0:T(8,128)S(1)} collective-permute-done((f32[2,2,48,256]{3,2,1,0:T(8,128)S(1)}, f32[2,2,48,256]{3,2,1,0:T(8,128)S(1)}, u32[]{:S(2)}, u32[]{:S(2)}) %collective-permute-start.20) | collective-permute-done | bytes 196640 | tf_op jit(solution)/shard_map/ppermute | solution.py:52
  170.6 3.1 %collective-permute-done.21.d = f32[2,2,48,256]{3,2,1,0:T(8,128)S(1)} collective-permute-done((f32[2,2,48,256]{3,2,1,0:T(8,128)S(1)}, f32[2,2,48,256]{3,2,1,0:T(8,128)S(1)}, u32[]{:S(2)}, u32[]{:S(2)}) %collective-permute-start.21) | collective-permute-done | bytes 196640 | tf_op jit(solution)/shard_map/ppermute | solution.py:52
  173.7 0.1 shard_map.77
  173.8 3.1 %collective-permute-start.23 = (f32[2,48,256]{2,1,0:T(8,128)S(1)}, f32[2,48,256]{2,1,0:T(8,128)S(1)}, u32[]{:S(2)}, u32[]{:S(2)}) collective-permute-start(f32[2,48,256]{2,1,0:T(8,128)S(1)} %get-tuple-element.30), channel_id=1, source_target_pairs={{0,8},{8,0},{1,9},{9,1},{2,10},{10,2},{3,11},{11,3},{4,12},{12,4},... | collective-permute-start | bytes 294920 | tf_op jit(solution)/shard_map/ppermute | solution.py:48
  176.9 0.6 collective-permute-start.24
  177.5 3.0 %collective-permute-start.25 = (f32[2,48,256]{2,1,0:T(8,128)S(1)}, f32[2,48,256]{2,1,0:T(8,128)S(1)}, u32[]{:S(2)}, u32[]{:S(2)}) collective-permute-start(f32[2,48,256]{2,1,0:T(8,128)S(1)} %get-tuple-element.33), channel_id=1, source_target_pairs={{0,4},{2,6},{4,0},{6,2},{1,5},{3,7},{5,1},{7,3},{8,12},{10,14},{12... | collective-permute-start | bytes 294920 | tf_op jit(solution)/shard_map/ppermute | solution.py:52
  180.5 2.0 %collective-permute-start.26 = (f32[2,48,256]{2,1,0:T(8,128)S(1)}, f32[2,48,256]{2,1,0:T(8,128)S(1)}, u32[]{:S(2)}, u32[]{:S(2)}) collective-permute-start(f32[2,48,256]{2,1,0:T(8,128)S(1)} %get-tuple-element.34), channel_id=1, source_target_pairs={{0,6},{2,0},{4,2},{6,4},{1,7},{3,1},{5,3},{7,5},{8,14},{10,8},{12,... | collective-permute-start | bytes 294920 | tf_op jit(solution)/shard_map/ppermute | solution.py:52
  182.5 1.5 collective-permute-done.25.e
  184.0 1.1 collective-permute-done.26.f
  185.1 0.7 shard_map.78
  185.8 1.7 shard_map.83
  (31 shorter events, 0.2 us)
Async XLA Ops:
  0.6 10.3 %collective-permute-start = (f32[4,48,256]{2,1,0:T(8,128)}, f32[4,48,256]{2,1,0:T(8,128)S(1)}, u32[]{:S(2)}, u32[]{:S(2)}) collective-permute-start(f32[4,48,256]{2,1,0:T(8,128)} %bitcast.18), channel_id=1, source_target_pairs={{0,0},{1,64},{2,16},{3,96},{4,32},{5,112},{6,48},{7,80},{8,128},{9... | collective-permute-start | bytes 589832 | tf_op jit(solution)/shard_map/ppermute | solution.py:32
  12.3 13.2 %collective-permute-start.7 = (f32[4,48,256]{2,1,0:T(8,128)S(1)}, f32[4,48,256]{2,1,0:T(8,128)S(1)}, u32[]{:S(2)}, u32[]{:S(2)}) collective-permute-start(f32[4,48,256]{2,1,0:T(8,128)S(1)} %shard_map.70.refs_0_), channel_id=1, source_target_pairs={{0,128},{128,0},{1,129},{129,1},{2,130},{130,2},{3,131},{131,3},{4... | collective-permute-start | bytes 589832 | tf_op jit(solution)/shard_map/ppermute | solution.py:36
  14.9 14.8 %collective-permute-start.1 = (f32[4,48,256]{2,1,0:T(8,128)S(1)}, f32[4,48,256]{2,1,0:T(8,128)S(1)}, u32[]{:S(2)}, u32[]{:S(2)}) collective-permute-start(f32[4,48,256]{2,1,0:T(8,128)S(1)} %shard_map.70.refs_0_), channel_id=1, source_target_pairs={{0,16},{16,32},{32,48},{48,64},{64,80},{80,96},{96,112},{112,0},{1... | collective-permute-start | bytes 589832 | tf_op jit(solution)/shard_map/ppermute | solution.py:40
  16.4 13.3 %collective-permute-start.4 = (f32[4,48,256]{2,1,0:T(8,128)S(1)}, f32[4,48,256]{2,1,0:T(8,128)S(1)}, u32[]{:S(2)}, u32[]{:S(2)}) collective-permute-start(f32[4,48,256]{2,1,0:T(8,128)S(1)} %shard_map.70.refs_0_), channel_id=1, source_target_pairs={{0,112},{16,0},{32,16},{48,32},{64,48},{80,64},{96,80},{112,96},{1... | collective-permute-start | bytes 589832 | tf_op jit(solution)/shard_map/ppermute | solution.py:40
  25.4 8.2 %collective-permute-start.8 = (f32[4,48,256]{2,1,0:T(8,128)S(1)}, f32[4,48,256]{2,1,0:T(8,128)S(1)}, u32[]{:S(2)}, u32[]{:S(2)}) collective-permute-start(f32[4,48,256]{2,1,0:T(8,128)S(1)} %collective-permute-done.7.refs_7_), channel_id=1, source_target_pairs={{0,16},{16,32},{32,48},{48,64},{64,80},{80,96},{96,112},{112,0},{1... | collective-permute-start | bytes 589832 | tf_op jit(solution)/shard_map/ppermute | solution.py:40
  25.4 8.2 %collective-permute-start.11 = (f32[4,48,256]{2,1,0:T(8,128)S(1)}, f32[4,48,256]{2,1,0:T(8,128)S(1)}, u32[]{:S(2)}, u32[]{:S(2)}) collective-permute-start(f32[4,48,256]{2,1,0:T(8,128)S(1)} %collective-permute-done.7.refs_7_), channel_id=1, source_target_pairs={{0,112},{16,0},{32,16},{48,32},{64,48},{80,64},{96,80},{112,96},{1... | collective-permute-start | bytes 589832 | tf_op jit(solution)/shard_map/ppermute | solution.py:40
  29.7 8.2 %collective-permute-start.2 = (f32[4,48,256]{2,1,0:T(8,128)S(1)}, f32[4,48,256]{2,1,0:T(8,128)S(1)}, u32[]{:S(2)}, u32[]{:S(2)}) collective-permute-start(f32[4,48,256]{2,1,0:T(8,128)S(1)} %collective-permute-done.1.refs_1_), channel_id=1, source_target_pairs={{0,16},{16,32},{32,48},{48,64},{64,80},{80,96},{96,112},{112,0},{1... | collective-permute-start | bytes 589832 | tf_op jit(solution)/shard_map/ppermute | solution.py:40
  29.7 8.2 %collective-permute-start.5 = (f32[4,48,256]{2,1,0:T(8,128)S(1)}, f32[4,48,256]{2,1,0:T(8,128)S(1)}, u32[]{:S(2)}, u32[]{:S(2)}) collective-permute-start(f32[4,48,256]{2,1,0:T(8,128)S(1)} %collective-permute-done.4.refs_4_), channel_id=1, source_target_pairs={{0,112},{16,0},{32,16},{48,32},{64,48},{80,64},{96,80},{112,96},{1... | collective-permute-start | bytes 589832 | tf_op jit(solution)/shard_map/ppermute | solution.py:40
  33.7 8.5 %collective-permute-start.9 = (f32[4,48,256]{2,1,0:T(8,128)S(1)}, f32[4,48,256]{2,1,0:T(8,128)S(1)}, u32[]{:S(2)}, u32[]{:S(2)}) collective-permute-start(f32[4,48,256]{2,1,0:T(8,128)S(1)} %collective-permute-done.8.refs_8_), channel_id=1, source_target_pairs={{0,16},{16,32},{32,48},{48,64},{64,80},{80,96},{96,112},{112,0},{1... | collective-permute-start | bytes 589832 | tf_op jit(solution)/shard_map/ppermute | solution.py:40
  33.7 8.5 %collective-permute-start.12 = (f32[4,48,256]{2,1,0:T(8,128)S(1)}, f32[4,48,256]{2,1,0:T(8,128)S(1)}, u32[]{:S(2)}, u32[]{:S(2)}) collective-permute-start(f32[4,48,256]{2,1,0:T(8,128)S(1)} %collective-permute-done.11.refs_11_), channel_id=1, source_target_pairs={{0,112},{16,0},{32,16},{48,32},{64,48},{80,64},{96,80},{112,96},{1... | collective-permute-start | bytes 589832 | tf_op jit(solution)/shard_map/ppermute | solution.py:40
  37.9 18.1 %collective-permute-start.3 = (f32[4,48,256]{2,1,0:T(8,128)S(1)}, f32[4,48,256]{2,1,0:T(8,128)S(1)}, u32[]{:S(2)}, u32[]{:S(2)}) collective-permute-start(f32[4,48,256]{2,1,0:T(8,128)S(1)} %collective-permute-done.2.refs_2_), channel_id=1, source_target_pairs={{0,16},{16,32},{32,48},{48,64},{64,80},{80,96},{96,112},{112,0},{1... | collective-permute-start | bytes 589832 | tf_op jit(solution)/shard_map/ppermute | solution.py:40
  37.9 18.2 %collective-permute-start.6 = (f32[4,48,256]{2,1,0:T(8,128)S(1)}, f32[4,48,256]{2,1,0:T(8,128)S(1)}, u32[]{:S(2)}, u32[]{:S(2)}) collective-permute-start(f32[4,48,256]{2,1,0:T(8,128)S(1)} %collective-permute-done.5.refs_5_), channel_id=1, source_target_pairs={{0,112},{16,0},{32,16},{48,32},{64,48},{80,64},{96,80},{112,96},{1... | collective-permute-start | bytes 589832 | tf_op jit(solution)/shard_map/ppermute | solution.py:40
  42.1 17.5 %collective-permute-start.10 = (f32[4,48,256]{2,1,0:T(8,128)S(1)}, f32[4,48,256]{2,1,0:T(8,128)S(1)}, u32[]{:S(2)}, u32[]{:S(2)}) collective-permute-start(f32[4,48,256]{2,1,0:T(8,128)S(1)} %collective-permute-done.9.refs_9_), channel_id=1, source_target_pairs={{0,16},{16,32},{32,48},{48,64},{64,80},{80,96},{96,112},{112,0},{1... | collective-permute-start | bytes 589832 | tf_op jit(solution)/shard_map/ppermute | solution.py:40
  42.1 17.6 %collective-permute-start.13 = (f32[4,48,256]{2,1,0:T(8,128)S(1)}, f32[4,48,256]{2,1,0:T(8,128)S(1)}, u32[]{:S(2)}, u32[]{:S(2)}) collective-permute-start(f32[4,48,256]{2,1,0:T(8,128)S(1)} %collective-permute-done.12.refs_12_), channel_id=1, source_target_pairs={{0,112},{16,0},{32,16},{48,32},{64,48},{80,64},{96,80},{112,96},{1... | collective-permute-start | bytes 589832 | tf_op jit(solution)/shard_map/ppermute | solution.py:40
  56.1 11.2 %collective-permute-start.14 = (f32[2,48,256]{2,1,0:T(8,128)S(1)}, f32[2,48,256]{2,1,0:T(8,128)S(1)}, u32[]{:S(2)}, u32[]{:S(2)}) collective-permute-start(f32[2,48,256]{2,1,0:T(8,128)S(1)} %slice.16), channel_id=1, source_target_pairs={{0,16},{16,32},{32,48},{48,64},{64,80},{80,96},{96,112},{112,0},{1... | collective-permute-start | bytes 294920 | tf_op jit(solution)/shard_map/ppermute | solution.py:40
  56.2 11.1 %collective-permute-start.15 = (f32[2,48,256]{2,1,0:T(8,128)S(1)}, f32[2,48,256]{2,1,0:T(8,128)S(1)}, u32[]{:S(2)}, u32[]{:S(2)}) collective-permute-start(f32[2,48,256]{2,1,0:T(8,128)S(1)} %slice.17), channel_id=1, source_target_pairs={{0,112},{16,0},{32,16},{48,32},{64,48},{80,64},{96,80},{112,96},{1... | collective-permute-start | bytes 294920 | tf_op jit(solution)/shard_map/ppermute | solution.py:40
  59.7 7.6 %collective-permute-start.16 = (f32[2,48,256]{2,1,0:T(8,128)S(1)}, f32[2,48,256]{2,1,0:T(8,128)S(1)}, u32[]{:S(2)}, u32[]{:S(2)}) collective-permute-start(f32[2,48,256]{2,1,0:T(8,128)S(1)} %slice.18), channel_id=1, source_target_pairs={{0,16},{16,32},{32,48},{48,64},{64,80},{80,96},{96,112},{112,0},{1... | collective-permute-start | bytes 294920 | tf_op jit(solution)/shard_map/ppermute | solution.py:40
  59.8 7.5 %collective-permute-start.17 = (f32[2,48,256]{2,1,0:T(8,128)S(1)}, f32[2,48,256]{2,1,0:T(8,128)S(1)}, u32[]{:S(2)}, u32[]{:S(2)}) collective-permute-start(f32[2,48,256]{2,1,0:T(8,128)S(1)} %slice.19), channel_id=1, source_target_pairs={{0,112},{16,0},{32,16},{48,32},{64,48},{80,64},{96,80},{112,96},{1... | collective-permute-start | bytes 294920 | tf_op jit(solution)/shard_map/ppermute | solution.py:40
  69.0 39.2 %collective-permute-start.18 = (f32[8,4,48,256]{3,2,1,0:T(8,128)S(1)}, f32[8,4,48,256]{3,2,1,0:T(8,128)S(1)}, u32[]{:S(2)}, u32[]{:S(2)}) collective-permute-start(f32[8,4,48,256]{3,2,1,0:T(8,128)S(1)} %shard_map.75), channel_id=1, source_target_pairs={{0,1},{1,0},{2,3},{3,2},{4,5},{5,4},{6,7},{7,6},{8,9},{9,8},{10,11... | collective-permute-start | bytes 4718600 | tf_op jit(solution)/shard_map/ppermute | solution.py:44
  69.1 7.9 %collective-permute-start.29 = (f32[4,48,256]{2,1,0:T(8,128)S(1)}, f32[4,48,256]{2,1,0:T(8,128)S(1)}, u32[]{:S(2)}, u32[]{:S(2)}) collective-permute-start(f32[4,48,256]{2,1,0:T(8,128)S(1)} %get-tuple-element.35), channel_id=1, source_target_pairs={{0,2},{2,4},{4,6},{6,0},{1,3},{3,5},{5,7},{7,1},{8,10},{10,12},{12... | collective-permute-start | bytes 589832 | tf_op jit(solution)/shard_map/ppermute | solution.py:52
  70.4 9.3 %collective-permute-start.28 = (f32[4,48,256]{2,1,0:T(8,128)S(1)}, f32[4,48,256]{2,1,0:T(8,128)S(1)}, u32[]{:S(2)}, u32[]{:S(2)}) collective-permute-start(f32[4,48,256]{2,1,0:T(8,128)S(1)} %get-tuple-element.35), channel_id=1, source_target_pairs={{0,4},{2,6},{4,0},{6,2},{1,5},{3,7},{5,1},{7,3},{8,12},{10,14},{12... | collective-permute-start | bytes 589832 | tf_op jit(solution)/shard_map/ppermute | solution.py:52
  70.8 11.1 %collective-permute-start.27 = (f32[4,48,256]{2,1,0:T(8,128)S(1)}, f32[4,48,256]{2,1,0:T(8,128)S(1)}, u32[]{:S(2)}, u32[]{:S(2)}) collective-permute-start(f32[4,48,256]{2,1,0:T(8,128)S(1)} %get-tuple-element.35), channel_id=1, source_target_pairs={{0,6},{2,0},{4,2},{6,4},{1,7},{3,1},{5,3},{7,5},{8,14},{10,8},{12,... | collective-permute-start | bytes 589832 | tf_op jit(solution)/shard_map/ppermute | solution.py:52
  82.0 21.3 %collective-permute-start.30 = (f32[4,4,48,256]{3,2,1,0:T(8,128)S(1)}, f32[4,4,48,256]{3,2,1,0:T(8,128)S(1)}, u32[]{:S(2)}, u32[]{:S(2)}) collective-permute-start(f32[4,4,48,256]{3,2,1,0:T(8,128)S(1)} %pad_maximum_fusion.refs_0_), channel_id=1, source_target_pairs={{0,8},{8,0},{1,9},{9,1},{2,10},{10,2},{3,11},{11,3},{4,12},{12,4},... | collective-permute-start | bytes 2359304 | tf_op jit(solution)/shard_map/ppermute | solution.py:48
  110.4 2.0 %collective-permute-start.31 = (f32[16,4,8,256]{3,2,1,0:T(8,128)S(1)}, f32[16,4,8,256]{3,2,1,0:T(8,128)S(1)}, u32[]{:S(2)}, u32[]{:S(2)}) collective-permute-start(f32[16,4,8,256]{3,2,1,0:T(8,128)S(1)} %get-tuple-element.37), channel_id=1, source_target_pairs={{0,1},{1,0},{2,3},{3,2},{4,5},{5,4},{6,7},{7,6},{8,9},{9,8},{10,11... | collective-permute-start | bytes 1572872 | tf_op jit(solution)/shard_map/ppermute | solution.py:44
  159.7 26.1 %collective-permute-start.32 = (f32[16,4,8,256]{3,2,1,0:T(8,128)S(1)}, f32[16,4,8,256]{3,2,1,0:T(8,128)S(1)}, u32[]{:S(2)}, u32[]{:S(2)}) collective-permute-start(f32[16,4,8,256]{3,2,1,0:T(8,128)S(1)} %all_to_all.17.own), channel_id=1, source_target_pairs={{0,1},{1,0},{2,3},{3,2},{4,5},{5,4},{6,7},{7,6},{8,9},{9,8},{10,11... | collective-permute-start | bytes 1572872 | tf_op jit(solution)/shard_map/ppermute | solution.py:44
  159.8 26.0 %copy-start = (f32[4,256,256]{2,1,0:T(8,128)S(1)}, f32[4,256,256]{2,1,0:T(8,128)}, u32[]{:S(2)}) copy-start(f32[4,256,256]{2,1,0:T(8,128)} %dinv.1) | copy-start | bytes 3145732
  159.9 13.9 %collective-permute-start.22 = (f32[4,2,48,256]{3,2,1,0:T(8,128)S(1)}, f32[4,2,48,256]{3,2,1,0:T(8,128)S(1)}, u32[]{:S(2)}, u32[]{:S(2)}) collective-permute-start(f32[4,2,48,256]{3,2,1,0:T(8,128)S(1)} %get-tuple-element.28), channel_id=1, source_target_pairs={{0,8},{8,0},{1,9},{9,1},{2,10},{10,2},{3,11},{11,3},{4,12},{12,4},... | collective-permute-start | bytes 1179656 | tf_op jit(solution)/shard_map/ppermute | solution.py:48
  160.8 7.8 %collective-permute-start.19 = (f32[2,2,48,256]{3,2,1,0:T(8,128)S(1)}, f32[2,2,48,256]{3,2,1,0:T(8,128)S(1)}, u32[]{:S(2)}, u32[]{:S(2)}) collective-permute-start(f32[2,2,48,256]{3,2,1,0:T(8,128)S(1)} %get-tuple-element.24), channel_id=1, source_target_pairs={{0,2},{2,4},{4,6},{6,0},{1,3},{3,5},{5,7},{7,1},{8,10},{10,12},{12... | collective-permute-start | bytes 589832 | tf_op jit(solution)/shard_map/ppermute | solution.py:52
  161.3 9.3 %collective-permute-start.20 = (f32[2,2,48,256]{3,2,1,0:T(8,128)S(1)}, f32[2,2,48,256]{3,2,1,0:T(8,128)S(1)}, u32[]{:S(2)}, u32[]{:S(2)}) collective-permute-start(f32[2,2,48,256]{3,2,1,0:T(8,128)S(1)} %get-tuple-element.25), channel_id=1, source_target_pairs={{0,4},{2,6},{4,0},{6,2},{1,5},{3,7},{5,1},{7,3},{8,12},{10,14},{12... | collective-permute-start | bytes 589832 | tf_op jit(solution)/shard_map/ppermute | solution.py:52
  164.3 9.4 %collective-permute-start.21 = (f32[2,2,48,256]{3,2,1,0:T(8,128)S(1)}, f32[2,2,48,256]{3,2,1,0:T(8,128)S(1)}, u32[]{:S(2)}, u32[]{:S(2)}) collective-permute-start(f32[2,2,48,256]{3,2,1,0:T(8,128)S(1)} %get-tuple-element.26), channel_id=1, source_target_pairs={{0,6},{2,0},{4,2},{6,4},{1,7},{3,1},{5,3},{7,5},{8,14},{10,8},{12,... | collective-permute-start | bytes 589832 | tf_op jit(solution)/shard_map/ppermute | solution.py:52
  173.8 8.7 %collective-permute-start.23 = (f32[2,48,256]{2,1,0:T(8,128)S(1)}, f32[2,48,256]{2,1,0:T(8,128)S(1)}, u32[]{:S(2)}, u32[]{:S(2)}) collective-permute-start(f32[2,48,256]{2,1,0:T(8,128)S(1)} %get-tuple-element.30), channel_id=1, source_target_pairs={{0,8},{8,0},{1,9},{9,1},{2,10},{10,2},{3,11},{11,3},{4,12},{12,4},... | collective-permute-start | bytes 294920 | tf_op jit(solution)/shard_map/ppermute | solution.py:48
  176.9 5.6 %collective-permute-start.24 = (f32[2,48,256]{2,1,0:T(8,128)S(1)}, f32[2,48,256]{2,1,0:T(8,128)S(1)}, u32[]{:S(2)}, u32[]{:S(2)}) collective-permute-start(f32[2,48,256]{2,1,0:T(8,128)S(1)} %get-tuple-element.32), channel_id=1, source_target_pairs={{0,2},{2,4},{4,6},{6,0},{1,3},{3,5},{5,7},{7,1},{8,10},{10,12},{12... | collective-permute-start | bytes 294920 | tf_op jit(solution)/shard_map/ppermute | solution.py:52
  177.5 6.5 %collective-permute-start.25 = (f32[2,48,256]{2,1,0:T(8,128)S(1)}, f32[2,48,256]{2,1,0:T(8,128)S(1)}, u32[]{:S(2)}, u32[]{:S(2)}) collective-permute-start(f32[2,48,256]{2,1,0:T(8,128)S(1)} %get-tuple-element.33), channel_id=1, source_target_pairs={{0,4},{2,6},{4,0},{6,2},{1,5},{3,7},{5,1},{7,3},{8,12},{10,14},{12... | collective-permute-start | bytes 294920 | tf_op jit(solution)/shard_map/ppermute | solution.py:52
  180.5 4.6 %collective-permute-start.26 = (f32[2,48,256]{2,1,0:T(8,128)S(1)}, f32[2,48,256]{2,1,0:T(8,128)S(1)}, u32[]{:S(2)}, u32[]{:S(2)}) collective-permute-start(f32[2,48,256]{2,1,0:T(8,128)S(1)} %get-tuple-element.34), channel_id=1, source_target_pairs={{0,6},{2,0},{4,2},{6,4},{1,7},{3,1},{5,3},{7,5},{8,14},{10,8},{12,... | collective-permute-start | bytes 294920 | tf_op jit(solution)/shard_map/ppermute | solution.py:52

commit v7 on v6

--- a/solution.py
+++ b/solution.py
@@ -1,5 +1,3 @@
-import functools
-
 import jax
 import jax.numpy as jnp
 from jax import lax
@@ -112,7 +110,7 @@
             out[s, at] = out[s, at] * live[s, i * 16 + p].astype(F32)
 
 
-def matrix_body(tab, source, out, rest, a, *sems):
+def matrix_body(tab, source, out, a, *sems):
     core, x, yh = tab[2], tab[3], tab[5]
     copies = []
     for i in range(3):
@@ -134,13 +132,6 @@
                     for term, part in enumerate((h, l, h)):
                         col = term * 768 + half * 384 + j * 128
                         out[at, col : col + 128] = part
-                    h, l = split_two(-pltpu.roll(block, (128 - tab[12]) % 128, 1)[:, :16])
-                    for term, part in enumerate((h, l, h)):
-                        col = term * 128 + half * 48 + j * 16
-                        rest[at, col : col + 16] = part
-            for term in range(3):
-                col = term * 128 + 96
-                rest[at, col : col + 32] = jnp.zeros((16, 32), BF16)
 
 
 def put(tab, out, s, block, flip, d):
@@ -154,15 +145,10 @@
 def join_body(tab, *refs):
     out = refs[14]
 
-    zeros = jnp.zeros((16, 256), BF16)
-    base = pl.multiple_of(tab[12], 16)
-
     @pl.loop(0, 4)
     def _(s):
         for n in range(14):
             put(tab, out, s, refs[n][s], n // 7, STEPS[n % 7])
-        for k in range(18):
-            out[s, pl.ds(k * 128 + base, 16), :] = zeros
 
 
 def multiply_side(side, s, matrix, joined, out):
@@ -173,30 +159,20 @@
         out[k, s] = value[k * 48 : k * 48 + 48]
 
 
-def side_body(side, matrix, joined, out):
-    @pl.loop(0, 4)
-    def _(s):
-        multiply_side(side, s, matrix, joined, out)
-
-
-def rest_body(side, tab, rest, before, a, b, c, d, out, held):
-    held[...] = jnp.zeros_like(held)
+def send_body(tab, matrix, before, a, b, c, d, out, joined):
     for s in range(4):
-        for flip, block in enumerate(((a if s < 2 else b)[s % 2], (c if s < 2 else d)[s % 2])):
-            start = pl.multiple_of((tab[1] + flip) % 2 * 48, 16)
-            h, l = split_two(block)
-            for i in range(3):
-                for term, part in enumerate((l, h, h)):
-                    at = pl.ds(term * 128 + i * 16 + start, 16)
-                    held[s, at, :] = part[i * 16 : i * 16 + 16]
-
-    @pl.loop(0, 4)
-    def _(s):
-        value = jnp.dot(
-            rest[side * 384 : side * 384 + 384, :], held[s], preferred_element_type=F32
-        )
-        for k in range(8):
-            out[k, s] = before[k, s] + value[k * 48 : k * 48 + 48]
+        put(tab, joined, s, (a if s < 2 else b)[s % 2], 0, 4)
+        put(tab, joined, s, (c if s < 2 else d)[s % 2], 1, 4)
+
+    @pl.loop(0, 4)
+    def _(s):
+        multiply_side(1, s, matrix, joined, out)
+
+
+def keep_body(matrix, joined, out):
+    @pl.loop(0, 4)
+    def _(s):
+        multiply_side(0, s, matrix, joined, out)
 
 
 def spread_body(*refs):
@@ -283,9 +259,9 @@
         [pltpu.SMEM((4, 48), jnp.int32), pltpu.VMEM((4, 48, 256), F32), DMA, DMA, DMA],
     )(tab, in_hbm(present), in_hbm(panel), in_hbm(diag_inv))
     near = [lhat] + [shift_x(lhat, -d) for d in (1, 2, 3)]
-    matrix, rest = call(
+    matrix = call(
         matrix_body,
-        [shape(768, 2304, dtype=BF16), shape(768, 384, dtype=BF16)],
+        shape(768, 2304, dtype=BF16),
         [SMEM, HBM],
         [pltpu.VMEM((4608, 128), F32), DMA, DMA, DMA],
     )(tab, in_hbm(ainv.reshape(4608, 128)))
@@ -317,28 +293,18 @@
     joined = call(
         join_body, shape(4, 2304, 256, dtype=BF16), [SMEM] + [VMEM] * 14, limit=12
     )(tab, *pieces[:7], *pieces[9:16])
-    halves = []
-    for side in (1, 0):
-        half = call(
-            functools.partial(side_body, side),
-            shape(8, 4, 48, 256),
-            [VMEM] * 2,
-            flops=6 * 384 * 768 * 1024,
-            limit=16,
-        )(matrix, joined)
-        if side == 0:
-            other = swap_core(halves[0])
-        halves.append(
-            call(
-                functools.partial(rest_body, side),
-                shape(8, 4, 48, 256),
-                [SMEM] + [VMEM] * 6,
-                [pltpu.VMEM((4, 384, 256), BF16)],
-                flops=6 * 384 * 96 * 1024,
-                limit=12,
-            )(tab, rest, half, *pieces[7:9], *pieces[16:18])
-        )
-    keep = halves[1]
+    send, joined = call(
+        send_body,
+        [shape(8, 4, 48, 256), shape(4, 2304, 256, dtype=BF16)],
+        [SMEM] + [VMEM] * 6,
+        flops=6 * 384 * 768 * 1024,
+        limit=16,
+        aliases={2: 1},
+    )(tab, matrix, joined, *pieces[7:9], *pieces[16:18])
+    other = swap_core(send)
+    keep = call(
+        keep_body, shape(8, 4, 48, 256), [VMEM] * 2, flops=6 * 384 * 768 * 1024, limit=16
+    )(matrix, joined)
     mine, yours = call(
         pair_body,
         [shape(16, 4, 8, 256)] * 2,

time: 189 us -> 180 us (0.952)
  Pallas kernels: 29.7 us -> 19.9 us
    pallas_call x5 -> x3, Pallas kernels: 18.5 us -> 8.95 us  [the longest x1 3.24 us: process(): call(matrix_body, shape(768, 2304, dtype=BF16), [SMEM, HBM], [pltpu.VMEM(...]
  transfers between devices with their start and end apart: 33 -> 33, of which waited for: 14 -> 15; matrix products, arithmetic and copies ran while one was open for 0% -> 0% of each run, Pallas kernels for 12% -> 7%
where the time goes in v7:
time: 180 us; the launch traced here: 178 us
  starting transfers between devices  65.9 us (37%)
  blocking collectives  46.3 us (26%)
  waiting for transfers between devices  44.9 us (25%)
  Pallas kernels  19.9 us (11%)
    ppermute x16, starting transfers between devices, shift_z(): return lax.ppermute(v, 'z', [(p, (p + d) % 8) for p in range(8)])  37.4 us
    ppermute x9, waiting for transfers between devices, shift_x(): return lax.ppermute(v, 'x', [(p, (p + d) % 4) for p in range(4)])  20.2 us
    all_to_all x1, blocking collectives, process(): total = lax.all_to_all(term, PLANE, 0, 0)  17.8 us
    ppermute x3, waiting for transfers between devices, flip_y(): return lax.ppermute(v, 'y_hi', [(0, 1), (1, 0)])  17 us
    all_to_all x1, blocking collectives, process(): total = lax.all_to_all(total, 'z', 0, 0)  15.8 us
    ppermute x9, starting transfers between devices, shift_x(): return lax.ppermute(v, 'x', [(p, (p + d) % 4) for p in range(4)])  14.3 us
    all_to_all x1, blocking collectives, process(): total = lax.all_to_all(total, PLANE, 0, 0)  12.8 us
    ppermute x3, starting transfers between devices, flip_y(): return lax.ppermute(v, 'y_hi', [(0, 1), (1, 0)])  7.51 us
  transfers between devices with their start and end apart: 33, of which 15 were waited for; matrix products, arithmetic and copies ran while one was open for 0% of the time, Pallas kernels for 7%

profile of v7, /device:TPU:2, one launch (start us, length us, event | category | flops | bytes accessed | tf_op | source)
XLA Modules:
  0.0 178.2 jit_solution(10347641731320999080)
XLA Ops:
  0.6 3.8 %collective-permute-start = (f32[4,48,256]{2,1,0:T(8,128)}, f32[4,48,256]{2,1,0:T(8,128)S(1)}, u32[]{:S(2)}, u32[]{:S(2)}) collective-permute-start(f32[4,48,256]{2,1,0:T(8,128)} %bitcast.18), channel_id=1, source_target_pairs={{0,0},{1,64},{2,16},{3,96},{4,32},{5,112},{6,48},{7,80},{8,128},{9... | collective-permute-start | bytes 589832 | tf_op jit(solution)/shard_map/ppermute | solution.py:30
  4.5 0.1 concatenate.3.tab
  4.6 2.6 %shard_map.69 = (f32[4,48,256]{2,1,0:T(8,128)S(1)}, f32[4,256,256]{2,1,0:T(8,128)S(1)}) custom-call(s32[16]{0:T(128)S(1)} %concatenate.3.tab, s32[4,48]{1,0:T(4,128)} %present.3, f32[4,48,256]{2,1,0:T(8,128)} %bitcast.19, f32[4,256,256]{2,1,0:T(8,128)} %inverse.1), custom_call_target="tpu_custom_call" | custom-call | bytes 4194304 | tf_op jit(solution)/shard_map/pallas_call | solution.py:255
  7.2 3.7 %collective-permute-done.rows = f32[4,48,256]{2,1,0:T(8,128)S(1)} collective-permute-done((f32[4,48,256]{2,1,0:T(8,128)}, f32[4,48,256]{2,1,0:T(8,128)S(1)}, u32[]{:S(2)}, u32[]{:S(2)}) %collective-permute-start) | collective-permute-done | bytes 196640 | tf_op jit(solution)/shard_map/ppermute | solution.py:30
  11.0 1.3 shard_map.70.refs_0_
  12.3 2.7 %collective-permute-start.7 = (f32[4,48,256]{2,1,0:T(8,128)S(1)}, f32[4,48,256]{2,1,0:T(8,128)S(1)}, u32[]{:S(2)}, u32[]{:S(2)}) collective-permute-start(f32[4,48,256]{2,1,0:T(8,128)S(1)} %shard_map.70.refs_0_), channel_id=1, source_target_pairs={{0,128},{128,0},{1,129},{129,1},{2,130},{130,2},{3,131},{131,3},{4... | collective-permute-start | bytes 589832 | tf_op jit(solution)/shard_map/ppermute | solution.py:34
  14.9 1.4 collective-permute-start.1
  16.4 9.0 %collective-permute-start.4 = (f32[4,48,256]{2,1,0:T(8,128)S(1)}, f32[4,48,256]{2,1,0:T(8,128)S(1)}, u32[]{:S(2)}, u32[]{:S(2)}) collective-permute-start(f32[4,48,256]{2,1,0:T(8,128)S(1)} %shard_map.70.refs_0_), channel_id=1, source_target_pairs={{0,112},{16,0},{32,16},{48,32},{64,48},{80,64},{96,80},{112,96},{1... | collective-permute-start | bytes 589832 | tf_op jit(solution)/shard_map/ppermute | solution.py:38
  25.4 0.0 collective-permute-done.7.refs_7_
  25.4 0.0 collective-permute-start.8
  25.4 4.3 %collective-permute-start.11 = (f32[4,48,256]{2,1,0:T(8,128)S(1)}, f32[4,48,256]{2,1,0:T(8,128)S(1)}, u32[]{:S(2)}, u32[]{:S(2)}) collective-permute-start(f32[4,48,256]{2,1,0:T(8,128)S(1)} %collective-permute-done.7.refs_7_), channel_id=1, source_target_pairs={{0,112},{16,0},{32,16},{48,32},{64,48},{80,64},{96,80},{112,96},{1... | collective-permute-start | bytes 589832 | tf_op jit(solution)/shard_map/ppermute | solution.py:38
  29.7 0.0 collective-permute-done.1.refs_1_
  29.7 3.3 %collective-permute-start.5 = (f32[4,48,256]{2,1,0:T(8,128)S(1)}, f32[4,48,256]{2,1,0:T(8,128)S(1)}, u32[]{:S(2)}, u32[]{:S(2)}) collective-permute-start(f32[4,48,256]{2,1,0:T(8,128)S(1)} %collective-permute-done.4.refs_4_), channel_id=1, source_target_pairs={{0,112},{16,0},{32,16},{48,32},{64,48},{80,64},{96,80},{112,96},{1... | collective-permute-start | bytes 589832 | tf_op jit(solution)/shard_map/ppermute | solution.py:38
  33.0 0.7 collective-permute-done.8.refs_8_
  33.7 3.8 %collective-permute-start.12 = (f32[4,48,256]{2,1,0:T(8,128)S(1)}, f32[4,48,256]{2,1,0:T(8,128)S(1)}, u32[]{:S(2)}, u32[]{:S(2)}) collective-permute-start(f32[4,48,256]{2,1,0:T(8,128)S(1)} %collective-permute-done.11.refs_11_), channel_id=1, source_target_pairs={{0,112},{16,0},{32,16},{48,32},{64,48},{80,64},{96,80},{112,96},{1... | collective-permute-start | bytes 589832 | tf_op jit(solution)/shard_map/ppermute | solution.py:38
  37.5 0.5 collective-permute-done.2.refs_2_
  37.9 3.7 %collective-permute-start.6 = (f32[4,48,256]{2,1,0:T(8,128)S(1)}, f32[4,48,256]{2,1,0:T(8,128)S(1)}, u32[]{:S(2)}, u32[]{:S(2)}) collective-permute-start(f32[4,48,256]{2,1,0:T(8,128)S(1)} %collective-permute-done.5.refs_5_), channel_id=1, source_target_pairs={{0,112},{16,0},{32,16},{48,32},{64,48},{80,64},{96,80},{112,96},{1... | collective-permute-start | bytes 589832 | tf_op jit(solution)/shard_map/ppermute | solution.py:38
  41.7 0.5 collective-permute-done.9.refs_9_
  42.1 3.7 %collective-permute-start.13 = (f32[4,48,256]{2,1,0:T(8,128)S(1)}, f32[4,48,256]{2,1,0:T(8,128)S(1)}, u32[]{:S(2)}, u32[]{:S(2)}) collective-permute-start(f32[4,48,256]{2,1,0:T(8,128)S(1)} %collective-permute-done.12.refs_12_), channel_id=1, source_target_pairs={{0,112},{16,0},{32,16},{48,32},{64,48},{80,64},{96,80},{112,96},{1... | collective-permute-start | bytes 589832 | tf_op jit(solution)/shard_map/ppermute | solution.py:38
  45.9 0.5 collective-permute-done.3.refs_3_
  46.4 0.1 collective-permute-start.14
  46.5 4.0 %collective-permute-start.15 = (f32[2,48,256]{2,1,0:T(8,128)S(1)}, f32[2,48,256]{2,1,0:T(8,128)S(1)}, u32[]{:S(2)}, u32[]{:S(2)}) collective-permute-start(f32[2,48,256]{2,1,0:T(8,128)S(1)} %slice.17), channel_id=1, source_target_pairs={{0,112},{16,0},{32,16},{48,32},{64,48},{80,64},{96,80},{112,96},{1... | collective-permute-start | bytes 294920 | tf_op jit(solution)/shard_map/ppermute | solution.py:38
  50.5 0.1 collective-permute-start.16
  50.6 3.9 %collective-permute-start.17 = (f32[2,48,256]{2,1,0:T(8,128)S(1)}, f32[2,48,256]{2,1,0:T(8,128)S(1)}, u32[]{:S(2)}, u32[]{:S(2)}) collective-permute-start(f32[2,48,256]{2,1,0:T(8,128)S(1)} %slice.19), channel_id=1, source_target_pairs={{0,112},{16,0},{32,16},{48,32},{64,48},{80,64},{96,80},{112,96},{1... | collective-permute-start | bytes 294920 | tf_op jit(solution)/shard_map/ppermute | solution.py:38
  54.5 3.2 %shard_map.68.matrix = bf16[768,2304]{1,0:T(8,128)(2,1)S(1)} custom-call(s32[16]{0:T(128)S(1)} %concatenate.3.tab, f32[4608,128]{1,0:T(8,128)} %bitcast.17), custom_call_target="tpu_custom_call" | custom-call | bytes 4194304 | tf_op jit(solution)/shard_map/pallas_call | solution.py:262
  57.8 1.6 shard_map.71.before
  59.4 3.1 %shard_map.72 = (f32[8,4,48,256]{3,2,1,0:T(8,128)S(1)}, bf16[4,2304,256]{2,1,0:T(8,128)(2,1)S(1)}) custom-call(s32[16]{0:T(128)S(1)} %concatenate.3.tab, bf16[768,2304]{1,0:T(8,128)(2,1)S(1)} %shard_map.68.matrix, bf16[4,2304,256]{2,1,0:T(8,128)(2,1)S(1)} %shard_map.71.before, ...), custom_call_target="tpu_custom_call", output_to_operand_aliasing={{1}: (2, {})} | custom-call | flops 1811939328 | bytes 4194304 | tf_op jit(solution)/shard_map/pallas_call | solution.py:296
  62.5 0.1 collective-permute-start.18
  62.6 0.1 collective-permute-start.27
  62.7 2.0 %collective-permute-start.28 = (f32[4,48,256]{2,1,0:T(8,128)S(1)}, f32[4,48,256]{2,1,0:T(8,128)S(1)}, u32[]{:S(2)}, u32[]{:S(2)}) collective-permute-start(f32[4,48,256]{2,1,0:T(8,128)S(1)} %get-tuple-element.35), channel_id=1, source_target_pairs={{0,4},{2,6},{4,0},{6,2},{1,5},{3,7},{5,1},{7,3},{8,12},{10,14},{12... | collective-permute-start | bytes 589832 | tf_op jit(solution)/shard_map/ppermute | solution.py:50
  64.8 2.5 %collective-permute-start.29 = (f32[4,48,256]{2,1,0:T(8,128)S(1)}, f32[4,48,256]{2,1,0:T(8,128)S(1)}, u32[]{:S(2)}, u32[]{:S(2)}) collective-permute-start(f32[4,48,256]{2,1,0:T(8,128)S(1)} %get-tuple-element.35), channel_id=1, source_target_pairs={{0,2},{2,4},{4,6},{6,0},{1,3},{3,5},{5,7},{7,1},{8,10},{10,12},{12... | collective-permute-start | bytes 589832 | tf_op jit(solution)/shard_map/ppermute | solution.py:50
  67.3 2.8 %collective-permute-done.27 = f32[4,48,256]{2,1,0:T(8,128)S(1)} collective-permute-done((f32[4,48,256]{2,1,0:T(8,128)S(1)}, f32[4,48,256]{2,1,0:T(8,128)S(1)}, u32[]{:S(2)}, u32[]{:S(2)}) %collective-permute-start.27) | collective-permute-done | bytes 196640 | tf_op jit(solution)/shard_map/ppermute | solution.py:50
  70.1 4.3 %collective-permute-done.28 = f32[4,48,256]{2,1,0:T(8,128)S(1)} collective-permute-done((f32[4,48,256]{2,1,0:T(8,128)S(1)}, f32[4,48,256]{2,1,0:T(8,128)S(1)}, u32[]{:S(2)}, u32[]{:S(2)}) %collective-permute-start.28) | collective-permute-done | bytes 196640 | tf_op jit(solution)/shard_map/ppermute | solution.py:50
  74.4 1.6 collective-permute-done.29
  76.0 0.1 pad_maximum_fusion.refs_0_
  76.0 3.7 %collective-permute-start.30 = (f32[4,4,48,256]{3,2,1,0:T(8,128)S(1)}, f32[4,4,48,256]{3,2,1,0:T(8,128)S(1)}, u32[]{:S(2)}, u32[]{:S(2)}) collective-permute-start(f32[4,4,48,256]{3,2,1,0:T(8,128)S(1)} %pad_maximum_fusion.refs_0_), channel_id=1, source_target_pairs={{0,8},{8,0},{1,9},{9,1},{2,10},{10,2},{3,11},{11,3},{4,12},{12,4},... | collective-permute-start | bytes 2359304 | tf_op jit(solution)/shard_map/ppermute | solution.py:46
  79.8 17.0 %collective-permute-done.30.refs_1_ = f32[4,4,48,256]{3,2,1,0:T(8,128)S(1)} collective-permute-done((f32[4,4,48,256]{3,2,1,0:T(8,128)S(1)}, f32[4,4,48,256]{3,2,1,0:T(8,128)S(1)}, u32[]{:S(2)}, u32[]{:S(2)}) %collective-permute-start.30) | collective-permute-done | bytes 786464 | tf_op jit(solution)/shard_map/ppermute | solution.py:46
  96.8 0.7 shard_map.77.spread
  97.5 2.6 %shard_map.73.keep = f32[8,4,48,256]{3,2,1,0:T(8,128)S(1)} custom-call(bf16[768,2304]{1,0:T(8,128)(2,1)S(1)} %shard_map.68.matrix, bf16[4,2304,256]{2,1,0:T(8,128)(2,1)S(1)} %get-tuple-element.21.joined), custom_call_target="tpu_custom_call" | custom-call | flops 1811939328 | bytes 4194304 | tf_op jit(solution)/shard_map/pallas_call | solution.py:305
  100.0 2.1 %shard_map.78 = (f32[16,4,8,256]{3,2,1,0:T(8,128)S(1)}, f32[16,4,8,256]{3,2,1,0:T(8,128)S(1)}) custom-call(s32[16]{0:T(128)S(1)} %concatenate.3.tab, f32[8,4,48,256]{3,2,1,0:T(8,128)S(1)} %shard_map.73.keep, f32[8,4,48,256]{3,2,1,0:T(8,128)S(1)} %collective-permute-done.18.other, bf16[4,256,1152]{2,1,0:T(8,128)(2,1)S(1)} %shard_map.77.spread), custom_call_target="tpu_custom_call" | custom-call | flops 603979776 | bytes 4194304 | tf_op jit(solution)/shard_map/pallas_call | solution.py:308
  102.1 0.1 collective-permute-start.31
  102.2 1.9 %collective-permute-done.31 = f32[16,4,8,256]{3,2,1,0:T(8,128)S(1)} collective-permute-done((f32[16,4,8,256]{3,2,1,0:T(8,128)S(1)}, f32[16,4,8,256]{3,2,1,0:T(8,128)S(1)}, u32[]{:S(2)}, u32[]{:S(2)}) %collective-permute-start.31) | collective-permute-done | bytes 524320 | tf_op jit(solution)/shard_map/ppermute | solution.py:42
  104.1 0.1 add.51
  104.2 17.8 %all_to_all.15.pieces = f32[16,4,8,256]{3,2,1,0:T(8,128)S(1)} all-to-all(f32[16,4,8,256]{3,2,1,0:T(8,128)S(1)} %add.51), channel_id=1, replica_groups=mesh['y_lo'=2,'z'=8,'y_hi'=2,'x'=4,'core'=2] {'y_lo','y_hi','x'}, dimensions={0} | all-to-all | bytes 1048576 | tf_op jit(solution)/shard_map/all_to_all | solution.py:333
  122.0 15.8 %all_to_all.16.pieces = f32[8,4,8,256]{3,2,1,0:T(8,128)S(1)} all-to-all(f32[8,4,8,256]{3,2,1,0:T(8,128)S(1)} %shard_map.79), channel_id=1, replica_groups=mesh['y_lo'=2,'z'=8,'y_hi'=2,'x'=4,'core'=2] {'z'}, dimensions={0} | all-to-all | bytes 524288 | tf_op jit(solution)/shard_map/all_to_all | solution.py:335
  137.8 0.1 shard_map.80
  137.9 12.8 %all_to_all.17.own = f32[16,4,8,256]{3,2,1,0:T(8,128)S(1)} all-to-all(f32[16,4,8,256]{3,2,1,0:T(8,128)S(1)} %shard_map.80), channel_id=1, replica_groups=mesh['y_lo'=2,'z'=8,'y_hi'=2,'x'=4,'core'=2] {'y_lo','y_hi','x'}, dimensions={0} | all-to-all | bytes 1048576 | tf_op jit(solution)/shard_map/all_to_all | solution.py:337
  150.6 0.2 shard_map.74
  150.8 0.9 collective-permute-start.22
  151.7 0.5 collective-permute-start.19
  152.2 3.1 %collective-permute-start.20 = (f32[2,2,48,256]{3,2,1,0:T(8,128)S(1)}, f32[2,2,48,256]{3,2,1,0:T(8,128)S(1)}, u32[]{:S(2)}, u32[]{:S(2)}) collective-permute-start(f32[2,2,48,256]{3,2,1,0:T(8,128)S(1)} %get-tuple-element.25), channel_id=1, source_target_pairs={{0,4},{2,6},{4,0},{6,2},{1,5},{3,7},{5,1},{7,3},{8,12},{10,14},{12... | collective-permute-start | bytes 589832 | tf_op jit(solution)/shard_map/ppermute | solution.py:50
  155.3 0.5 collective-permute-start.21
  155.8 3.7 %collective-permute-done.19.b = f32[2,2,48,256]{3,2,1,0:T(8,128)S(1)} collective-permute-done((f32[2,2,48,256]{3,2,1,0:T(8,128)S(1)}, f32[2,2,48,256]{3,2,1,0:T(8,128)S(1)}, u32[]{:S(2)}, u32[]{:S(2)}) %collective-permute-start.19) | collective-permute-done | bytes 196640 | tf_op jit(solution)/shard_map/ppermute | solution.py:50
  159.5 2.0 %collective-permute-done.20.c = f32[2,2,48,256]{3,2,1,0:T(8,128)S(1)} collective-permute-done((f32[2,2,48,256]{3,2,1,0:T(8,128)S(1)}, f32[2,2,48,256]{3,2,1,0:T(8,128)S(1)}, u32[]{:S(2)}, u32[]{:S(2)}) %collective-permute-start.20) | collective-permute-done | bytes 196640 | tf_op jit(solution)/shard_map/ppermute | solution.py:50
  161.5 3.1 %collective-permute-done.21.d = f32[2,2,48,256]{3,2,1,0:T(8,128)S(1)} collective-permute-done((f32[2,2,48,256]{3,2,1,0:T(8,128)S(1)}, f32[2,2,48,256]{3,2,1,0:T(8,128)S(1)}, u32[]{:S(2)}, u32[]{:S(2)}) %collective-permute-start.21) | collective-permute-done | bytes 196640 | tf_op jit(solution)/shard_map/ppermute | solution.py:50
  164.7 0.1 shard_map.75
  164.8 2.8 %collective-permute-start.23 = (f32[2,48,256]{2,1,0:T(8,128)S(1)}, f32[2,48,256]{2,1,0:T(8,128)S(1)}, u32[]{:S(2)}, u32[]{:S(2)}) collective-permute-start(f32[2,48,256]{2,1,0:T(8,128)S(1)} %get-tuple-element.30), channel_id=1, source_target_pairs={{0,8},{8,0},{1,9},{9,1},{2,10},{10,2},{3,11},{11,3},{4,12},{12,4},... | collective-permute-start | bytes 294920 | tf_op jit(solution)/shard_map/ppermute | solution.py:46
  167.6 0.6 collective-permute-start.24
  168.2 3.0 %collective-permute-start.25 = (f32[2,48,256]{2,1,0:T(8,128)S(1)}, f32[2,48,256]{2,1,0:T(8,128)S(1)}, u32[]{:S(2)}, u32[]{:S(2)}) collective-permute-start(f32[2,48,256]{2,1,0:T(8,128)S(1)} %get-tuple-element.33), channel_id=1, source_target_pairs={{0,4},{2,6},{4,0},{6,2},{1,5},{3,7},{5,1},{7,3},{8,12},{10,14},{12... | collective-permute-start | bytes 294920 | tf_op jit(solution)/shard_map/ppermute | solution.py:50
  171.2 2.0 %collective-permute-start.26 = (f32[2,48,256]{2,1,0:T(8,128)S(1)}, f32[2,48,256]{2,1,0:T(8,128)S(1)}, u32[]{:S(2)}, u32[]{:S(2)}) collective-permute-start(f32[2,48,256]{2,1,0:T(8,128)S(1)} %get-tuple-element.34), channel_id=1, source_target_pairs={{0,6},{2,0},{4,2},{6,4},{1,7},{3,1},{5,3},{7,5},{8,14},{10,8},{12,... | collective-permute-start | bytes 294920 | tf_op jit(solution)/shard_map/ppermute | solution.py:50
  173.2 1.5 collective-permute-done.25.e
  174.7 1.1 collective-permute-done.26.f
  175.8 0.7 shard_map.76
  176.5 1.6 shard_map.81
  (29 shorter events, 0.1 us)
Async XLA Ops:
  0.6 10.3 %collective-permute-start = (f32[4,48,256]{2,1,0:T(8,128)}, f32[4,48,256]{2,1,0:T(8,128)S(1)}, u32[]{:S(2)}, u32[]{:S(2)}) collective-permute-start(f32[4,48,256]{2,1,0:T(8,128)} %bitcast.18), channel_id=1, source_target_pairs={{0,0},{1,64},{2,16},{3,96},{4,32},{5,112},{6,48},{7,80},{8,128},{9... | collective-permute-start | bytes 589832 | tf_op jit(solution)/shard_map/ppermute | solution.py:30
  12.3 13.2 %collective-permute-start.7 = (f32[4,48,256]{2,1,0:T(8,128)S(1)}, f32[4,48,256]{2,1,0:T(8,128)S(1)}, u32[]{:S(2)}, u32[]{:S(2)}) collective-permute-start(f32[4,48,256]{2,1,0:T(8,128)S(1)} %shard_map.70.refs_0_), channel_id=1, source_target_pairs={{0,128},{128,0},{1,129},{129,1},{2,130},{130,2},{3,131},{131,3},{4... | collective-permute-start | bytes 589832 | tf_op jit(solution)/shard_map/ppermute | solution.py:34
  14.9 14.8 %collective-permute-start.1 = (f32[4,48,256]{2,1,0:T(8,128)S(1)}, f32[4,48,256]{2,1,0:T(8,128)S(1)}, u32[]{:S(2)}, u32[]{:S(2)}) collective-permute-start(f32[4,48,256]{2,1,0:T(8,128)S(1)} %shard_map.70.refs_0_), channel_id=1, source_target_pairs={{0,16},{16,32},{32,48},{48,64},{64,80},{80,96},{96,112},{112,0},{1... | collective-permute-start | bytes 589832 | tf_op jit(solution)/shard_map/ppermute | solution.py:38
  16.4 13.3 %collective-permute-start.4 = (f32[4,48,256]{2,1,0:T(8,128)S(1)}, f32[4,48,256]{2,1,0:T(8,128)S(1)}, u32[]{:S(2)}, u32[]{:S(2)}) collective-permute-start(f32[4,48,256]{2,1,0:T(8,128)S(1)} %shard_map.70.refs_0_), channel_id=1, source_target_pairs={{0,112},{16,0},{32,16},{48,32},{64,48},{80,64},{96,80},{112,96},{1... | collective-permute-start | bytes 589832 | tf_op jit(solution)/shard_map/ppermute | solution.py:38
  25.4 8.2 %collective-permute-start.8 = (f32[4,48,256]{2,1,0:T(8,128)S(1)}, f32[4,48,256]{2,1,0:T(8,128)S(1)}, u32[]{:S(2)}, u32[]{:S(2)}) collective-permute-start(f32[4,48,256]{2,1,0:T(8,128)S(1)} %collective-permute-done.7.refs_7_), channel_id=1, source_target_pairs={{0,16},{16,32},{32,48},{48,64},{64,80},{80,96},{96,112},{112,0},{1... | collective-permute-start | bytes 589832 | tf_op jit(solution)/shard_map/ppermute | solution.py:38
  25.4 8.2 %collective-permute-start.11 = (f32[4,48,256]{2,1,0:T(8,128)S(1)}, f32[4,48,256]{2,1,0:T(8,128)S(1)}, u32[]{:S(2)}, u32[]{:S(2)}) collective-permute-start(f32[4,48,256]{2,1,0:T(8,128)S(1)} %collective-permute-done.7.refs_7_), channel_id=1, source_target_pairs={{0,112},{16,0},{32,16},{48,32},{64,48},{80,64},{96,80},{112,96},{1... | collective-permute-start | bytes 589832 | tf_op jit(solution)/shard_map/ppermute | solution.py:38
  29.7 8.2 %collective-permute-start.2 = (f32[4,48,256]{2,1,0:T(8,128)S(1)}, f32[4,48,256]{2,1,0:T(8,128)S(1)}, u32[]{:S(2)}, u32[]{:S(2)}) collective-permute-start(f32[4,48,256]{2,1,0:T(8,128)S(1)} %collective-permute-done.1.refs_1_), channel_id=1, source_target_pairs={{0,16},{16,32},{32,48},{48,64},{64,80},{80,96},{96,112},{112,0},{1... | collective-permute-start | bytes 589832 | tf_op jit(solution)/shard_map/ppermute | solution.py:38
  29.7 8.2 %collective-permute-start.5 = (f32[4,48,256]{2,1,0:T(8,128)S(1)}, f32[4,48,256]{2,1,0:T(8,128)S(1)}, u32[]{:S(2)}, u32[]{:S(2)}) collective-permute-start(f32[4,48,256]{2,1,0:T(8,128)S(1)} %collective-permute-done.4.refs_4_), channel_id=1, source_target_pairs={{0,112},{16,0},{32,16},{48,32},{64,48},{80,64},{96,80},{112,96},{1... | collective-permute-start | bytes 589832 | tf_op jit(solution)/shard_map/ppermute | solution.py:38
  33.7 8.5 %collective-permute-start.9 = (f32[4,48,256]{2,1,0:T(8,128)S(1)}, f32[4,48,256]{2,1,0:T(8,128)S(1)}, u32[]{:S(2)}, u32[]{:S(2)}) collective-permute-start(f32[4,48,256]{2,1,0:T(8,128)S(1)} %collective-permute-done.8.refs_8_), channel_id=1, source_target_pairs={{0,16},{16,32},{32,48},{48,64},{64,80},{80,96},{96,112},{112,0},{1... | collective-permute-start | bytes 589832 | tf_op jit(solution)/shard_map/ppermute | solution.py:38
  33.7 8.5 %collective-permute-start.12 = (f32[4,48,256]{2,1,0:T(8,128)S(1)}, f32[4,48,256]{2,1,0:T(8,128)S(1)}, u32[]{:S(2)}, u32[]{:S(2)}) collective-permute-start(f32[4,48,256]{2,1,0:T(8,128)S(1)} %collective-permute-done.11.refs_11_), channel_id=1, source_target_pairs={{0,112},{16,0},{32,16},{48,32},{64,48},{80,64},{96,80},{112,96},{1... | collective-permute-start | bytes 589832 | tf_op jit(solution)/shard_map/ppermute | solution.py:38
  37.9 8.4 %collective-permute-start.3 = (f32[4,48,256]{2,1,0:T(8,128)S(1)}, f32[4,48,256]{2,1,0:T(8,128)S(1)}, u32[]{:S(2)}, u32[]{:S(2)}) collective-permute-start(f32[4,48,256]{2,1,0:T(8,128)S(1)} %collective-permute-done.2.refs_2_), channel_id=1, source_target_pairs={{0,16},{16,32},{32,48},{48,64},{64,80},{80,96},{96,112},{112,0},{1... | collective-permute-start | bytes 589832 | tf_op jit(solution)/shard_map/ppermute | solution.py:38
  37.9 8.5 %collective-permute-start.6 = (f32[4,48,256]{2,1,0:T(8,128)S(1)}, f32[4,48,256]{2,1,0:T(8,128)S(1)}, u32[]{:S(2)}, u32[]{:S(2)}) collective-permute-start(f32[4,48,256]{2,1,0:T(8,128)S(1)} %collective-permute-done.5.refs_5_), channel_id=1, source_target_pairs={{0,112},{16,0},{32,16},{48,32},{64,48},{80,64},{96,80},{112,96},{1... | collective-permute-start | bytes 589832 | tf_op jit(solution)/shard_map/ppermute | solution.py:38
  42.1 8.3 %collective-permute-start.10 = (f32[4,48,256]{2,1,0:T(8,128)S(1)}, f32[4,48,256]{2,1,0:T(8,128)S(1)}, u32[]{:S(2)}, u32[]{:S(2)}) collective-permute-start(f32[4,48,256]{2,1,0:T(8,128)S(1)} %collective-permute-done.9.refs_9_), channel_id=1, source_target_pairs={{0,16},{16,32},{32,48},{48,64},{64,80},{80,96},{96,112},{112,0},{1... | collective-permute-start | bytes 589832 | tf_op jit(solution)/shard_map/ppermute | solution.py:38
  42.1 8.4 %collective-permute-start.13 = (f32[4,48,256]{2,1,0:T(8,128)S(1)}, f32[4,48,256]{2,1,0:T(8,128)S(1)}, u32[]{:S(2)}, u32[]{:S(2)}) collective-permute-start(f32[4,48,256]{2,1,0:T(8,128)S(1)} %collective-permute-done.12.refs_12_), channel_id=1, source_target_pairs={{0,112},{16,0},{32,16},{48,32},{64,48},{80,64},{96,80},{112,96},{1... | collective-permute-start | bytes 589832 | tf_op jit(solution)/shard_map/ppermute | solution.py:38
  46.4 13.0 %collective-permute-start.14 = (f32[2,48,256]{2,1,0:T(8,128)S(1)}, f32[2,48,256]{2,1,0:T(8,128)S(1)}, u32[]{:S(2)}, u32[]{:S(2)}) collective-permute-start(f32[2,48,256]{2,1,0:T(8,128)S(1)} %slice.16), channel_id=1, source_target_pairs={{0,16},{16,32},{32,48},{48,64},{64,80},{80,96},{96,112},{112,0},{1... | collective-permute-start | bytes 294920 | tf_op jit(solution)/shard_map/ppermute | solution.py:38
  46.5 12.9 %collective-permute-start.15 = (f32[2,48,256]{2,1,0:T(8,128)S(1)}, f32[2,48,256]{2,1,0:T(8,128)S(1)}, u32[]{:S(2)}, u32[]{:S(2)}) collective-permute-start(f32[2,48,256]{2,1,0:T(8,128)S(1)} %slice.17), channel_id=1, source_target_pairs={{0,112},{16,0},{32,16},{48,32},{64,48},{80,64},{96,80},{112,96},{1... | collective-permute-start | bytes 294920 | tf_op jit(solution)/shard_map/ppermute | solution.py:38
  50.5 8.9 %collective-permute-start.16 = (f32[2,48,256]{2,1,0:T(8,128)S(1)}, f32[2,48,256]{2,1,0:T(8,128)S(1)}, u32[]{:S(2)}, u32[]{:S(2)}) collective-permute-start(f32[2,48,256]{2,1,0:T(8,128)S(1)} %slice.18), channel_id=1, source_target_pairs={{0,16},{16,32},{32,48},{48,64},{64,80},{80,96},{96,112},{112,0},{1... | collective-permute-start | bytes 294920 | tf_op jit(solution)/shard_map/ppermute | solution.py:38
  50.6 8.8 %collective-permute-start.17 = (f32[2,48,256]{2,1,0:T(8,128)S(1)}, f32[2,48,256]{2,1,0:T(8,128)S(1)}, u32[]{:S(2)}, u32[]{:S(2)}) collective-permute-start(f32[2,48,256]{2,1,0:T(8,128)S(1)} %slice.19), channel_id=1, source_target_pairs={{0,112},{16,0},{32,16},{48,32},{64,48},{80,64},{96,80},{112,96},{1... | collective-permute-start | bytes 294920 | tf_op jit(solution)/shard_map/ppermute | solution.py:38
  62.5 37.5 %collective-permute-start.18 = (f32[8,4,48,256]{3,2,1,0:T(8,128)S(1)}, f32[8,4,48,256]{3,2,1,0:T(8,128)S(1)}, u32[]{:S(2)}, u32[]{:S(2)}) collective-permute-start(f32[8,4,48,256]{3,2,1,0:T(8,128)S(1)} %get-tuple-element.22), channel_id=1, source_target_pairs={{0,1},{1,0},{2,3},{3,2},{4,5},{5,4},{6,7},{7,6},{8,9},{9,8},{10,11... | collective-permute-start | bytes 4718600 | tf_op jit(solution)/shard_map/ppermute | solution.py:42
  62.6 7.5 %collective-permute-start.27 = (f32[4,48,256]{2,1,0:T(8,128)S(1)}, f32[4,48,256]{2,1,0:T(8,128)S(1)}, u32[]{:S(2)}, u32[]{:S(2)}) collective-permute-start(f32[4,48,256]{2,1,0:T(8,128)S(1)} %get-tuple-element.35), channel_id=1, source_target_pairs={{0,6},{2,0},{4,2},{6,4},{1,7},{3,1},{5,3},{7,5},{8,14},{10,8},{12,... | collective-permute-start | bytes 589832 | tf_op jit(solution)/shard_map/ppermute | solution.py:50
  62.7 11.6 %collective-permute-start.28 = (f32[4,48,256]{2,1,0:T(8,128)S(1)}, f32[4,48,256]{2,1,0:T(8,128)S(1)}, u32[]{:S(2)}, u32[]{:S(2)}) collective-permute-start(f32[4,48,256]{2,1,0:T(8,128)S(1)} %get-tuple-element.35), channel_id=1, source_target_pairs={{0,4},{2,6},{4,0},{6,2},{1,5},{3,7},{5,1},{7,3},{8,12},{10,14},{12... | collective-permute-start | bytes 589832 | tf_op jit(solution)/shard_map/ppermute | solution.py:50
  64.8 11.2 %collective-permute-start.29 = (f32[4,48,256]{2,1,0:T(8,128)S(1)}, f32[4,48,256]{2,1,0:T(8,128)S(1)}, u32[]{:S(2)}, u32[]{:S(2)}) collective-permute-start(f32[4,48,256]{2,1,0:T(8,128)S(1)} %get-tuple-element.35), channel_id=1, source_target_pairs={{0,2},{2,4},{4,6},{6,0},{1,3},{3,5},{5,7},{7,1},{8,10},{10,12},{12... | collective-permute-start | bytes 589832 | tf_op jit(solution)/shard_map/ppermute | solution.py:50
  76.0 20.7 %collective-permute-start.30 = (f32[4,4,48,256]{3,2,1,0:T(8,128)S(1)}, f32[4,4,48,256]{3,2,1,0:T(8,128)S(1)}, u32[]{:S(2)}, u32[]{:S(2)}) collective-permute-start(f32[4,4,48,256]{3,2,1,0:T(8,128)S(1)} %pad_maximum_fusion.refs_0_), channel_id=1, source_target_pairs={{0,8},{8,0},{1,9},{9,1},{2,10},{10,2},{3,11},{11,3},{4,12},{12,4},... | collective-permute-start | bytes 2359304 | tf_op jit(solution)/shard_map/ppermute | solution.py:46
  102.1 2.0 %collective-permute-start.31 = (f32[16,4,8,256]{3,2,1,0:T(8,128)S(1)}, f32[16,4,8,256]{3,2,1,0:T(8,128)S(1)}, u32[]{:S(2)}, u32[]{:S(2)}) collective-permute-start(f32[16,4,8,256]{3,2,1,0:T(8,128)S(1)} %get-tuple-element.37), channel_id=1, source_target_pairs={{0,1},{1,0},{2,3},{3,2},{4,5},{5,4},{6,7},{7,6},{8,9},{9,8},{10,11... | collective-permute-start | bytes 1572872 | tf_op jit(solution)/shard_map/ppermute | solution.py:42
  150.6 25.9 %copy-start = (f32[4,256,256]{2,1,0:T(8,128)S(1)}, f32[4,256,256]{2,1,0:T(8,128)}, u32[]{:S(2)}) copy-start(f32[4,256,256]{2,1,0:T(8,128)} %dinv.1) | copy-start | bytes 3145732
  150.6 25.9 %collective-permute-start.32 = (f32[16,4,8,256]{3,2,1,0:T(8,128)S(1)}, f32[16,4,8,256]{3,2,1,0:T(8,128)S(1)}, u32[]{:S(2)}, u32[]{:S(2)}) collective-permute-start(f32[16,4,8,256]{3,2,1,0:T(8,128)S(1)} %all_to_all.17.own), channel_id=1, source_target_pairs={{0,1},{1,0},{2,3},{3,2},{4,5},{5,4},{6,7},{7,6},{8,9},{9,8},{10,11... | collective-permute-start | bytes 1572872 | tf_op jit(solution)/shard_map/ppermute | solution.py:42
  150.8 13.9 %collective-permute-start.22 = (f32[4,2,48,256]{3,2,1,0:T(8,128)S(1)}, f32[4,2,48,256]{3,2,1,0:T(8,128)S(1)}, u32[]{:S(2)}, u32[]{:S(2)}) collective-permute-start(f32[4,2,48,256]{3,2,1,0:T(8,128)S(1)} %get-tuple-element.28), channel_id=1, source_target_pairs={{0,8},{8,0},{1,9},{9,1},{2,10},{10,2},{3,11},{11,3},{4,12},{12,4},... | collective-permute-start | bytes 1179656 | tf_op jit(solution)/shard_map/ppermute | solution.py:46
  151.7 7.8 %collective-permute-start.19 = (f32[2,2,48,256]{3,2,1,0:T(8,128)S(1)}, f32[2,2,48,256]{3,2,1,0:T(8,128)S(1)}, u32[]{:S(2)}, u32[]{:S(2)}) collective-permute-start(f32[2,2,48,256]{3,2,1,0:T(8,128)S(1)} %get-tuple-element.24), channel_id=1, source_target_pairs={{0,2},{2,4},{4,6},{6,0},{1,3},{3,5},{5,7},{7,1},{8,10},{10,12},{12... | collective-permute-start | bytes 589832 | tf_op jit(solution)/shard_map/ppermute | solution.py:50
  152.2 9.3 %collective-permute-start.20 = (f32[2,2,48,256]{3,2,1,0:T(8,128)S(1)}, f32[2,2,48,256]{3,2,1,0:T(8,128)S(1)}, u32[]{:S(2)}, u32[]{:S(2)}) collective-permute-start(f32[2,2,48,256]{3,2,1,0:T(8,128)S(1)} %get-tuple-element.25), channel_id=1, source_target_pairs={{0,4},{2,6},{4,0},{6,2},{1,5},{3,7},{5,1},{7,3},{8,12},{10,14},{12... | collective-permute-start | bytes 589832 | tf_op jit(solution)/shard_map/ppermute | solution.py:50
  155.3 9.4 %collective-permute-start.21 = (f32[2,2,48,256]{3,2,1,0:T(8,128)S(1)}, f32[2,2,48,256]{3,2,1,0:T(8,128)S(1)}, u32[]{:S(2)}, u32[]{:S(2)}) collective-permute-start(f32[2,2,48,256]{3,2,1,0:T(8,128)S(1)} %get-tuple-element.26), channel_id=1, source_target_pairs={{0,6},{2,0},{4,2},{6,4},{1,7},{3,1},{5,3},{7,5},{8,14},{10,8},{12,... | collective-permute-start | bytes 589832 | tf_op jit(solution)/shard_map/ppermute | solution.py:50
  164.8 8.4 %collective-permute-start.23 = (f32[2,48,256]{2,1,0:T(8,128)S(1)}, f32[2,48,256]{2,1,0:T(8,128)S(1)}, u32[]{:S(2)}, u32[]{:S(2)}) collective-permute-start(f32[2,48,256]{2,1,0:T(8,128)S(1)} %get-tuple-element.30), channel_id=1, source_target_pairs={{0,8},{8,0},{1,9},{9,1},{2,10},{10,2},{3,11},{11,3},{4,12},{12,4},... | collective-permute-start | bytes 294920 | tf_op jit(solution)/shard_map/ppermute | solution.py:46
  167.6 5.6 %collective-permute-start.24 = (f32[2,48,256]{2,1,0:T(8,128)S(1)}, f32[2,48,256]{2,1,0:T(8,128)S(1)}, u32[]{:S(2)}, u32[]{:S(2)}) collective-permute-start(f32[2,48,256]{2,1,0:T(8,128)S(1)} %get-tuple-element.32), channel_id=1, source_target_pairs={{0,2},{2,4},{4,6},{6,0},{1,3},{3,5},{5,7},{7,1},{8,10},{10,12},{12... | collective-permute-start | bytes 294920 | tf_op jit(solution)/shard_map/ppermute | solution.py:50
  168.2 6.5 %collective-permute-start.25 = (f32[2,48,256]{2,1,0:T(8,128)S(1)}, f32[2,48,256]{2,1,0:T(8,128)S(1)}, u32[]{:S(2)}, u32[]{:S(2)}) collective-permute-start(f32[2,48,256]{2,1,0:T(8,128)S(1)} %get-tuple-element.33), channel_id=1, source_target_pairs={{0,4},{2,6},{4,0},{6,2},{1,5},{3,7},{5,1},{7,3},{8,12},{10,14},{12... | collective-permute-start | bytes 294920 | tf_op jit(solution)/shard_map/ppermute | solution.py:50
  171.2 4.6 %collective-permute-start.26 = (f32[2,48,256]{2,1,0:T(8,128)S(1)}, f32[2,48,256]{2,1,0:T(8,128)S(1)}, u32[]{:S(2)}, u32[]{:S(2)}) collective-permute-start(f32[2,48,256]{2,1,0:T(8,128)S(1)} %get-tuple-element.34), channel_id=1, source_target_pairs={{0,6},{2,0},{4,2},{6,4},{1,7},{3,1},{5,3},{7,5},{8,14},{10,8},{12,... | collective-permute-start | bytes 294920 | tf_op jit(solution)/shard_map/ppermute | solution.py:50
